TPU v7x, 32 devices: a whole 2x2x4 slice. The times are simulated.
32 devices in a mesh: groups: 2 (over y), qry: 4 (over x, core), ref: 4 (over z).
Axes of the slice: x: 2, y: 2, z: 4, core: 2. Of those that a mesh axis runs over, the one named last changes fastest.
Arguments:
- query_feats: bfloat16 [1024, 9, 3840], P(('groups', 'qry')), parts along dimension 0, may hold values from -6 to 6
- ref_feats: bfloat16 [256, 4, 9, 3840], P(('groups', 'ref'), 'qry'), parts along dimension 0, may hold values from -6 to 6
- pair_table: int32 [8, 4], P('groups'), parts along dimension 0, may hold values from 0 to 1, as said below
- lengths: int32 [4], P('groups'), parts along dimension 0, may hold values from 1 to 96, 128 in all
- query_len: int32 [2], P('groups'), parts along dimension 0, may hold values from 64 to 128
- conv1_weight: float32 [3, 3, 32], replicated, may hold values from -2 to 2
- conv1_bias: float32 [32], replicated, may hold values from -3 to 3
- conv2_weight: bfloat16 [3, 3, 64, 32], replicated, may hold values from -0.375 to 0.375
- conv2_bias: float32 [64], replicated, may hold values from -3 to 3
- conv3_weight: bfloat16 [3, 3, 128, 64], replicated, may hold values from -0.25 to 0.25
- conv3_bias: float32 [128], replicated, may hold values from -3 to 3
- conv4_weight: bfloat16 [128], replicated, may hold values from -0.5 to 0.5
- conv4_bias: float32 [1], replicated, may hold values from -3 to 3
Outputs:
- score_map: float32 [256, 128], P(('groups', 'qry'), 'ref'), parts along dimension 0
- video_scores: float32 [4], P('groups'), parts along dimension 0
There are 2 independent parts, one for each index of `groups`. A program takes and returns all parts, laid end to end along the dimension named above; an argument that names none is the same for every part. Nothing has to cross between parts.
Inputs may be any that keep to these rules, and one draw needn't show every extreme that they name: `pair_table`: in each row, at most 1 of the 1 tiles in the block of one index of ref are 1, and some such block holds exactly 1 in every draw.
All inputs are finite; a program needn't handle non-finite values.
Results may differ from a plain program's by a relative error of at most 0.01.
Values may be sent and summed in bfloat16 or wider, within the bound.
No kernel may reach another device: no remote copies, remote signals or barrier semaphores. Data moves between devices by JAX's collectives and lax.ppermute only.
A program may use at most 128 MiB of HBM per device.

v0:
```python
import functools
import math

import jax
import jax.numpy as jnp
from jax import lax
from jax.experimental import pallas as pl
from jax.experimental.pallas import tpu as pltpu
from jax.sharding import PartitionSpec as P


GRANT = 20 * 1024 * 1024
PIECE = 8
PHASES = 4
HALO = 2
EDGE = 8
GROUP = 3
WINDOW = PHASES * GROUP + 2
BF = jnp.bfloat16
F32 = jnp.float32


def in_hbm(array):
    return pltpu.with_memory_space_constraint(array, pltpu.HBM)


def shift(array, axis, pairs):
    return lax.ppermute(array, axis, pairs)


def cut_kernel(order, source_ref, *refs):
    outs, sems = refs[:-1], refs[-1]
    copies = []
    for index, (at, out) in enumerate(zip(order, outs)):
        piece = source_ref.at[:, pl.ds(at * PIECE, PIECE), :]
        copies.append(pltpu.make_async_copy(piece, out, sems.at[index]))
    for copy in copies:
        copy.start()
    for copy in copies:
        copy.wait()


def cut(source, order):
    regions, _, channels = source.shape
    shape = (regions, PIECE, channels)
    pieces = pl.pallas_call(
        functools.partial(cut_kernel, order),
        in_specs=[pl.BlockSpec(memory_space=pltpu.HBM)],
        out_specs=[pl.BlockSpec(memory_space=pltpu.VMEM) for _ in order],
        out_shape=[jax.ShapeDtypeStruct(shape, source.dtype) for _ in order],
        scratch_shapes=[pltpu.SemaphoreType.DMA((len(order),))],
        compiler_params=pltpu.CompilerParams(vmem_limit_bytes=GRANT),
        cost_estimate=pl.CostEstimate(
            flops=0, bytes_accessed=4 * source.size, transcendentals=0
        ),
        name="cut",
    )(in_hbm(source))
    return [piece.reshape(regions * PIECE, channels) for piece in pieces]


def write_edges(pos_ref, arrays, core_ref, chip_ref):
    total = jnp.concatenate(arrays, axis=0)
    frames = total.shape[1]
    eights = [total[at : at + 8] for at in range(0, total.shape[0], 8)]
    first = jnp.concatenate([eight[:, 0:EDGE] for eight in eights], axis=1)
    last = jnp.concatenate([eight[:, frames - EDGE : frames] for eight in eights], axis=1)
    even = pos_ref[0] % 2 == 0
    core_ref[...] = jnp.where(even, last, first)
    chip_ref[...] = jnp.where(even, first, last)


def edge_shapes(columns):
    return [jax.ShapeDtypeStruct((8, columns // 8 * EDGE), F32)] * 2


def edges_kernel(pos_ref, *refs):
    write_edges(pos_ref, [ref[...] for ref in refs[:-2]], *refs[-2:])


def edge_rows(position, sources):
    smem = pl.BlockSpec(memory_space=pltpu.SMEM)
    vmem = pl.BlockSpec(memory_space=pltpu.VMEM)
    return pl.pallas_call(
        edges_kernel,
        in_specs=[smem] + [vmem for _ in sources],
        out_specs=[vmem, vmem],
        out_shape=edge_shapes(sum(source.shape[0] for source in sources)),
        name="edges",
    )(position, *sources)


def sims_kernel(scale, spans, others, fetch, pos_ref, table_ref, query_ref, *refs):
    pieces, refs = refs[: len(spans)], refs[len(spans) :]
    done, refs = refs[:others], refs[others:]
    out_ref = refs[0]
    if fetch:
        rows_ref, sems = refs[-2], refs[-1]
    regions, frames, channels = query_ref.shape
    width = 3 if regions % 3 == 0 else 1
    if fetch:
        copies, arriving = [], []
        start = 0
        for index, (span, piece) in enumerate(zip(spans, pieces)):
            rows = pl.ds(start, span * regions)
            copies.append(pltpu.make_async_copy(piece, rows_ref.at[rows, :], sems.at[index]))
            start += span * regions
        for copy in copies:
            copy.start()
        for step in range(regions // width):
            block = pl.ds(step * width, width)
            arriving.append(
                pltpu.make_async_copy(
                    query_ref.at[block], refs[1].at[block], sems.at[len(spans) + step]
                )
            )
        for copy in arriving:
            copy.start()
        query_ref = refs[1]
        for copy in copies:
            copy.wait()

    total = None
    for step in range(regions // width):
        if fetch:
            arriving[step].wait()
        rows = (
            rows_ref[...]
            if fetch
            else jnp.concatenate([piece[...] for piece in pieces], axis=0)
        )
        products = lax.dot_general(
            rows,
            query_ref[step * width : (step + 1) * width].reshape(-1, channels),
            (((1,), (1,)), ((), ())),
            preferred_element_type=F32,
        )
        parts = []
        start = 0
        for span in spans:
            best = products[start : start + span]
            for other in range(1, regions):
                best = jnp.maximum(
                    best, products[start + other * span : start + (other + 1) * span]
                )
            part = best[:, 0:frames]
            for other in range(1, width):
                part = part + best[:, other * frames : (other + 1) * frames]
            parts.append(part)
            start += span * regions
        part = jnp.concatenate(parts, axis=0)
        total = part if total is None else total + part
    active = table_ref[pos_ref[0], pos_ref[1]] == 1
    total = total * jnp.where(active, scale, 0.0).astype(F32)
    out_ref[...] = total
    if done:
        write_edges(pos_ref, [ref[...] for ref in done] + [total], *refs[1:3])


def similarities(query, pieces, position, table, done=(), fetch=False):
    regions, frames, channels = query.shape
    spans = [piece.shape[0] // regions for piece in pieces]
    scale = 1.0 / (regions * math.sqrt(channels))
    rows = sum(spans)
    shapes = [jax.ShapeDtypeStruct((rows, frames), F32)]
    if done:
        shapes += edge_shapes(rows + sum(array.shape[0] for array in done))
    steps = 0
    if fetch:
        shapes.append(pltpu.VMEM(query.shape, query.dtype))
        steps = regions
    smem = pl.BlockSpec(memory_space=pltpu.SMEM)
    vmem = pl.BlockSpec(memory_space=pltpu.VMEM)
    return pl.pallas_call(
        functools.partial(sims_kernel, scale, spans, len(done), fetch),
        in_specs=[smem, smem, pl.BlockSpec(memory_space=pltpu.HBM) if fetch else vmem]
        + [pl.BlockSpec(memory_space=pltpu.HBM) if fetch else vmem for _ in pieces]
        + [vmem for _ in done],
        out_specs=[vmem for _ in shapes],
        out_shape=shapes,
        scratch_shapes=[
            pltpu.VMEM((rows * regions, channels), BF),
            pltpu.SemaphoreType.DMA((len(pieces) + steps,)),
        ]
        if fetch
        else [],
        compiler_params=pltpu.CompilerParams(vmem_limit_bytes=GRANT),
        cost_estimate=pl.CostEstimate(
            flops=2 * rows * regions * regions * frames * channels,
            bytes_accessed=2 * channels * regions * rows,
            transcendentals=0,
        ),
        name="similarities",
    )(position, table, *(map(in_hbm, (query, *pieces)) if fetch else (query, *pieces)), *done)


def convolve(sims_ref, weights, scratch, score_ref, pos_ref, block, limits, padding):
    w1_ref, b1_ref, w2_ref, b2_ref, w3_ref, b3_ref, w4_ref, b4_ref = weights
    y_ref, first_ref, lhs2_ref, second_ref, lhs3_ref = scratch
    map_rows, map_cols = limits
    jf, js, jt = padding
    rows1 = block + 2 * HALO
    groups = rows1 // GROUP
    row0 = pos_ref[0] * block
    col0 = pos_ref[1] * block
    lanes = sims_ref.shape[2]

    sources = [(PHASES - 1, 0)] + [(phase, 1) for phase in range(PHASES)] + [(0, 2)]
    bases = [sims_ref[phase, at : at + jf, :] for phase, at in sources]
    terms = len(sources) * WINDOW
    zero = jnp.zeros((jf, 128 - terms), F32)
    reach = PHASES * HALO + 1
    lane = lax.broadcasted_iota(jnp.int32, (jf, 128), 1)
    for group in range(groups):
        low = PHASES * GROUP * group - reach
        parts = []
        for base in bases:
            if low < 0:
                parts.append(base[:, lanes + low : lanes])
                parts.append(base[:, 0 : low + WINDOW])
            else:
                parts.append(base[:, low : low + WINDOW])
        window = jnp.concatenate(parts + [zero], axis=1)
        high = window.astype(BF).astype(F32)
        rest = pltpu.roll(window - high, terms, 1)
        again = pltpu.roll(high, 2 * terms - 128, 1)
        row = slice(group * jf, (group + 1) * jf)
        y_ref[row, 0:128] = jnp.where(lane < terms, high, rest).astype(BF)
        y_ref[row, 128:256] = jnp.where(lane < 2 * terms - 128, rest, again).astype(BF)

    cell = lax.broadcasted_iota(jnp.int32, (jf, 128), 0)

    def inside(halo, count):
        at = cell[0:count] + (col0 - halo)
        return jnp.where((at >= 0) & (at < map_cols), 1.0, 0.0).astype(F32)

    def row_flag(at):
        return jnp.where((at >= 0) & (at < map_rows), 1.0, 0.0).astype(F32)

    keep_cols = inside(HALO, jf)
    for member in range(GROUP):
        result = jnp.dot(
            y_ref[0 : groups * jf, :],
            w1_ref[:, member * 512 : (member + 1) * 512],
            preferred_element_type=F32,
        )
        pooled = jnp.maximum(
            jnp.maximum(result[:, 0:128], result[:, 128:256]),
            jnp.maximum(result[:, 256:384], result[:, 384:512]),
        )
        pooled = jnp.maximum(pooled + b1_ref[...], 0.0)
        for group in range(groups):
            at = group * GROUP + member
            keep = keep_cols * row_flag(row0 + at - HALO)
            first_ref[at, 0:jf, :] = (
                (pooled[group * jf : (group + 1) * jf] * keep).astype(BF).astype(F32)
            )

    upper = lane < 64
    left = (lane // 32) % 2 == 0
    rows2 = block + 2
    for at in range(rows2):
        centre = first_ref[at + 1, 0:jf, :]
        across = jnp.where(upper, first_ref[at + 2, 0:jf, :], first_ref[at, 0:jf, :])
        row = slice(at * js, (at + 1) * js)
        for index, value in enumerate((centre, across)):
            here = pltpu.roll(value, jf - 1, 0)
            beside = jnp.where(left, pltpu.roll(value, jf - 2, 0), value)
            lhs2_ref[row, index * 256 : index * 256 + 128] = here[0:js].astype(BF)
            lhs2_ref[row, index * 256 + 128 : index * 256 + 256] = beside[0:js].astype(BF)
    result = jnp.dot(lhs2_ref[0 : rows2 * js, :], w2_ref[...], preferred_element_type=F32)
    pooled = jnp.maximum(result[:, 0:128], result[:, 128:256])
    pooled = jnp.maximum(pooled, pltpu.roll(pooled, 64, 1))
    pooled = jnp.maximum(pooled + b2_ref[...], 0.0)
    keep_cols = inside(1, js)
    for at in range(rows2):
        keep = keep_cols * row_flag(row0 + at - 1)
        second_ref[at, 0:js, :] = (pooled[at * js : (at + 1) * js] * keep).astype(BF).astype(F32)
        if js < jt + 8:
            second_ref[at, js : jt + 8, :] = jnp.zeros((jt + 8 - js, 128), F32)

    upper = upper[0:jt]
    for at in range(block // 2):
        row = slice(at * jt, (at + 1) * jt)
        rows = [second_ref.at[2 * at + down] for down in range(4)]
        for down in range(4):
            pair = jnp.where(upper, rows[down][0:jt, :], rows[down][1 : 1 + jt, :])
            lhs3_ref[row, down * 128 : (down + 1) * 128] = pair.astype(BF)
        for half in range(2):
            pair = jnp.where(
                upper, rows[2 * half][2 : 2 + jt, :], rows[2 * half + 1][2 : 2 + jt, :]
            )
            lhs3_ref[row, (4 + half) * 128 : (5 + half) * 128] = pair.astype(BF)
    third = jnp.dot(lhs3_ref[...], w3_ref[...], preferred_element_type=F32)
    third = jnp.maximum(third + b3_ref[...], 0.0).astype(BF)
    flat = lax.dot_general(
        w4_ref[...], third, (((1,), (1,)), ((), ())), preferred_element_type=F32
    )
    flat = flat[0:8] + b4_ref[0]
    for at in range(block // 2):
        score_ref[2 * at : 2 * at + 2, :] = flat[0:2, at * jt : at * jt + block]


def pad_cells(cells):
    js = -(-(cells + 2) // 8) * 8
    return (max(-(-(cells + 4) // 8) * 8, js), js, -(-cells // 16) * 16)


def convolve_scratch(block, padding):
    jf, js, jt = padding
    rows1 = block + 2 * HALO
    return [
        pltpu.VMEM((rows1 // GROUP * jf, 256), BF),
        pltpu.VMEM((rows1, jf, 128), F32),
        pltpu.VMEM(((block + 2) * js, 512), BF),
        pltpu.VMEM((block + 2, max(js, jt + 8), 128), F32),
        pltpu.VMEM((block // 2 * jt, 768), BF),
    ]


def place(pos_ref, sims_ref, sources, segments):
    for source, row, size, shard, cell in segments:
        if source < len(sources):
            rows = slice(3 + cell, 3 + cell + size)
            sims_ref[pos_ref[2 + shard], rows, 0 : sources[source].shape[1]] = sources[source][
                row : row + size, :
            ]


def place_edges(pos_ref, sims_ref, starts, segments, table, edge_ref, side):
    for source, row, size, shard, cell in segments:
        for at in range(0, size, 8):
            start = starts[source] + row + at
            count = min(8, size - at)
            lane = start // 8 * EDGE
            sims_ref[pos_ref[table + shard], 3 + cell + at : 3 + cell + at + count, side] = edge_ref[
                start % 8 : start % 8 + count, lane : lane + EDGE
            ]


def assemble_kernel(segments, pos_ref, *refs):
    sources, sims_ref = refs[:-1], refs[-1]
    sims_ref[...] = jnp.zeros_like(sims_ref)
    place(pos_ref, sims_ref, sources, segments)


def assembled(position, sources, segments, block):
    smem = pl.BlockSpec(memory_space=pltpu.SMEM)
    vmem = pl.BlockSpec(memory_space=pltpu.VMEM)
    frames = sources[0].shape[1]
    return pl.pallas_call(
        functools.partial(assemble_kernel, segments),
        in_specs=[smem] + [vmem for _ in sources],
        out_specs=vmem,
        out_shape=jax.ShapeDtypeStruct((PHASES, block + 24, 2 * frames), F32),
        compiler_params=pltpu.CompilerParams(vmem_limit_bytes=GRANT),
        cost_estimate=pl.CostEstimate(flops=0, bytes_accessed=500_000, transcendentals=0),
        name="assemble",
    )(position, *sources)


def network_kernel(limits, padding, starts, segments, pos_ref, len_ref, base_ref, *refs):
    (late_ref, core_ref, chip_ref), refs = refs[:3], refs[3:]
    weights, (score_ref, peak_ref, sims_ref), scratch = refs[:8], refs[8:11], refs[11:]
    block = score_ref.shape[0]
    last = len(starts) - 1
    place(
        pos_ref, sims_ref, [late_ref], [(0, *rest) for source, *rest in segments if source == last]
    )
    lanes = sims_ref.shape[2]
    above, below = slice(lanes - EDGE, lanes), slice(lanes // 2, lanes // 2 + EDGE)

    def edges(core_side, chip_side):
        place_edges(pos_ref, sims_ref, starts, segments, 6, core_ref, core_side)
        place_edges(pos_ref, sims_ref, starts, segments, 10, chip_ref, chip_side)

    pl.when(pos_ref[0] % 2 == 0)(lambda: edges(below, above))
    pl.when(pos_ref[0] % 2 == 1)(lambda: edges(above, below))
    convolve(sims_ref, weights, scratch, score_ref, pos_ref, block, limits, padding)

    score = score_ref[...]
    videos = len_ref.shape[0]
    column = pos_ref[1] * block + lax.broadcasted_iota(jnp.int32, (block, block), 1)
    slot = lax.broadcasted_iota(jnp.int32, (block, 128), 1)
    start = jnp.int32(0)
    peaks = jnp.zeros((block, 128), F32)
    for video in range(videos):
        end = start + len_ref[video]
        member = (column >= start) & (column < end)
        best = jnp.max(jnp.where(member, score, -jnp.inf), axis=1, keepdims=True)
        peaks = jnp.where(slot == video, best, peaks)
        start = end
    peak_ref[...] = jnp.transpose(peaks)[0:videos]


def network(position, lengths, base, late, edges, starts, segments, weights, block, limits):
    smem = pl.BlockSpec(memory_space=pltpu.SMEM)
    vmem = pl.BlockSpec(memory_space=pltpu.VMEM)
    padding = pad_cells(block)
    arrays = [base, late, *edges]
    score, peaks, _ = pl.pallas_call(
        functools.partial(network_kernel, limits, padding, starts, segments),
        in_specs=[smem, smem] + [vmem] * len(arrays) + [vmem] * 7 + [smem],
        out_specs=[vmem, vmem, vmem],
        out_shape=[
            jax.ShapeDtypeStruct((block, block), F32),
            jax.ShapeDtypeStruct((lengths.shape[0], block), F32),
            jax.ShapeDtypeStruct(base.shape, F32),
        ],
        scratch_shapes=convolve_scratch(block, padding),
        input_output_aliases={2: 2},
        cost_estimate=pl.CostEstimate(
            flops=6_000_000_000, bytes_accessed=4_000_000, transcendentals=0
        ),
        compiler_params=pltpu.CompilerParams(vmem_limit_bytes=GRANT),
        name="network",
    )(position, lengths, *arrays, *weights)
    return score, peaks


def weights_kernel(w1_ref, b1_ref, w2_ref, b2_ref, w3_ref, b3_ref, w4_ref, *outs):
    f1_ref, o1_ref, f2_ref, o2_ref, f3_ref, o3_ref, f4_ref = outs
    c1, c2, c3 = w1_ref.shape[2], w2_ref.shape[3], w3_ref.shape[3]
    rows = lax.broadcasted_iota(jnp.int32, (256, 16 * c1), 0)
    lane = lax.broadcasted_iota(jnp.int32, (256, 16 * c1), 1) // c1
    terms = 6 * WINDOW
    third = rows >= 2 * terms
    valid = rows < 3 * terms
    rows = rows - jnp.where(third, 2 * terms, jnp.where(rows >= terms, terms, 0))
    along = jnp.zeros_like(rows)
    for offset in range(1, 6):
        along = along + jnp.where(rows >= offset * WINDOW, 1, 0)
    down = rows - along * WINDOW - 2 * ((lane // 2) % 2) - lane // 8
    along = along - 2 * (lane % 2) - (lane // 4) % 2
    taps = []
    for di in range(3):
        for dj in range(3):
            tap = jnp.concatenate([w1_ref[di, dj : dj + 1, :]] * (128 // c1), axis=1)
            taps.append(jnp.concatenate([tap] * (16 * c1 // 128), axis=1))
    for member in range(GROUP):
        dense = jnp.zeros(rows.shape, F32)
        for di in range(3):
            for dj in range(3):
                here = (down == di + PHASES * member) & (along == dj) & valid
                dense = jnp.where(here, taps[3 * di + dj], dense)
        high = dense.astype(BF).astype(F32)
        at = slice(member * 16 * c1, (member + 1) * 16 * c1)
        f1_ref[:, at] = jnp.where(third, dense - high, high).astype(BF)
    o1_ref[...] = jnp.concatenate([b1_ref[...]] * (128 // c1), axis=1)
    o2_ref[...] = jnp.concatenate([b2_ref[...]] * (128 // c2), axis=1)
    f2_ref[...] = jnp.zeros_like(f2_ref)
    reach = ((0, 1), (2, -1))
    for index in range(16):
        row_kind, col_kind, sr, sc = (index >> 3) & 1, (index >> 2) & 1, (index >> 1) & 1, index & 1
        for phase in range(4):
            di = reach[row_kind][sr] - phase // 2 + 1
            dj = reach[col_kind][sc] - phase % 2 + 1
            if 0 <= di <= 2 and 0 <= dj <= 2:
                f2_ref[index * c1 : (index + 1) * c1, phase * c2 : (phase + 1) * c2] = w2_ref[
                    di, dj
                ]
    f3_ref[...] = jnp.zeros_like(f3_ref)
    order = [(row, col) for row in range(4) for col in range(2)] + [(row, 2) for row in range(4)]
    for index, (row, dj) in enumerate(order):
        for output in range(2):
            if 0 <= row - output <= 2:
                f3_ref[index * c2 : (index + 1) * c2, output * c3 : (output + 1) * c3] = w3_ref[
                    row - output, dj
                ]
    o3_ref[...] = jnp.concatenate([b3_ref[...]] * 2, axis=1)
    fourth = jnp.concatenate([w4_ref[...].astype(F32)] * 2, axis=1)
    half = lax.broadcasted_iota(jnp.int32, f4_ref.shape, 1) // c3
    output = lax.broadcasted_iota(jnp.int32, f4_ref.shape, 0)
    f4_ref[...] = jnp.where(half == output, fourth, 0.0).astype(BF)


def network_weights(w1, b1, w2, b2, w3, b3, w4, b4):
    c1, c2, c3 = w1.shape[2], w2.shape[2], w3.shape[2]
    shapes = [
        ((256, GROUP * 16 * c1), BF),
        ((1, 128), F32),
        ((16 * c1, 4 * c2), BF),
        ((1, 128), F32),
        ((12 * c2, 2 * c3), BF),
        ((1, 2 * c3), F32),
        ((16, 2 * c3), BF),
    ]
    f1, o1, f2, o2, f3, o3, f4 = pl.pallas_call(
        weights_kernel,
        out_shape=[jax.ShapeDtypeStruct(shape, dtype) for shape, dtype in shapes],
        cost_estimate=pl.CostEstimate(flops=100_000_000, bytes_accessed=4_000_000, transcendentals=0),
        compiler_params=pltpu.CompilerParams(vmem_limit_bytes=GRANT),
        name="weights",
    )(
        w1,
        b1[None],
        jnp.transpose(w2, (0, 1, 3, 2)),
        b2[None],
        jnp.transpose(w3, (0, 1, 3, 2)),
        b3[None],
        w4[None],
    )
    return (f1, o1, f2, o2, f3, o3, f4, b4)


def body(
    query_feats,
    ref_feats,
    pair_table,
    lengths,
    query_len,
    conv1_weight,
    conv1_bias,
    conv2_weight,
    conv2_bias,
    conv3_weight,
    conv3_bias,
    conv4_weight,
    conv4_bias,
):
    qry_index = lax.axis_index("qry")
    ref_index = lax.axis_index("ref")
    senders = lax.axis_size("qry")
    blocks = lax.axis_size("ref")
    frames, regions, channels = query_feats.shape
    rows = ref_feats.shape[0]
    block = frames // PHASES
    limits = (block * senders, block * blocks)
    count = rows // PIECE
    split = count >= 3 and senders == PHASES
    odd = qry_index % 2
    nearest = (qry_index + 2 * odd - 1) % senders
    entries = [qry_index, ref_index]
    for place in (qry_index, qry_index ^ 1, nearest):
        entries += [place ^ flip if split else flip for flip in range(PHASES)]
    position = jnp.stack([jnp.asarray(entry, jnp.int32) for entry in entries])
    query = jnp.transpose(query_feats, (1, 0, 2))
    own = jnp.transpose(ref_feats[:, 0], (1, 0, 2))
    chips = senders // 2
    across = [
        [(i, (i - 2 * step) % senders) for i in range(senders)] for step in range(1, chips)
    ]
    beside = [(i, i ^ 1) for i in range(senders)]

    if split:
        late = count // 2
        middle = [at for at in range(1, count - 1) if at != late]
        groups = [[0], [count - 1]] + [[at] for at in middle] + [[late]]
    else:
        groups = [list(range(count))]

    order = [at for group in groups for at in group]
    (piece,) = cut(own, order[:1])
    source, piece = lax.optimization_barrier((own, piece))
    whole = source.reshape(regions * rows, channels)
    cuts = [piece]
    if len(order) > 1:
        cuts += cut(source, order[1:])
    found = []
    for pairs in across:
        trips = []
        for piece in cuts:
            trips.append(shift(piece, "qry", pairs))
        found.append(trips)
    sibling = shift(whole, "qry", beside)
    weights = network_weights(
        conv1_weight,
        conv1_bias,
        conv2_weight,
        conv2_bias,
        conv3_weight,
        conv3_bias,
        conv4_weight,
        conv4_bias,
    )
    here, query = similarities(
        query, [whole, sibling], position, pair_table, fetch=True
    )
    sources, segments = [here], [(0, 0, rows, 0, 0), (0, rows, rows, 1, 0)]
    shard = 2
    last = []
    for pieces in found:
        pieces = list(pieces)
        for index, group in enumerate(groups):
            batch = []
            for at in group:
                piece = pieces.pop(0)
                batch += [piece, shift(piece, "qry", beside)]
            if split and index == len(groups) - 1:
                last = batch
                break
            here = similarities(query, batch, position, pair_table)[0]
            for order, at in enumerate(group):
                for half in range(2):
                    start = PIECE * (2 * order + half)
                    segments.append((len(sources), start, PIECE, shard + half, at * PIECE))
            sources.append(here)
        shard += 2
    if not split:
        tiles = [[None] * rows for _ in range(senders)]
        for source, row, size, place, cell in segments:
            for at in range(0, size, PIECE):
                tiles[place][cell + at] = sources[source][row + at : row + at + PIECE]
        tiles = [
            jnp.concatenate([part for part in parts if part is not None], axis=0)
            for parts in tiles
        ]
        sender = jnp.arange(senders, dtype=jnp.int32)
        step = (sender // 2 - qry_index // 2) % chips
        ordered = jnp.stack(tiles)[2 * step + ((sender % 2) ^ (qry_index % 2))]
        sims = ordered.reshape(senders // PHASES, PHASES, rows, frames).transpose(1, 2, 0, 3)
        sources = [sims.reshape(PHASES * block, frames)]
        segments = [(0, phase * block, block, phase, 0) for phase in range(PHASES)]

    def cells(low):
        parts = []
        for want in range(PHASES):
            for source, row, size, place, cell in segments:
                if place == want and cell <= low and low + HALO <= cell + size:
                    parts.append(sources[source][row + low - cell : row + low - cell + HALO])
        return jnp.concatenate(parts, axis=0)

    up = [(i, i + 1) for i in range(blocks - 1)]
    down = [(b, a) for a, b in up]
    right = shift(cells(0), "ref", down)
    left = shift(cells(block - HALO), "ref", up)
    for edge, cell in ((left, -HALO), (right, block)):
        segments += [(len(sources), HALO * k, HALO, k, cell) for k in range(PHASES)]
        sources.append(edge)
    base = assembled(position, sources, segments, block)
    if split:
        for half in range(2):
            segments.append((len(sources), PIECE * half, PIECE, 2 + half, late * PIECE))
        done, core, chip = similarities(query, last, position, pair_table, sources)
        sources.append(done)
    else:
        core, chip = edge_rows(position, sources)
        done = sources[-1]
    starts = [0]
    for source in sources[:-1]:
        starts.append(starts[-1] + source.shape[0])
    pairs = [(i, i + 1) for i in range(1, senders - 1, 2)]
    chip = shift(chip, "qry", pairs + [(b, a) for a, b in pairs])
    core = shift(core, "qry", beside)
    score_map, peaks = network(
        position,
        lengths,
        base,
        done,
        (core, chip),
        starts,
        segments,
        weights,
        block,
        limits,
    )
    place = jnp.stack([qry_index, qry_index ^ 1])
    peaks = jnp.stack([peaks, shift(peaks, "qry", beside)])

    def between_odd(array, flip_qry, flip_ref):
        pairs = [
            (q * blocks + r, (q ^ flip_qry) * blocks + (r ^ flip_ref))
            for q in range(1, senders, 2)
            for r in range(blocks)
        ]
        return shift(array, ("qry", "ref"), pairs)

    bit = 1
    while bit < blocks:
        peaks = jnp.maximum(peaks, between_odd(peaks, 0, bit))
        bit *= 2
    row_ids = place[:, None] * block + jnp.arange(block, dtype=jnp.int32)[None]
    total = jnp.sum(jnp.where((row_ids < query_len[0])[:, None], peaks, 0.0), axis=(0, 2))
    bit = senders // 2
    while bit > 1:
        total = total + between_odd(total, bit, 0)
        bit //= 2
    total = total / query_len[0].astype(F32)
    given = shift(total, "qry", [(q, q ^ 1) for q in range(1, senders, 2)])
    return (score_map, jnp.where(odd == 1, total, given))


def solution(mesh):
    placed = (
        P(("groups", "qry"), None, None),
        P(("groups", "ref"), "qry", None, None),
        P("groups", None),
        P("groups"),
        P("groups"),
    ) + (P(),) * 8

    return jax.shard_map(
        body,
        mesh=mesh,
        in_specs=placed,
        out_specs=(P(("groups", "qry"), "ref"), P("groups")),
        check_vma=False,
    )
```

profile of v0, /device:TPU:0, one launch (start us, length us, event | category | flops | bytes accessed | tf_op | source)
XLA Modules:
  0.0 114.5 jit_solution(16359716474634619193)
XLA Ops:
  0.6 1.1 cut.2
  2.3 2.6 %collective-permute-start.1 = (bf16[72,3840]{1,0:T(8,128)(2,1)S(1)}, bf16[72,3840]{1,0:T(8,128)(2,1)S(1)}, u32[]{:S(2)}, u32[]{:S(2)}) collective-permute-start(bf16[72,3840]{1,0:T(8,128)(2,1)S(1)} %bitcast.32), channel_id=1, source_target_pairs={{0,8},{4,12},{8,0},{12,4},{1,9},{5,13},{9,1},{13,5},{2,10},{6,14},... | collective-permute-start | bytes 1658888 | tf_op jit(solution)/shard_map/ppermute | solution.py:28
  4.8 2.4 %cut.3 = (bf16[9,8,3840]{2,1,0:T(8,128)(2,1)}, bf16[9,8,3840]{2,1,0:T(8,128)(2,1)}, bf16[9,8,3840]{2,1,0:T(8,128)(2,1)S(1)}) custom-call(bf16[9,32,3840]{2,1,0:T(8,128)(2,1)} %bitcast.45), custom_call_target="tpu_custom_call" | custom-call | bytes 4423680 | tf_op jit(solution)/shard_map/cut/pallas_call | solution.py:46
  7.3 2.0 %collective-permute-start.5 = (bf16[72,3840]{1,0:T(8,128)(2,1)}, bf16[72,3840]{1,0:T(8,128)(2,1)S(1)}, u32[]{:S(2)}, u32[]{:S(2)}) collective-permute-start(bf16[72,3840]{1,0:T(8,128)(2,1)} %bitcast.19), channel_id=1, source_target_pairs={{0,8},{4,12},{8,0},{12,4},{1,9},{5,13},{9,1},{13,5},{2,10},{6,14},... | collective-permute-start | bytes 1658888 | tf_op jit(solution)/shard_map/ppermute | solution.py:28
  9.4 8.8 %collective-permute-done.1.refs_0_ = bf16[72,3840]{1,0:T(8,128)(2,1)S(1)} collective-permute-done((bf16[72,3840]{1,0:T(8,128)(2,1)S(1)}, bf16[72,3840]{1,0:T(8,128)(2,1)S(1)}, u32[]{:S(2)}, u32[]{:S(2)}) %collective-permute-start.1) | collective-permute-done | bytes 552992 | tf_op jit(solution)/shard_map/ppermute | solution.py:28
  18.3 11.8 %collective-permute-done.3.refs_0_ = bf16[72,3840]{1,0:T(8,128)(2,1)S(1)} collective-permute-done((bf16[72,3840]{1,0:T(8,128)(2,1)}, bf16[72,3840]{1,0:T(8,128)(2,1)S(1)}, u32[]{:S(2)}, u32[]{:S(2)}) %collective-permute-start.3) | collective-permute-done | bytes 552992 | tf_op jit(solution)/shard_map/ppermute | solution.py:28
  30.1 11.8 %collective-permute-done.5.refs_0_ = bf16[72,3840]{1,0:T(8,128)(2,1)S(1)} collective-permute-done((bf16[72,3840]{1,0:T(8,128)(2,1)}, bf16[72,3840]{1,0:T(8,128)(2,1)S(1)}, u32[]{:S(2)}, u32[]{:S(2)}) %collective-permute-start.5) | collective-permute-done | bytes 552992 | tf_op jit(solution)/shard_map/ppermute | solution.py:28
  41.9 11.6 %collective-permute-done.9.refs_0_ = bf16[72,3840]{1,0:T(8,128)(2,1)S(1)} collective-permute-done((bf16[72,3840]{1,0:T(8,128)(2,1)S(1)}, bf16[72,3840]{1,0:T(8,128)(2,1)S(1)}, u32[]{:S(2)}, u32[]{:S(2)}) %collective-permute-start.9) | collective-permute-done | bytes 552992 | tf_op jit(solution)/shard_map/ppermute | solution.py:28
  53.5 0.7 copy-done
  54.2 11.3 %similarities.5 = (f32[64,128]{1,0:T(8,128)S(1)}, bf16[9,128,3840]{2,1,0:T(8,128)(2,1)S(1)}) custom-call(s32[14]{0:T(128)S(1)} %stack.67.pos_ref, s32[4,4]{1,0:T(4,128)S(1)} %copy-done, bf16[9,128,3840]{2,1,0:T(8,128)(2,1)} %bitcast.50, bf16[288,3840]{1,0:T(8,128)(2,1)} %bitcast.46, bf16[288,3840]{1,0:T(8,128)(2,1)} %collective-permute-done.refs_1_), custom_call_target="tpu_custom_call" | custom-call | flops 5096079360 | bytes 4423680 | tf_op jit(solution)/shard_map/similarities/pallas_call | solution.py:173
  65.5 3.2 %similarities.6.refs_1_.refs_3_ = f32[16,128]{1,0:T(8,128)S(1)} custom-call(s32[14]{0:T(128)S(1)} %stack.67.pos_ref, s32[4,4]{1,0:T(4,128)S(1)} %copy-done, bf16[9,128,3840]{2,1,0:T(8,128)(2,1)S(1)} %get-tuple-element.23.query_ref, bf16[72,3840]{1,0:T(8,128)(2,1)S(1)} %collective-permute-done.1.refs_0_, bf16[72,3840]{1,0:T(8,128)(2,1)S(1)} %collective-permute-done.2.refs_1_), custom_call_target="tpu_custom_call" | custom-call | flops 1274019840 | bytes 1105920 | tf_op jit(solution)/shard_map/similarities/pallas_call | solution.py:173
  68.7 1.3 %collective-permute-start.8 = (f32[8,128]{1,0:T(8,128)S(1)}, f32[8,128]{1,0:T(8,128)S(1)}, u32[]{:S(2)}, u32[]{:S(2)}) collective-permute-start(f32[8,128]{1,0:T(8,128)S(1)} %pad_maximum_fusion.1), channel_id=1, source_target_pairs={{1,0},{2,1},{3,2},{5,4},{6,5},{7,6},{9,8},{10,9},{11,10},{13,12},{... | collective-permute-start | bytes 12296 | tf_op jit(solution)/shard_map/ppermute | solution.py:28
  70.0 3.2 %similarities.7.refs_2_.refs_4_ = f32[16,128]{1,0:T(8,128)S(1)} custom-call(s32[14]{0:T(128)S(1)} %stack.67.pos_ref, s32[4,4]{1,0:T(4,128)S(1)} %copy-done, bf16[9,128,3840]{2,1,0:T(8,128)(2,1)S(1)} %get-tuple-element.23.query_ref, bf16[72,3840]{1,0:T(8,128)(2,1)S(1)} %collective-permute-done.3.refs_0_, bf16[72,3840]{1,0:T(8,128)(2,1)S(1)} %collective-permute-done.4.refs_1_), custom_call_target="tpu_custom_call" | custom-call | flops 1274019840 | bytes 1105920 | tf_op jit(solution)/shard_map/similarities/pallas_call | solution.py:173
  73.3 4.7 %collective-permute-start.7 = (f32[8,128]{1,0:T(8,128)S(1)}, f32[8,128]{1,0:T(8,128)S(1)}, u32[]{:S(2)}, u32[]{:S(2)}) collective-permute-start(f32[8,128]{1,0:T(8,128)S(1)} %pad_maximum_fusion), channel_id=1, source_target_pairs={{0,1},{1,2},{2,3},{4,5},{5,6},{6,7},{8,9},{9,10},{10,11},{12,13},{... | collective-permute-start | bytes 12296 | tf_op jit(solution)/shard_map/ppermute | solution.py:28
  78.0 3.2 %similarities.8.refs_3_.refs_5_ = f32[16,128]{1,0:T(8,128)S(1)} custom-call(s32[14]{0:T(128)S(1)} %stack.67.pos_ref, s32[4,4]{1,0:T(4,128)S(1)} %copy-done, bf16[9,128,3840]{2,1,0:T(8,128)(2,1)S(1)} %get-tuple-element.23.query_ref, bf16[72,3840]{1,0:T(8,128)(2,1)S(1)} %collective-permute-done.5.refs_0_, bf16[72,3840]{1,0:T(8,128)(2,1)S(1)} %collective-permute-done.6.refs_1_), custom_call_target="tpu_custom_call" | custom-call | flops 1274019840 | bytes 1105920 | tf_op jit(solution)/shard_map/similarities/pallas_call | solution.py:173
  81.3 3.2 %similarities.9 = (f32[16,128]{1,0:T(8,128)S(1)}, f32[8,144]{1,0:T(8,128)S(1)}, f32[8,144]{1,0:T(8,128)S(1)}) custom-call(s32[14]{0:T(128)S(1)} %stack.67.pos_ref, s32[4,4]{1,0:T(4,128)S(1)} %copy-done, bf16[9,128,3840]{2,1,0:T(8,128)(2,1)S(1)} %get-tuple-element.23.query_ref, bf16[72,3840]{1,0:T(8,128)(2,1)S(1)} %collective-permute-done.9.refs_0_, ...), custom_call_target="tpu_custom_call" | custom-call | flops 1274019840 | bytes 1105920 | tf_op jit(solution)/shard_map/similarities/pallas_call | solution.py:173
  84.6 0.8 collective-permute-start.12
  85.5 3.1 %weights.1 = (bf16[256,1536]{1,0:T(8,128)(2,1)S(1)}, f32[1,128]{1,0:T(1,128)S(1)}, bf16[512,256]{1,0:T(8,128)(2,1)S(1)}, f32[1,128]{1,0:T(1,128)S(1)}, bf16[768,...) custom-call(f32[3,3,32]{2,1,0:T(4,128)S(1)} %copy-done.3, f32[1,32]{1,0:T(1,128)S(1)} %bitcast.39, ...), custom_call_target="tpu_custom_call" | custom-call | flops 100000000 | bytes 4000000 | tf_op jit(solution)/shard_map/weights/pallas_call | solution.py:487
  89.8 4.0 %network.1 = (f32[32,32]{1,0:T(8,128)}, f32[2,32]{1,0:T(2,128)S(1)}, f32[4,56,256]{2,1,0:T(8,128)S(1)}) custom-call(s32[14]{0:T(128)S(1)} %stack.67.pos_ref, s32[2]{0:T(128)S(1)} %copy-done.8, f32[4,56,256]{2,1,0:T(8,128)S(1)} %assemble.1.base_ref, f32[16,128]{1,0:T(8,128)S(1)} %get-tuple-element.28.refs_0_, ...), custom_call_target="tpu_custom_call", output_to_operand_aliasing={{2}: (2, {})} | custom-call | flops 6000000000 | bytes 4000000 | tf_op jit(solution)/shard_map/network/pallas_call | solution.py:400
  93.8 3.1 %collective-permute-start.13 = (f32[2,32]{1,0:T(2,128)S(1)}, f32[2,32]{1,0:T(2,128)S(1)}, u32[]{:S(2)}, u32[]{:S(2)}) collective-permute-start(f32[2,32]{1,0:T(2,128)S(1)} %get-tuple-element.39), channel_id=1, source_target_pairs={{0,4},{4,0},{8,12},{12,8},{1,5},{5,1},{9,13},{13,9},{2,6},{6,2},{1... | collective-permute-start | bytes 776 | tf_op jit(solution)/shard_map/ppermute | solution.py:28
  96.9 0.8 collective-permute-done.13
  99.1 0.7 collective-permute-start.15
  100.7 1.3 %collective-permute-start.17 = (f32[2]{0:T(128)S(1)}, f32[2]{0:T(128)S(1)}, u32[]{:S(2)}, u32[]{:S(2)}) collective-permute-start(f32[2]{0:T(128)S(1)} %add_divide_fusion), channel_id=1, source_target_pairs={{4,0},{12,8},{5,1},{13,9},{6,2},{14,10},{7,3},{15,11},{20,16},{28,... | collective-permute-start | bytes 32 | tf_op jit(solution)/shard_map/ppermute | solution.py:28
  102.0 12.0 %collective-permute-done.17 = f32[2]{0:T(128)S(1)} collective-permute-done((f32[2]{0:T(128)S(1)}, f32[2]{0:T(128)S(1)}, u32[]{:S(2)}, u32[]{:S(2)}) %collective-permute-start.17) | collective-permute-done | bytes 40 | tf_op jit(solution)/shard_map/ppermute | solution.py:28
  (53 shorter events, 3.7 us)
Async XLA Ops:
  1.7 51.8 %collective-permute-start = (bf16[288,3840]{1,0:T(8,128)(2,1)}, bf16[288,3840]{1,0:T(8,128)(2,1)}, u32[]{:S(2)}, u32[]{:S(2)}) collective-permute-start(bf16[288,3840]{1,0:T(8,128)(2,1)} %bitcast.44), channel_id=1, source_target_pairs={{0,4},{4,0},{8,12},{12,8},{1,5},{5,1},{9,13},{13,9},{2,6},{6,2},{1... | collective-permute-start | bytes 6635528 | tf_op jit(solution)/shard_map/ppermute | solution.py:28
  2.3 15.9 %collective-permute-start.1 = (bf16[72,3840]{1,0:T(8,128)(2,1)S(1)}, bf16[72,3840]{1,0:T(8,128)(2,1)S(1)}, u32[]{:S(2)}, u32[]{:S(2)}) collective-permute-start(bf16[72,3840]{1,0:T(8,128)(2,1)S(1)} %bitcast.32), channel_id=1, source_target_pairs={{0,8},{4,12},{8,0},{12,4},{1,9},{5,13},{9,1},{13,5},{2,10},{6,14},... | collective-permute-start | bytes 1658888 | tf_op jit(solution)/shard_map/ppermute | solution.py:28
  7.2 22.8 %collective-permute-start.3 = (bf16[72,3840]{1,0:T(8,128)(2,1)}, bf16[72,3840]{1,0:T(8,128)(2,1)S(1)}, u32[]{:S(2)}, u32[]{:S(2)}) collective-permute-start(bf16[72,3840]{1,0:T(8,128)(2,1)} %bitcast.18), channel_id=1, source_target_pairs={{0,8},{4,12},{8,0},{12,4},{1,9},{5,13},{9,1},{13,5},{2,10},{6,14},... | collective-permute-start | bytes 1658888 | tf_op jit(solution)/shard_map/ppermute | solution.py:28
  7.3 34.6 %collective-permute-start.5 = (bf16[72,3840]{1,0:T(8,128)(2,1)}, bf16[72,3840]{1,0:T(8,128)(2,1)S(1)}, u32[]{:S(2)}, u32[]{:S(2)}) collective-permute-start(bf16[72,3840]{1,0:T(8,128)(2,1)} %bitcast.19), channel_id=1, source_target_pairs={{0,8},{4,12},{8,0},{12,4},{1,9},{5,13},{9,1},{13,5},{2,10},{6,14},... | collective-permute-start | bytes 1658888 | tf_op jit(solution)/shard_map/ppermute | solution.py:28
  9.3 44.2 %collective-permute-start.9 = (bf16[72,3840]{1,0:T(8,128)(2,1)S(1)}, bf16[72,3840]{1,0:T(8,128)(2,1)S(1)}, u32[]{:S(2)}, u32[]{:S(2)}) collective-permute-start(bf16[72,3840]{1,0:T(8,128)(2,1)S(1)} %bitcast.36), channel_id=1, source_target_pairs={{0,8},{4,12},{8,0},{12,4},{1,9},{5,13},{9,1},{13,5},{2,10},{6,14},... | collective-permute-start | bytes 1658888 | tf_op jit(solution)/shard_map/ppermute | solution.py:28
  18.2 47.3 %collective-permute-start.2 = (bf16[72,3840]{1,0:T(8,128)(2,1)S(1)}, bf16[72,3840]{1,0:T(8,128)(2,1)S(1)}, u32[]{:S(2)}, u32[]{:S(2)}) collective-permute-start(bf16[72,3840]{1,0:T(8,128)(2,1)S(1)} %collective-permute-done.1.refs_0_), channel_id=1, source_target_pairs={{0,4},{4,0},{8,12},{12,8},{1,5},{5,1},{9,13},{13,9},{2,6},{6,2},{1... | collective-permute-start | bytes 1658888 | tf_op jit(solution)/shard_map/ppermute | solution.py:28
  30.1 40.0 %collective-permute-start.4 = (bf16[72,3840]{1,0:T(8,128)(2,1)S(1)}, bf16[72,3840]{1,0:T(8,128)(2,1)S(1)}, u32[]{:S(2)}, u32[]{:S(2)}) collective-permute-start(bf16[72,3840]{1,0:T(8,128)(2,1)S(1)} %collective-permute-done.3.refs_0_), channel_id=1, source_target_pairs={{0,4},{4,0},{8,12},{12,8},{1,5},{5,1},{9,13},{13,9},{2,6},{6,2},{1... | collective-permute-start | bytes 1658888 | tf_op jit(solution)/shard_map/ppermute | solution.py:28
  41.9 36.1 %collective-permute-start.6 = (bf16[72,3840]{1,0:T(8,128)(2,1)S(1)}, bf16[72,3840]{1,0:T(8,128)(2,1)S(1)}, u32[]{:S(2)}, u32[]{:S(2)}) collective-permute-start(bf16[72,3840]{1,0:T(8,128)(2,1)S(1)} %collective-permute-done.5.refs_0_), channel_id=1, source_target_pairs={{0,4},{4,0},{8,12},{12,8},{1,5},{5,1},{9,13},{13,9},{2,6},{6,2},{1... | collective-permute-start | bytes 1658888 | tf_op jit(solution)/shard_map/ppermute | solution.py:28
  53.5 27.7 %collective-permute-start.10 = (bf16[72,3840]{1,0:T(8,128)(2,1)S(1)}, bf16[72,3840]{1,0:T(8,128)(2,1)S(1)}, u32[]{:S(2)}, u32[]{:S(2)}) collective-permute-start(bf16[72,3840]{1,0:T(8,128)(2,1)S(1)} %collective-permute-done.9.refs_0_), channel_id=1, source_target_pairs={{0,4},{4,0},{8,12},{12,8},{1,5},{5,1},{9,13},{13,9},{2,6},{6,2},{1... | collective-permute-start | bytes 1658888 | tf_op jit(solution)/shard_map/ppermute | solution.py:28
  68.7 12.5 %collective-permute-start.8 = (f32[8,128]{1,0:T(8,128)S(1)}, f32[8,128]{1,0:T(8,128)S(1)}, u32[]{:S(2)}, u32[]{:S(2)}) collective-permute-start(f32[8,128]{1,0:T(8,128)S(1)} %pad_maximum_fusion.1), channel_id=1, source_target_pairs={{1,0},{2,1},{3,2},{5,4},{6,5},{7,6},{9,8},{10,9},{11,10},{13,12},{... | collective-permute-start | bytes 12296 | tf_op jit(solution)/shard_map/ppermute | solution.py:28
  73.2 12.2 %copy-start.1 = (bf16[3,3,128,64]{2,3,1,0:T(8,128)(2,1)S(1)}, bf16[3,3,128,64]{2,3,1,0:T(8,128)(2,1)}, u32[]{:S(2)}) copy-start(bf16[3,3,128,64]{2,3,1,0:T(8,128)(2,1)} %param.22) | copy-start | bytes 442372
  73.3 12.2 %copy-start.2 = (bf16[3,3,64,32]{2,3,1,0:T(8,128)(2,1)S(1)}, bf16[3,3,64,32]{2,3,1,0:T(8,128)(2,1)}, u32[]{:S(2)}) copy-start(bf16[3,3,64,32]{2,3,1,0:T(8,128)(2,1)} %param.20) | copy-start | bytes 110596
  73.3 12.2 %copy-start.3 = (f32[3,3,32]{2,1,0:T(4,128)S(1)}, f32[3,3,32]{2,1,0:T(4,128)}, u32[]{:S(2)}) copy-start(f32[3,3,32]{2,1,0:T(4,128)} %w1_ref.1) | copy-start | bytes 3460
  73.3 12.2 %copy-start.4 = (f32[32]{0:T(128)S(1)}, f32[32]{0:T(128)}, u32[]{:S(2)}) copy-start(f32[32]{0:T(128)} %param.19) | copy-start | bytes 388
  73.3 12.2 %copy-start.5 = (f32[64]{0:T(128)S(1)}, f32[64]{0:T(128)}, u32[]{:S(2)}) copy-start(f32[64]{0:T(128)} %param.21) | copy-start | bytes 772
  73.3 16.5 %copy-start.8 = (s32[2]{0:T(128)S(1)}, s32[2]{0:T(128)}, u32[]{:S(2)}) copy-start(s32[2]{0:T(128)} %len_ref.1) | copy-start | bytes 28
  73.3 7.9 %collective-permute-start.7 = (f32[8,128]{1,0:T(8,128)S(1)}, f32[8,128]{1,0:T(8,128)S(1)}, u32[]{:S(2)}, u32[]{:S(2)}) collective-permute-start(f32[8,128]{1,0:T(8,128)S(1)} %pad_maximum_fusion), channel_id=1, source_target_pairs={{0,1},{1,2},{2,3},{4,5},{5,6},{6,7},{8,9},{9,10},{10,11},{12,13},{... | collective-permute-start | bytes 12296 | tf_op jit(solution)/shard_map/ppermute | solution.py:28
  84.5 5.3 %collective-permute-start.11 = (f32[8,144]{1,0:T(8,128)S(1)}, f32[8,144]{1,0:T(8,128)S(1)}, u32[]{:S(2)}, u32[]{:S(2)}) collective-permute-start(f32[8,144]{1,0:T(8,128)S(1)} %get-tuple-element.29), channel_id=1, source_target_pairs={{0,4},{4,0},{8,12},{12,8},{1,5},{5,1},{9,13},{13,9},{2,6},{6,2},{1... | collective-permute-start | bytes 13832 | tf_op jit(solution)/shard_map/ppermute | solution.py:28
  84.6 5.2 %collective-permute-start.12 = (f32[8,144]{1,0:T(8,128)S(1)}, f32[8,144]{1,0:T(8,128)S(1)}, u32[]{:S(2)}, u32[]{:S(2)}) collective-permute-start(f32[8,144]{1,0:T(8,128)S(1)} %get-tuple-element.30), channel_id=1, source_target_pairs={{4,8},{8,4},{5,9},{9,5},{6,10},{10,6},{7,11},{11,7},{20,24},{24,20... | collective-permute-start | bytes 13832 | tf_op jit(solution)/shard_map/ppermute | solution.py:28
  93.8 3.9 %collective-permute-start.13 = (f32[2,32]{1,0:T(2,128)S(1)}, f32[2,32]{1,0:T(2,128)S(1)}, u32[]{:S(2)}, u32[]{:S(2)}) collective-permute-start(f32[2,32]{1,0:T(2,128)S(1)} %get-tuple-element.39), channel_id=1, source_target_pairs={{0,4},{4,0},{8,12},{12,8},{1,5},{5,1},{9,13},{13,9},{2,6},{6,2},{1... | collective-permute-start | bytes 776 | tf_op jit(solution)/shard_map/ppermute | solution.py:28
  97.7 1.4 %collective-permute-start.14 = (f32[2,2,32]{2,1,0:T(2,128)S(1)}, f32[2,2,32]{2,1,0:T(2,128)S(1)}, u32[]{:S(2)}, u32[]{:S(2)}) collective-permute-start(f32[2,2,32]{2,1,0:T(2,128)S(1)} %pad_maximum_fusion.2), channel_id=1, source_target_pairs={{4,5},{5,4},{6,7},{7,6},{12,13},{13,12},{14,15},{15,14},{20,21},{2... | collective-permute-start | bytes 1544 | tf_op jit(solution)/shard_map/ppermute | solution.py:28
  99.1 0.7 collective-permute-start.15
  100.0 0.7 collective-permute-start.16
  100.7 13.3 %collective-permute-start.17 = (f32[2]{0:T(128)S(1)}, f32[2]{0:T(128)S(1)}, u32[]{:S(2)}, u32[]{:S(2)}) collective-permute-start(f32[2]{0:T(128)S(1)} %add_divide_fusion), channel_id=1, source_target_pairs={{4,0},{12,8},{5,1},{13,9},{6,2},{14,10},{7,3},{15,11},{20,16},{28,... | collective-permute-start | bytes 32 | tf_op jit(solution)/shard_map/ppermute | solution.py:28
  (3 other events, 25.0 us)
where the time goes:
time: 115 us; the launch traced here: 114 us
  waiting for transfers between devices  56.8 us (49%)
  Pallas kernels  35.2 us (31%)
  starting transfers between devices  18.5 us (16%)
  between operations  2.32 us (2%)
    ppermute x18, waiting for transfers between devices, shift(): return lax.ppermute(array, axis, pairs)  56.8 us
    pallas_call x5, Pallas kernels, similarities(): pl.pallas_call(functools.partial(sims_kernel, scale, spans, len(done), fe...  24.1 us
    ppermute x18, starting transfers between devices, shift(): return lax.ppermute(array, axis, pairs)  18.5 us
    pallas_call x1, Pallas kernels, network(): pl.pallas_call(functools.partial(network_kernel, limits, padding, starts,...  3.98 us
    pallas_call x2, Pallas kernels, cut(): pl.pallas_call(functools.partial(cut_kernel, order), in_specs=[pl.BlockSp...  3.49 us
    pallas_call x1, Pallas kernels, network_weights(): pl.pallas_call(weights_kernel, out_shape=[jax.ShapeDtypeStruct(shape, dty...  3.09 us
  transfers between devices with their start and end apart: 18, of which 6 were waited for; matrix products, arithmetic and copies ran while one was open for 0% of the time, Pallas kernels for 24%

commit v1 on v0

--- a/solution.py
+++ b/solution.py
@@ -326,13 +326,13 @@
             ]
 
 
-def place_edges(pos_ref, sims_ref, starts, segments, table, edge_ref, side):
+def place_edges(pos_ref, sims_ref, starts, segments, table, edge, side):
     for source, row, size, shard, cell in segments:
         for at in range(0, size, 8):
             start = starts[source] + row + at
             count = min(8, size - at)
             lane = start // 8 * EDGE
-            sims_ref[pos_ref[table + shard], 3 + cell + at : 3 + cell + at + count, side] = edge_ref[
+            sims_ref[pos_ref[table + shard], 3 + cell + at : 3 + cell + at + count, side] = edge[
                 start % 8 : start % 8 + count, lane : lane + EDGE
             ]
 
@@ -369,9 +369,12 @@
     lanes = sims_ref.shape[2]
     above, below = slice(lanes - EDGE, lanes), slice(lanes // 2, lanes // 2 + EDGE)
 
+    ends = (pos_ref[0] == 0) | (pos_ref[0] == limits[0] // block - 1)
+    core, chip = core_ref[...], jnp.where(ends, 0.0, chip_ref[...])
+
     def edges(core_side, chip_side):
-        place_edges(pos_ref, sims_ref, starts, segments, 6, core_ref, core_side)
-        place_edges(pos_ref, sims_ref, starts, segments, 10, chip_ref, chip_side)
+        place_edges(pos_ref, sims_ref, starts, segments, 6, core, core_side)
+        place_edges(pos_ref, sims_ref, starts, segments, 10, chip, chip_side)
 
     pl.when(pos_ref[0] % 2 == 0)(lambda: edges(below, above))
     pl.when(pos_ref[0] % 2 == 1)(lambda: edges(above, below))
@@ -638,7 +641,7 @@
     starts = [0]
     for source in sources[:-1]:
         starts.append(starts[-1] + source.shape[0])
-    pairs = [(i, i + 1) for i in range(1, senders - 1, 2)]
+    pairs = [(i, (i + 1) % senders) for i in range(1, senders, 2)]
     chip = shift(chip, "qry", pairs + [(b, a) for a, b in pairs])
     core = shift(core, "qry", beside)
     score_map, peaks = network(
@@ -653,30 +656,17 @@
         block,
         limits,
     )
-    place = jnp.stack([qry_index, qry_index ^ 1])
-    peaks = jnp.stack([peaks, shift(peaks, "qry", beside)])
-
-    def between_odd(array, flip_qry, flip_ref):
-        pairs = [
-            (q * blocks + r, (q ^ flip_qry) * blocks + (r ^ flip_ref))
-            for q in range(1, senders, 2)
-            for r in range(blocks)
-        ]
-        return shift(array, ("qry", "ref"), pairs)
-
     bit = 1
     while bit < blocks:
-        peaks = jnp.maximum(peaks, between_odd(peaks, 0, bit))
+        peaks = jnp.maximum(peaks, shift(peaks, "ref", [(i, i ^ bit) for i in range(blocks)]))
         bit *= 2
-    row_ids = place[:, None] * block + jnp.arange(block, dtype=jnp.int32)[None]
-    total = jnp.sum(jnp.where((row_ids < query_len[0])[:, None], peaks, 0.0), axis=(0, 2))
+    row_ids = qry_index * block + jnp.arange(block, dtype=jnp.int32)
+    total = jnp.sum(jnp.where((row_ids < query_len[0])[None], peaks, 0.0), axis=1)
     bit = senders // 2
-    while bit > 1:
-        total = total + between_odd(total, bit, 0)
+    while bit >= 1:
+        total = total + shift(total, "qry", [(i, i ^ bit) for i in range(senders)])
         bit //= 2
-    total = total / query_len[0].astype(F32)
-    given = shift(total, "qry", [(q, q ^ 1) for q in range(1, senders, 2)])
-    return (score_map, jnp.where(odd == 1, total, given))
+    return (score_map, total / query_len[0].astype(F32))
 
 
 def solution(mesh):

time: 115 us -> 109 us (0.948)
  waiting for transfers between devices: 56.8 us -> 51.6 us
    ppermute x18 -> x17, waiting for transfers between devices: 56.8 us -> 51.6 us  [shift(): return lax.ppermute(array, axis, pairs)]
    ppermute x18 -> x17, starting transfers between devices: 18.5 us -> 17.9 us  [shift(): return lax.ppermute(array, axis, pairs)]
  transfers between devices with their start and end apart: 18 -> 17, of which waited for: 6 -> 8; matrix products, arithmetic and copies ran while one was open for 0% -> 0% of each run, Pallas kernels for 24% -> 25%
where the time goes in v1:
time: 109 us; the launch traced here: 108 us
  waiting for transfers between devices  51.6 us (47%)
  Pallas kernels  35.2 us (32%)
  starting transfers between devices  17.9 us (16%)
  between operations  2.23 us (2%)
    ppermute x17, waiting for transfers between devices, shift(): return lax.ppermute(array, axis, pairs)  51.6 us
    pallas_call x5, Pallas kernels, similarities(): pl.pallas_call(functools.partial(sims_kernel, scale, spans, len(done), fe...  24.1 us
    ppermute x17, starting transfers between devices, shift(): return lax.ppermute(array, axis, pairs)  17.9 us
    pallas_call x1, Pallas kernels, network(): pl.pallas_call(functools.partial(network_kernel, limits, padding, starts,...  3.98 us
    pallas_call x2, Pallas kernels, cut(): pl.pallas_call(functools.partial(cut_kernel, order), in_specs=[pl.BlockSp...  3.49 us
    pallas_call x1, Pallas kernels, network_weights(): pl.pallas_call(weights_kernel, out_shape=[jax.ShapeDtypeStruct(shape, dty...  3.09 us
  transfers between devices with their start and end apart: 17, of which 8 were waited for; matrix products, arithmetic and copies ran while one was open for 0% of the time, Pallas kernels for 25%

profile of v1, /device:TPU:0, one launch (start us, length us, event | category | flops | bytes accessed | tf_op | source)
XLA Modules:
  0.0 108.4 jit_solution(13799815100040379997)
XLA Ops:
  0.6 1.1 cut.2
  2.3 2.6 %collective-permute-start.1 = (bf16[72,3840]{1,0:T(8,128)(2,1)S(1)}, bf16[72,3840]{1,0:T(8,128)(2,1)S(1)}, u32[]{:S(2)}, u32[]{:S(2)}) collective-permute-start(bf16[72,3840]{1,0:T(8,128)(2,1)S(1)} %bitcast.30), channel_id=1, source_target_pairs={{0,8},{4,12},{8,0},{12,4},{1,9},{5,13},{9,1},{13,5},{2,10},{6,14},... | collective-permute-start | bytes 1658888 | tf_op jit(solution)/shard_map/ppermute | solution.py:28
  4.8 2.4 %cut.3 = (bf16[9,8,3840]{2,1,0:T(8,128)(2,1)}, bf16[9,8,3840]{2,1,0:T(8,128)(2,1)}, bf16[9,8,3840]{2,1,0:T(8,128)(2,1)S(1)}) custom-call(bf16[9,32,3840]{2,1,0:T(8,128)(2,1)} %bitcast.40), custom_call_target="tpu_custom_call" | custom-call | bytes 4423680 | tf_op jit(solution)/shard_map/cut/pallas_call | solution.py:46
  7.3 2.0 %collective-permute-start.5 = (bf16[72,3840]{1,0:T(8,128)(2,1)}, bf16[72,3840]{1,0:T(8,128)(2,1)S(1)}, u32[]{:S(2)}, u32[]{:S(2)}) collective-permute-start(bf16[72,3840]{1,0:T(8,128)(2,1)} %bitcast.19), channel_id=1, source_target_pairs={{0,8},{4,12},{8,0},{12,4},{1,9},{5,13},{9,1},{13,5},{2,10},{6,14},... | collective-permute-start | bytes 1658888 | tf_op jit(solution)/shard_map/ppermute | solution.py:28
  9.4 8.8 %collective-permute-done.1.refs_0_ = bf16[72,3840]{1,0:T(8,128)(2,1)S(1)} collective-permute-done((bf16[72,3840]{1,0:T(8,128)(2,1)S(1)}, bf16[72,3840]{1,0:T(8,128)(2,1)S(1)}, u32[]{:S(2)}, u32[]{:S(2)}) %collective-permute-start.1) | collective-permute-done | bytes 552992 | tf_op jit(solution)/shard_map/ppermute | solution.py:28
  18.3 11.8 %collective-permute-done.3.refs_0_ = bf16[72,3840]{1,0:T(8,128)(2,1)S(1)} collective-permute-done((bf16[72,3840]{1,0:T(8,128)(2,1)}, bf16[72,3840]{1,0:T(8,128)(2,1)S(1)}, u32[]{:S(2)}, u32[]{:S(2)}) %collective-permute-start.3) | collective-permute-done | bytes 552992 | tf_op jit(solution)/shard_map/ppermute | solution.py:28
  30.1 11.8 %collective-permute-done.5.refs_0_ = bf16[72,3840]{1,0:T(8,128)(2,1)S(1)} collective-permute-done((bf16[72,3840]{1,0:T(8,128)(2,1)}, bf16[72,3840]{1,0:T(8,128)(2,1)S(1)}, u32[]{:S(2)}, u32[]{:S(2)}) %collective-permute-start.5) | collective-permute-done | bytes 552992 | tf_op jit(solution)/shard_map/ppermute | solution.py:28
  41.9 11.6 %collective-permute-done.9.refs_0_ = bf16[72,3840]{1,0:T(8,128)(2,1)S(1)} collective-permute-done((bf16[72,3840]{1,0:T(8,128)(2,1)S(1)}, bf16[72,3840]{1,0:T(8,128)(2,1)S(1)}, u32[]{:S(2)}, u32[]{:S(2)}) %collective-permute-start.9) | collective-permute-done | bytes 552992 | tf_op jit(solution)/shard_map/ppermute | solution.py:28
  54.2 11.3 %similarities.5 = (f32[64,128]{1,0:T(8,128)S(1)}, bf16[9,128,3840]{2,1,0:T(8,128)(2,1)S(1)}) custom-call(s32[14]{0:T(128)S(1)} %stack.53.pos_ref, s32[4,4]{1,0:T(4,128)S(1)} %copy-done, bf16[9,128,3840]{2,1,0:T(8,128)(2,1)} %bitcast.42, bf16[288,3840]{1,0:T(8,128)(2,1)} %bitcast.41, bf16[288,3840]{1,0:T(8,128)(2,1)} %collective-permute-done.refs_1_), custom_call_target="tpu_custom_call" | custom-call | flops 5096079360 | bytes 4423680 | tf_op jit(solution)/shard_map/similarities/pallas_call | solution.py:173
  65.5 3.2 %similarities.6.refs_1_.refs_3_ = f32[16,128]{1,0:T(8,128)S(1)} custom-call(s32[14]{0:T(128)S(1)} %stack.53.pos_ref, s32[4,4]{1,0:T(4,128)S(1)} %copy-done, bf16[9,128,3840]{2,1,0:T(8,128)(2,1)S(1)} %get-tuple-element.23.query_ref, bf16[72,3840]{1,0:T(8,128)(2,1)S(1)} %collective-permute-done.1.refs_0_, bf16[72,3840]{1,0:T(8,128)(2,1)S(1)} %collective-permute-done.2.refs_1_), custom_call_target="tpu_custom_call" | custom-call | flops 1274019840 | bytes 1105920 | tf_op jit(solution)/shard_map/similarities/pallas_call | solution.py:173
  68.7 1.3 %collective-permute-start.8 = (f32[8,128]{1,0:T(8,128)S(1)}, f32[8,128]{1,0:T(8,128)S(1)}, u32[]{:S(2)}, u32[]{:S(2)}) collective-permute-start(f32[8,128]{1,0:T(8,128)S(1)} %pad_maximum_fusion.1), channel_id=1, source_target_pairs={{1,0},{2,1},{3,2},{5,4},{6,5},{7,6},{9,8},{10,9},{11,10},{13,12},{... | collective-permute-start | bytes 12296 | tf_op jit(solution)/shard_map/ppermute | solution.py:28
  70.0 3.2 %similarities.7.refs_2_.refs_4_ = f32[16,128]{1,0:T(8,128)S(1)} custom-call(s32[14]{0:T(128)S(1)} %stack.53.pos_ref, s32[4,4]{1,0:T(4,128)S(1)} %copy-done, bf16[9,128,3840]{2,1,0:T(8,128)(2,1)S(1)} %get-tuple-element.23.query_ref, bf16[72,3840]{1,0:T(8,128)(2,1)S(1)} %collective-permute-done.3.refs_0_, bf16[72,3840]{1,0:T(8,128)(2,1)S(1)} %collective-permute-done.4.refs_1_), custom_call_target="tpu_custom_call" | custom-call | flops 1274019840 | bytes 1105920 | tf_op jit(solution)/shard_map/similarities/pallas_call | solution.py:173
  73.3 4.9 %collective-permute-start.7 = (f32[8,128]{1,0:T(8,128)S(1)}, f32[8,128]{1,0:T(8,128)S(1)}, u32[]{:S(2)}, u32[]{:S(2)}) collective-permute-start(f32[8,128]{1,0:T(8,128)S(1)} %pad_maximum_fusion), channel_id=1, source_target_pairs={{0,1},{1,2},{2,3},{4,5},{5,6},{6,7},{8,9},{9,10},{10,11},{12,13},{... | collective-permute-start | bytes 12296 | tf_op jit(solution)/shard_map/ppermute | solution.py:28
  78.2 3.2 %similarities.8.refs_3_.refs_5_ = f32[16,128]{1,0:T(8,128)S(1)} custom-call(s32[14]{0:T(128)S(1)} %stack.53.pos_ref, s32[4,4]{1,0:T(4,128)S(1)} %copy-done, bf16[9,128,3840]{2,1,0:T(8,128)(2,1)S(1)} %get-tuple-element.23.query_ref, bf16[72,3840]{1,0:T(8,128)(2,1)S(1)} %collective-permute-done.5.refs_0_, bf16[72,3840]{1,0:T(8,128)(2,1)S(1)} %collective-permute-done.6.refs_1_), custom_call_target="tpu_custom_call" | custom-call | flops 1274019840 | bytes 1105920 | tf_op jit(solution)/shard_map/similarities/pallas_call | solution.py:173
  81.4 3.2 %similarities.9 = (f32[16,128]{1,0:T(8,128)S(1)}, f32[8,144]{1,0:T(8,128)S(1)}, f32[8,144]{1,0:T(8,128)S(1)}) custom-call(s32[14]{0:T(128)S(1)} %stack.53.pos_ref, s32[4,4]{1,0:T(4,128)S(1)} %copy-done, bf16[9,128,3840]{2,1,0:T(8,128)(2,1)S(1)} %get-tuple-element.23.query_ref, bf16[72,3840]{1,0:T(8,128)(2,1)S(1)} %collective-permute-done.9.refs_0_, ...), custom_call_target="tpu_custom_call" | custom-call | flops 1274019840 | bytes 1105920 | tf_op jit(solution)/shard_map/similarities/pallas_call | solution.py:173
  84.7 1.8 %collective-permute-start.12 = (f32[8,144]{1,0:T(8,128)S(1)}, f32[8,144]{1,0:T(8,128)S(1)}, u32[]{:S(2)}, u32[]{:S(2)}) collective-permute-start(f32[8,144]{1,0:T(8,128)S(1)} %get-tuple-element.30), channel_id=1, source_target_pairs={{4,8},{12,0},{8,4},{0,12},{5,9},{13,1},{9,5},{1,13},{6,10},{14,2},... | collective-permute-start | bytes 13832 | tf_op jit(solution)/shard_map/ppermute | solution.py:28
  86.6 3.1 %weights.1 = (bf16[256,1536]{1,0:T(8,128)(2,1)S(1)}, f32[1,128]{1,0:T(1,128)S(1)}, bf16[512,256]{1,0:T(8,128)(2,1)S(1)}, f32[1,128]{1,0:T(1,128)S(1)}, bf16[768,...) custom-call(f32[3,3,32]{2,1,0:T(4,128)S(1)} %copy-done.3, f32[1,32]{1,0:T(1,128)S(1)} %bitcast.34, ...), custom_call_target="tpu_custom_call" | custom-call | flops 100000000 | bytes 4000000 | tf_op jit(solution)/shard_map/weights/pallas_call | solution.py:490
  91.0 4.0 %network.1 = (f32[32,32]{1,0:T(8,128)}, f32[2,32]{1,0:T(2,128)S(1)}, f32[4,56,256]{2,1,0:T(8,128)S(1)}) custom-call(s32[14]{0:T(128)S(1)} %stack.53.pos_ref, s32[2]{0:T(128)S(1)} %copy-done.8, f32[4,56,256]{2,1,0:T(8,128)S(1)} %assemble.1.base_ref, f32[16,128]{1,0:T(8,128)S(1)} %get-tuple-element.28.refs_0_, ...), custom_call_target="tpu_custom_call", output_to_operand_aliasing={{2}: (2, {})} | custom-call | flops 6000000000 | bytes 4000000 | tf_op jit(solution)/shard_map/network/pallas_call | solution.py:403
  94.9 1.6 %collective-permute-start.13 = (f32[2,32]{1,0:T(2,128)S(1)}, f32[2,32]{1,0:T(2,128)S(1)}, u32[]{:S(2)}, u32[]{:S(2)}) collective-permute-start(f32[2,32]{1,0:T(2,128)S(1)} %get-tuple-element.39), channel_id=1, source_target_pairs={{0,1},{1,0},{2,3},{3,2},{4,5},{5,4},{6,7},{7,6},{8,9},{9,8},{10,11... | collective-permute-start | bytes 776 | tf_op jit(solution)/shard_map/ppermute | solution.py:28
  97.2 1.3 %collective-permute-done.13 = f32[2,32]{1,0:T(2,128)S(1)} collective-permute-done((f32[2,32]{1,0:T(2,128)S(1)}, f32[2,32]{1,0:T(2,128)S(1)}, u32[]{:S(2)}, u32[]{:S(2)}) %collective-permute-start.13) | collective-permute-done | bytes 288 | tf_op jit(solution)/shard_map/ppermute | solution.py:28
  98.5 2.6 %collective-permute-start.14 = (f32[2,32]{1,0:T(2,128)S(1)}, f32[2,32]{1,0:T(2,128)S(1)}, u32[]{:S(2)}, u32[]{:S(2)}) collective-permute-start(f32[2,32]{1,0:T(2,128)S(1)} %max.6), channel_id=1, source_target_pairs={{0,2},{1,3},{2,0},{3,1},{4,6},{5,7},{6,4},{7,5},{8,10},{9,11},{10,... | collective-permute-start | bytes 776 | tf_op jit(solution)/shard_map/ppermute | solution.py:28
  101.1 1.9 %collective-permute-done.14 = f32[2,32]{1,0:T(2,128)S(1)} collective-permute-done((f32[2,32]{1,0:T(2,128)S(1)}, f32[2,32]{1,0:T(2,128)S(1)}, u32[]{:S(2)}, u32[]{:S(2)}) %collective-permute-start.14) | collective-permute-done | bytes 288 | tf_op jit(solution)/shard_map/ppermute | solution.py:28
  103.5 3.3 %collective-permute-done.15 = f32[2]{0:T(128)S(1)} collective-permute-done((f32[2]{0:T(128)S(1)}, f32[2]{0:T(128)S(1)}, u32[]{:S(2)}, u32[]{:S(2)}) %collective-permute-start.15) | collective-permute-done | bytes 40 | tf_op jit(solution)/shard_map/ppermute | solution.py:28
  106.7 1.2 %collective-permute-done.16 = f32[2]{0:T(128)S(1)} collective-permute-done((f32[2]{0:T(128)S(1)}, f32[2]{0:T(128)S(1)}, u32[]{:S(2)}, u32[]{:S(2)}) %collective-permute-start.16) | collective-permute-done | bytes 40 | tf_op jit(solution)/shard_map/ppermute | solution.py:28
  (49 shorter events, 3.2 us)
Async XLA Ops:
  1.7 51.8 %collective-permute-start = (bf16[288,3840]{1,0:T(8,128)(2,1)}, bf16[288,3840]{1,0:T(8,128)(2,1)}, u32[]{:S(2)}, u32[]{:S(2)}) collective-permute-start(bf16[288,3840]{1,0:T(8,128)(2,1)} %bitcast.39), channel_id=1, source_target_pairs={{0,4},{4,0},{8,12},{12,8},{1,5},{5,1},{9,13},{13,9},{2,6},{6,2},{1... | collective-permute-start | bytes 6635528 | tf_op jit(solution)/shard_map/ppermute | solution.py:28
  2.3 15.9 %collective-permute-start.1 = (bf16[72,3840]{1,0:T(8,128)(2,1)S(1)}, bf16[72,3840]{1,0:T(8,128)(2,1)S(1)}, u32[]{:S(2)}, u32[]{:S(2)}) collective-permute-start(bf16[72,3840]{1,0:T(8,128)(2,1)S(1)} %bitcast.30), channel_id=1, source_target_pairs={{0,8},{4,12},{8,0},{12,4},{1,9},{5,13},{9,1},{13,5},{2,10},{6,14},... | collective-permute-start | bytes 1658888 | tf_op jit(solution)/shard_map/ppermute | solution.py:28
  7.2 22.8 %collective-permute-start.3 = (bf16[72,3840]{1,0:T(8,128)(2,1)}, bf16[72,3840]{1,0:T(8,128)(2,1)S(1)}, u32[]{:S(2)}, u32[]{:S(2)}) collective-permute-start(bf16[72,3840]{1,0:T(8,128)(2,1)} %bitcast.18), channel_id=1, source_target_pairs={{0,8},{4,12},{8,0},{12,4},{1,9},{5,13},{9,1},{13,5},{2,10},{6,14},... | collective-permute-start | bytes 1658888 | tf_op jit(solution)/shard_map/ppermute | solution.py:28
  7.3 34.6 %collective-permute-start.5 = (bf16[72,3840]{1,0:T(8,128)(2,1)}, bf16[72,3840]{1,0:T(8,128)(2,1)S(1)}, u32[]{:S(2)}, u32[]{:S(2)}) collective-permute-start(bf16[72,3840]{1,0:T(8,128)(2,1)} %bitcast.19), channel_id=1, source_target_pairs={{0,8},{4,12},{8,0},{12,4},{1,9},{5,13},{9,1},{13,5},{2,10},{6,14},... | collective-permute-start | bytes 1658888 | tf_op jit(solution)/shard_map/ppermute | solution.py:28
  9.3 44.1 %collective-permute-start.9 = (bf16[72,3840]{1,0:T(8,128)(2,1)S(1)}, bf16[72,3840]{1,0:T(8,128)(2,1)S(1)}, u32[]{:S(2)}, u32[]{:S(2)}) collective-permute-start(bf16[72,3840]{1,0:T(8,128)(2,1)S(1)} %bitcast.31), channel_id=1, source_target_pairs={{0,8},{4,12},{8,0},{12,4},{1,9},{5,13},{9,1},{13,5},{2,10},{6,14},... | collective-permute-start | bytes 1658888 | tf_op jit(solution)/shard_map/ppermute | solution.py:28
  18.2 47.3 %collective-permute-start.2 = (bf16[72,3840]{1,0:T(8,128)(2,1)S(1)}, bf16[72,3840]{1,0:T(8,128)(2,1)S(1)}, u32[]{:S(2)}, u32[]{:S(2)}) collective-permute-start(bf16[72,3840]{1,0:T(8,128)(2,1)S(1)} %collective-permute-done.1.refs_0_), channel_id=1, source_target_pairs={{0,4},{4,0},{8,12},{12,8},{1,5},{5,1},{9,13},{13,9},{2,6},{6,2},{1... | collective-permute-start | bytes 1658888 | tf_op jit(solution)/shard_map/ppermute | solution.py:28
  30.1 40.0 %collective-permute-start.4 = (bf16[72,3840]{1,0:T(8,128)(2,1)S(1)}, bf16[72,3840]{1,0:T(8,128)(2,1)S(1)}, u32[]{:S(2)}, u32[]{:S(2)}) collective-permute-start(bf16[72,3840]{1,0:T(8,128)(2,1)S(1)} %collective-permute-done.3.refs_0_), channel_id=1, source_target_pairs={{0,4},{4,0},{8,12},{12,8},{1,5},{5,1},{9,13},{13,9},{2,6},{6,2},{1... | collective-permute-start | bytes 1658888 | tf_op jit(solution)/shard_map/ppermute | solution.py:28
  41.9 36.3 %collective-permute-start.6 = (bf16[72,3840]{1,0:T(8,128)(2,1)S(1)}, bf16[72,3840]{1,0:T(8,128)(2,1)S(1)}, u32[]{:S(2)}, u32[]{:S(2)}) collective-permute-start(bf16[72,3840]{1,0:T(8,128)(2,1)S(1)} %collective-permute-done.5.refs_0_), channel_id=1, source_target_pairs={{0,4},{4,0},{8,12},{12,8},{1,5},{5,1},{9,13},{13,9},{2,6},{6,2},{1... | collective-permute-start | bytes 1658888 | tf_op jit(solution)/shard_map/ppermute | solution.py:28
  53.5 27.9 %collective-permute-start.10 = (bf16[72,3840]{1,0:T(8,128)(2,1)S(1)}, bf16[72,3840]{1,0:T(8,128)(2,1)S(1)}, u32[]{:S(2)}, u32[]{:S(2)}) collective-permute-start(bf16[72,3840]{1,0:T(8,128)(2,1)S(1)} %collective-permute-done.9.refs_0_), channel_id=1, source_target_pairs={{0,4},{4,0},{8,12},{12,8},{1,5},{5,1},{9,13},{13,9},{2,6},{6,2},{1... | collective-permute-start | bytes 1658888 | tf_op jit(solution)/shard_map/ppermute | solution.py:28
  68.7 12.7 %collective-permute-start.8 = (f32[8,128]{1,0:T(8,128)S(1)}, f32[8,128]{1,0:T(8,128)S(1)}, u32[]{:S(2)}, u32[]{:S(2)}) collective-permute-start(f32[8,128]{1,0:T(8,128)S(1)} %pad_maximum_fusion.1), channel_id=1, source_target_pairs={{1,0},{2,1},{3,2},{5,4},{6,5},{7,6},{9,8},{10,9},{11,10},{13,12},{... | collective-permute-start | bytes 12296 | tf_op jit(solution)/shard_map/ppermute | solution.py:28
  73.2 13.3 %copy-start.1 = (bf16[3,3,128,64]{2,3,1,0:T(8,128)(2,1)S(1)}, bf16[3,3,128,64]{2,3,1,0:T(8,128)(2,1)}, u32[]{:S(2)}) copy-start(bf16[3,3,128,64]{2,3,1,0:T(8,128)(2,1)} %param.22) | copy-start | bytes 442372
  73.3 13.3 %copy-start.2 = (bf16[3,3,64,32]{2,3,1,0:T(8,128)(2,1)S(1)}, bf16[3,3,64,32]{2,3,1,0:T(8,128)(2,1)}, u32[]{:S(2)}) copy-start(bf16[3,3,64,32]{2,3,1,0:T(8,128)(2,1)} %param.20) | copy-start | bytes 110596
  73.3 13.3 %copy-start.3 = (f32[3,3,32]{2,1,0:T(4,128)S(1)}, f32[3,3,32]{2,1,0:T(4,128)}, u32[]{:S(2)}) copy-start(f32[3,3,32]{2,1,0:T(4,128)} %w1_ref.1) | copy-start | bytes 3460
  73.3 13.3 %copy-start.4 = (f32[32]{0:T(128)S(1)}, f32[32]{0:T(128)}, u32[]{:S(2)}) copy-start(f32[32]{0:T(128)} %param.19) | copy-start | bytes 388
  73.3 13.3 %copy-start.5 = (f32[64]{0:T(128)S(1)}, f32[64]{0:T(128)}, u32[]{:S(2)}) copy-start(f32[64]{0:T(128)} %param.21) | copy-start | bytes 772
  73.3 13.3 %copy-start.6 = (f32[128]{0:T(128)S(1)}, f32[128]{0:T(128)}, u32[]{:S(2)}) copy-start(f32[128]{0:T(128)} %param.23) | copy-start | bytes 1540
  73.3 17.6 %copy-start.8 = (s32[2]{0:T(128)S(1)}, s32[2]{0:T(128)}, u32[]{:S(2)}) copy-start(s32[2]{0:T(128)} %len_ref.1) | copy-start | bytes 28
  73.3 8.1 %collective-permute-start.7 = (f32[8,128]{1,0:T(8,128)S(1)}, f32[8,128]{1,0:T(8,128)S(1)}, u32[]{:S(2)}, u32[]{:S(2)}) collective-permute-start(f32[8,128]{1,0:T(8,128)S(1)} %pad_maximum_fusion), channel_id=1, source_target_pairs={{0,1},{1,2},{2,3},{4,5},{5,6},{6,7},{8,9},{9,10},{10,11},{12,13},{... | collective-permute-start | bytes 12296 | tf_op jit(solution)/shard_map/ppermute | solution.py:28
  84.7 6.3 %collective-permute-start.11 = (f32[8,144]{1,0:T(8,128)S(1)}, f32[8,144]{1,0:T(8,128)S(1)}, u32[]{:S(2)}, u32[]{:S(2)}) collective-permute-start(f32[8,144]{1,0:T(8,128)S(1)} %get-tuple-element.29), channel_id=1, source_target_pairs={{0,4},{4,0},{8,12},{12,8},{1,5},{5,1},{9,13},{13,9},{2,6},{6,2},{1... | collective-permute-start | bytes 13832 | tf_op jit(solution)/shard_map/ppermute | solution.py:28
  84.7 6.2 %collective-permute-start.12 = (f32[8,144]{1,0:T(8,128)S(1)}, f32[8,144]{1,0:T(8,128)S(1)}, u32[]{:S(2)}, u32[]{:S(2)}) collective-permute-start(f32[8,144]{1,0:T(8,128)S(1)} %get-tuple-element.30), channel_id=1, source_target_pairs={{4,8},{12,0},{8,4},{0,12},{5,9},{13,1},{9,5},{1,13},{6,10},{14,2},... | collective-permute-start | bytes 13832 | tf_op jit(solution)/shard_map/ppermute | solution.py:28
  94.9 3.6 %collective-permute-start.13 = (f32[2,32]{1,0:T(2,128)S(1)}, f32[2,32]{1,0:T(2,128)S(1)}, u32[]{:S(2)}, u32[]{:S(2)}) collective-permute-start(f32[2,32]{1,0:T(2,128)S(1)} %get-tuple-element.39), channel_id=1, source_target_pairs={{0,1},{1,0},{2,3},{3,2},{4,5},{5,4},{6,7},{7,6},{8,9},{9,8},{10,11... | collective-permute-start | bytes 776 | tf_op jit(solution)/shard_map/ppermute | solution.py:28
  98.5 4.5 %collective-permute-start.14 = (f32[2,32]{1,0:T(2,128)S(1)}, f32[2,32]{1,0:T(2,128)S(1)}, u32[]{:S(2)}, u32[]{:S(2)}) collective-permute-start(f32[2,32]{1,0:T(2,128)S(1)} %max.6), channel_id=1, source_target_pairs={{0,2},{1,3},{2,0},{3,1},{4,6},{5,7},{6,4},{7,5},{8,10},{9,11},{10,... | collective-permute-start | bytes 776 | tf_op jit(solution)/shard_map/ppermute | solution.py:28
  103.1 3.6 %collective-permute-start.15 = (f32[2]{0:T(128)S(1)}, f32[2]{0:T(128)S(1)}, u32[]{:S(2)}, u32[]{:S(2)}) collective-permute-start(f32[2]{0:T(128)S(1)} %select_reduce_fusion), channel_id=1, source_target_pairs={{0,8},{4,12},{8,0},{12,4},{1,9},{5,13},{9,1},{13,5},{2,10},{6,14},... | collective-permute-start | bytes 32 | tf_op jit(solution)/shard_map/ppermute | solution.py:28
  106.7 1.2 %collective-permute-start.16 = (f32[2]{0:T(128)S(1)}, f32[2]{0:T(128)S(1)}, u32[]{:S(2)}, u32[]{:S(2)}) collective-permute-start(f32[2]{0:T(128)S(1)} %add.32), channel_id=1, source_target_pairs={{0,4},{4,0},{8,12},{12,8},{1,5},{5,1},{9,13},{13,9},{2,6},{6,2},{1... | collective-permute-start | bytes 32 | tf_op jit(solution)/shard_map/ppermute | solution.py:28
  (2 other events, 14.0 us)

commit v2 on v1

--- a/solution.py
+++ b/solution.py
@@ -656,17 +656,29 @@
         block,
         limits,
     )
+    place = jnp.stack([qry_index, qry_index ^ 1])
+    peaks = jnp.stack([peaks, shift(peaks, "qry", beside)])
+
+    def between_odd(array, flip_qry, flip_ref):
+        pairs = []
+        for q in range(senders):
+            for r in range(blocks):
+                to = (q ^ flip_qry, r ^ flip_ref) if q % 2 else (q, r)
+                pairs.append((q * blocks + r, to[0] * blocks + to[1]))
+        return shift(array, ("qry", "ref"), pairs)
+
     bit = 1
     while bit < blocks:
-        peaks = jnp.maximum(peaks, shift(peaks, "ref", [(i, i ^ bit) for i in range(blocks)]))
+        peaks = jnp.maximum(peaks, between_odd(peaks, 0, bit))
         bit *= 2
-    row_ids = qry_index * block + jnp.arange(block, dtype=jnp.int32)
-    total = jnp.sum(jnp.where((row_ids < query_len[0])[None], peaks, 0.0), axis=1)
+    row_ids = place[:, None] * block + jnp.arange(block, dtype=jnp.int32)[None]
+    total = jnp.sum(jnp.where((row_ids < query_len[0])[:, None], peaks, 0.0), axis=(0, 2))
     bit = senders // 2
-    while bit >= 1:
-        total = total + shift(total, "qry", [(i, i ^ bit) for i in range(senders)])
+    while bit > 1:
+        total = total + between_odd(total, bit, 0)
         bit //= 2
-    return (score_map, total / query_len[0].astype(F32))
+    given = shift(total, "qry", beside)
+    return (score_map, jnp.where(odd == 1, total, given) / query_len[0].astype(F32))
 
 
 def solution(mesh):

time: 109 us -> 112 us (1.028)
  starting transfers between devices: 17.9 us -> 26.5 us
  waiting for transfers between devices: 51.6 us -> 45.9 us
    ppermute x17 -> x18, starting transfers between devices: 17.9 us -> 26.5 us  [shift(): return lax.ppermute(array, axis, pairs)]
    ppermute x17 -> x18, waiting for transfers between devices: 51.6 us -> 45.9 us  [shift(): return lax.ppermute(array, axis, pairs)]
  transfers between devices with their start and end apart: 17 -> 18, of which waited for: 8 -> 6; matrix products, arithmetic and copies ran while one was open for 0% -> 0% of each run, Pallas kernels for 25% -> 24%
where the time goes in v2:
time: 112 us
  waiting for transfers between devices  45.9 us (41%)
  Pallas kernels  35.2 us (31%)
  starting transfers between devices  26.5 us (24%)
  between operations  2.28 us (2%)
    ppermute x18, waiting for transfers between devices, shift(): return lax.ppermute(array, axis, pairs)  45.9 us
    ppermute x18, starting transfers between devices, shift(): return lax.ppermute(array, axis, pairs)  26.5 us
    pallas_call x5, Pallas kernels, similarities(): pl.pallas_call(functools.partial(sims_kernel, scale, spans, len(done), fe...  24.1 us
    pallas_call x1, Pallas kernels, network(): pl.pallas_call(functools.partial(network_kernel, limits, padding, starts,...  3.98 us
    pallas_call x2, Pallas kernels, cut(): pl.pallas_call(functools.partial(cut_kernel, order), in_specs=[pl.BlockSp...  3.49 us
    pallas_call x1, Pallas kernels, network_weights(): pl.pallas_call(weights_kernel, out_shape=[jax.ShapeDtypeStruct(shape, dty...  3.09 us
  transfers between devices with their start and end apart: 18, of which 6 were waited for; matrix products, arithmetic and copies ran while one was open for 0% of the time, Pallas kernels for 24%

profile of v2, /device:TPU:0, one launch (start us, length us, event | category | flops | bytes accessed | tf_op | source)
XLA Modules:
  0.0 111.6 jit_solution(11772732002560676628)
XLA Ops:
  0.6 1.1 cut.2
  2.3 2.6 %collective-permute-start.1 = (bf16[72,3840]{1,0:T(8,128)(2,1)S(1)}, bf16[72,3840]{1,0:T(8,128)(2,1)S(1)}, u32[]{:S(2)}, u32[]{:S(2)}) collective-permute-start(bf16[72,3840]{1,0:T(8,128)(2,1)S(1)} %bitcast.32), channel_id=1, source_target_pairs={{0,8},{4,12},{8,0},{12,4},{1,9},{5,13},{9,1},{13,5},{2,10},{6,14},... | collective-permute-start | bytes 1658888 | tf_op jit(solution)/shard_map/ppermute | solution.py:28
  4.8 2.4 %cut.3 = (bf16[9,8,3840]{2,1,0:T(8,128)(2,1)}, bf16[9,8,3840]{2,1,0:T(8,128)(2,1)}, bf16[9,8,3840]{2,1,0:T(8,128)(2,1)S(1)}) custom-call(bf16[9,32,3840]{2,1,0:T(8,128)(2,1)} %bitcast.45), custom_call_target="tpu_custom_call" | custom-call | bytes 4423680 | tf_op jit(solution)/shard_map/cut/pallas_call | solution.py:46
  7.3 2.0 %collective-permute-start.5 = (bf16[72,3840]{1,0:T(8,128)(2,1)}, bf16[72,3840]{1,0:T(8,128)(2,1)S(1)}, u32[]{:S(2)}, u32[]{:S(2)}) collective-permute-start(bf16[72,3840]{1,0:T(8,128)(2,1)} %bitcast.19), channel_id=1, source_target_pairs={{0,8},{4,12},{8,0},{12,4},{1,9},{5,13},{9,1},{13,5},{2,10},{6,14},... | collective-permute-start | bytes 1658888 | tf_op jit(solution)/shard_map/ppermute | solution.py:28
  9.4 8.8 %collective-permute-done.1.refs_0_ = bf16[72,3840]{1,0:T(8,128)(2,1)S(1)} collective-permute-done((bf16[72,3840]{1,0:T(8,128)(2,1)S(1)}, bf16[72,3840]{1,0:T(8,128)(2,1)S(1)}, u32[]{:S(2)}, u32[]{:S(2)}) %collective-permute-start.1) | collective-permute-done | bytes 552992 | tf_op jit(solution)/shard_map/ppermute | solution.py:28
  18.3 11.8 %collective-permute-done.3.refs_0_ = bf16[72,3840]{1,0:T(8,128)(2,1)S(1)} collective-permute-done((bf16[72,3840]{1,0:T(8,128)(2,1)}, bf16[72,3840]{1,0:T(8,128)(2,1)S(1)}, u32[]{:S(2)}, u32[]{:S(2)}) %collective-permute-start.3) | collective-permute-done | bytes 552992 | tf_op jit(solution)/shard_map/ppermute | solution.py:28
  30.1 11.8 %collective-permute-done.5.refs_0_ = bf16[72,3840]{1,0:T(8,128)(2,1)S(1)} collective-permute-done((bf16[72,3840]{1,0:T(8,128)(2,1)}, bf16[72,3840]{1,0:T(8,128)(2,1)S(1)}, u32[]{:S(2)}, u32[]{:S(2)}) %collective-permute-start.5) | collective-permute-done | bytes 552992 | tf_op jit(solution)/shard_map/ppermute | solution.py:28
  41.9 11.6 %collective-permute-done.9.refs_0_ = bf16[72,3840]{1,0:T(8,128)(2,1)S(1)} collective-permute-done((bf16[72,3840]{1,0:T(8,128)(2,1)S(1)}, bf16[72,3840]{1,0:T(8,128)(2,1)S(1)}, u32[]{:S(2)}, u32[]{:S(2)}) %collective-permute-start.9) | collective-permute-done | bytes 552992 | tf_op jit(solution)/shard_map/ppermute | solution.py:28
  53.5 0.7 copy-done
  54.2 11.3 %similarities.5 = (f32[64,128]{1,0:T(8,128)S(1)}, bf16[9,128,3840]{2,1,0:T(8,128)(2,1)S(1)}) custom-call(s32[14]{0:T(128)S(1)} %stack.67.pos_ref, s32[4,4]{1,0:T(4,128)S(1)} %copy-done, bf16[9,128,3840]{2,1,0:T(8,128)(2,1)} %bitcast.50, bf16[288,3840]{1,0:T(8,128)(2,1)} %bitcast.46, bf16[288,3840]{1,0:T(8,128)(2,1)} %collective-permute-done.refs_1_), custom_call_target="tpu_custom_call" | custom-call | flops 5096079360 | bytes 4423680 | tf_op jit(solution)/shard_map/similarities/pallas_call | solution.py:173
  65.5 3.2 %similarities.6.refs_1_.refs_3_ = f32[16,128]{1,0:T(8,128)S(1)} custom-call(s32[14]{0:T(128)S(1)} %stack.67.pos_ref, s32[4,4]{1,0:T(4,128)S(1)} %copy-done, bf16[9,128,3840]{2,1,0:T(8,128)(2,1)S(1)} %get-tuple-element.23.query_ref, bf16[72,3840]{1,0:T(8,128)(2,1)S(1)} %collective-permute-done.1.refs_0_, bf16[72,3840]{1,0:T(8,128)(2,1)S(1)} %collective-permute-done.2.refs_1_), custom_call_target="tpu_custom_call" | custom-call | flops 1274019840 | bytes 1105920 | tf_op jit(solution)/shard_map/similarities/pallas_call | solution.py:173
  68.7 1.3 %collective-permute-start.8 = (f32[8,128]{1,0:T(8,128)S(1)}, f32[8,128]{1,0:T(8,128)S(1)}, u32[]{:S(2)}, u32[]{:S(2)}) collective-permute-start(f32[8,128]{1,0:T(8,128)S(1)} %pad_maximum_fusion.1), channel_id=1, source_target_pairs={{1,0},{2,1},{3,2},{5,4},{6,5},{7,6},{9,8},{10,9},{11,10},{13,12},{... | collective-permute-start | bytes 12296 | tf_op jit(solution)/shard_map/ppermute | solution.py:28
  70.0 3.2 %similarities.7.refs_2_.refs_4_ = f32[16,128]{1,0:T(8,128)S(1)} custom-call(s32[14]{0:T(128)S(1)} %stack.67.pos_ref, s32[4,4]{1,0:T(4,128)S(1)} %copy-done, bf16[9,128,3840]{2,1,0:T(8,128)(2,1)S(1)} %get-tuple-element.23.query_ref, bf16[72,3840]{1,0:T(8,128)(2,1)S(1)} %collective-permute-done.3.refs_0_, bf16[72,3840]{1,0:T(8,128)(2,1)S(1)} %collective-permute-done.4.refs_1_), custom_call_target="tpu_custom_call" | custom-call | flops 1274019840 | bytes 1105920 | tf_op jit(solution)/shard_map/similarities/pallas_call | solution.py:173
  73.3 4.9 %collective-permute-start.7 = (f32[8,128]{1,0:T(8,128)S(1)}, f32[8,128]{1,0:T(8,128)S(1)}, u32[]{:S(2)}, u32[]{:S(2)}) collective-permute-start(f32[8,128]{1,0:T(8,128)S(1)} %pad_maximum_fusion), channel_id=1, source_target_pairs={{0,1},{1,2},{2,3},{4,5},{5,6},{6,7},{8,9},{9,10},{10,11},{12,13},{... | collective-permute-start | bytes 12296 | tf_op jit(solution)/shard_map/ppermute | solution.py:28
  78.2 3.2 %similarities.8.refs_3_.refs_5_ = f32[16,128]{1,0:T(8,128)S(1)} custom-call(s32[14]{0:T(128)S(1)} %stack.67.pos_ref, s32[4,4]{1,0:T(4,128)S(1)} %copy-done, bf16[9,128,3840]{2,1,0:T(8,128)(2,1)S(1)} %get-tuple-element.23.query_ref, bf16[72,3840]{1,0:T(8,128)(2,1)S(1)} %collective-permute-done.5.refs_0_, bf16[72,3840]{1,0:T(8,128)(2,1)S(1)} %collective-permute-done.6.refs_1_), custom_call_target="tpu_custom_call" | custom-call | flops 1274019840 | bytes 1105920 | tf_op jit(solution)/shard_map/similarities/pallas_call | solution.py:173
  81.4 3.2 %similarities.9 = (f32[16,128]{1,0:T(8,128)S(1)}, f32[8,144]{1,0:T(8,128)S(1)}, f32[8,144]{1,0:T(8,128)S(1)}) custom-call(s32[14]{0:T(128)S(1)} %stack.67.pos_ref, s32[4,4]{1,0:T(4,128)S(1)} %copy-done, bf16[9,128,3840]{2,1,0:T(8,128)(2,1)S(1)} %get-tuple-element.23.query_ref, bf16[72,3840]{1,0:T(8,128)(2,1)S(1)} %collective-permute-done.9.refs_0_, ...), custom_call_target="tpu_custom_call" | custom-call | flops 1274019840 | bytes 1105920 | tf_op jit(solution)/shard_map/similarities/pallas_call | solution.py:173
  84.7 1.8 %collective-permute-start.12 = (f32[8,144]{1,0:T(8,128)S(1)}, f32[8,144]{1,0:T(8,128)S(1)}, u32[]{:S(2)}, u32[]{:S(2)}) collective-permute-start(f32[8,144]{1,0:T(8,128)S(1)} %get-tuple-element.30), channel_id=1, source_target_pairs={{4,8},{12,0},{8,4},{0,12},{5,9},{13,1},{9,5},{1,13},{6,10},{14,2},... | collective-permute-start | bytes 13832 | tf_op jit(solution)/shard_map/ppermute | solution.py:28
  86.6 3.1 %weights.1 = (bf16[256,1536]{1,0:T(8,128)(2,1)S(1)}, f32[1,128]{1,0:T(1,128)S(1)}, bf16[512,256]{1,0:T(8,128)(2,1)S(1)}, f32[1,128]{1,0:T(1,128)S(1)}, bf16[768,...) custom-call(f32[3,3,32]{2,1,0:T(4,128)S(1)} %copy-done.3, f32[1,32]{1,0:T(1,128)S(1)} %bitcast.39, ...), custom_call_target="tpu_custom_call" | custom-call | flops 100000000 | bytes 4000000 | tf_op jit(solution)/shard_map/weights/pallas_call | solution.py:490
  91.0 4.0 %network.1 = (f32[32,32]{1,0:T(8,128)}, f32[2,32]{1,0:T(2,128)S(1)}, f32[4,56,256]{2,1,0:T(8,128)S(1)}) custom-call(s32[14]{0:T(128)S(1)} %stack.67.pos_ref, s32[2]{0:T(128)S(1)} %copy-done.8, f32[4,56,256]{2,1,0:T(8,128)S(1)} %assemble.1.base_ref, f32[16,128]{1,0:T(8,128)S(1)} %get-tuple-element.28.refs_0_, ...), custom_call_target="tpu_custom_call", output_to_operand_aliasing={{2}: (2, {})} | custom-call | flops 6000000000 | bytes 4000000 | tf_op jit(solution)/shard_map/network/pallas_call | solution.py:403
  95.0 1.1 collective-permute-done.13
  97.5 0.7 collective-permute-start.15
  98.4 0.7 collective-permute-start.16
  99.1 11.2 %collective-permute-start.17 = (f32[2]{0:T(128)S(1)}, f32[2]{0:T(128)S(1)}, u32[]{:S(2)}, u32[]{:S(2)}) collective-permute-start(f32[2]{0:T(128)S(1)} %add.37), channel_id=1, source_target_pairs={{0,4},{4,0},{8,12},{12,8},{1,5},{5,1},{9,13},{13,9},{2,6},{6,2},{1... | collective-permute-start | bytes 32 | tf_op jit(solution)/shard_map/ppermute | solution.py:28
  110.2 0.8 collective-permute-done.17
  (53 shorter events, 3.1 us)
Async XLA Ops:
  1.7 51.8 %collective-permute-start = (bf16[288,3840]{1,0:T(8,128)(2,1)}, bf16[288,3840]{1,0:T(8,128)(2,1)}, u32[]{:S(2)}, u32[]{:S(2)}) collective-permute-start(bf16[288,3840]{1,0:T(8,128)(2,1)} %bitcast.44), channel_id=1, source_target_pairs={{0,4},{4,0},{8,12},{12,8},{1,5},{5,1},{9,13},{13,9},{2,6},{6,2},{1... | collective-permute-start | bytes 6635528 | tf_op jit(solution)/shard_map/ppermute | solution.py:28
  2.3 15.9 %collective-permute-start.1 = (bf16[72,3840]{1,0:T(8,128)(2,1)S(1)}, bf16[72,3840]{1,0:T(8,128)(2,1)S(1)}, u32[]{:S(2)}, u32[]{:S(2)}) collective-permute-start(bf16[72,3840]{1,0:T(8,128)(2,1)S(1)} %bitcast.32), channel_id=1, source_target_pairs={{0,8},{4,12},{8,0},{12,4},{1,9},{5,13},{9,1},{13,5},{2,10},{6,14},... | collective-permute-start | bytes 1658888 | tf_op jit(solution)/shard_map/ppermute | solution.py:28
  7.2 22.8 %collective-permute-start.3 = (bf16[72,3840]{1,0:T(8,128)(2,1)}, bf16[72,3840]{1,0:T(8,128)(2,1)S(1)}, u32[]{:S(2)}, u32[]{:S(2)}) collective-permute-start(bf16[72,3840]{1,0:T(8,128)(2,1)} %bitcast.18), channel_id=1, source_target_pairs={{0,8},{4,12},{8,0},{12,4},{1,9},{5,13},{9,1},{13,5},{2,10},{6,14},... | collective-permute-start | bytes 1658888 | tf_op jit(solution)/shard_map/ppermute | solution.py:28
  7.3 34.6 %collective-permute-start.5 = (bf16[72,3840]{1,0:T(8,128)(2,1)}, bf16[72,3840]{1,0:T(8,128)(2,1)S(1)}, u32[]{:S(2)}, u32[]{:S(2)}) collective-permute-start(bf16[72,3840]{1,0:T(8,128)(2,1)} %bitcast.19), channel_id=1, source_target_pairs={{0,8},{4,12},{8,0},{12,4},{1,9},{5,13},{9,1},{13,5},{2,10},{6,14},... | collective-permute-start | bytes 1658888 | tf_op jit(solution)/shard_map/ppermute | solution.py:28
  9.3 44.2 %collective-permute-start.9 = (bf16[72,3840]{1,0:T(8,128)(2,1)S(1)}, bf16[72,3840]{1,0:T(8,128)(2,1)S(1)}, u32[]{:S(2)}, u32[]{:S(2)}) collective-permute-start(bf16[72,3840]{1,0:T(8,128)(2,1)S(1)} %bitcast.36), channel_id=1, source_target_pairs={{0,8},{4,12},{8,0},{12,4},{1,9},{5,13},{9,1},{13,5},{2,10},{6,14},... | collective-permute-start | bytes 1658888 | tf_op jit(solution)/shard_map/ppermute | solution.py:28
  18.2 47.3 %collective-permute-start.2 = (bf16[72,3840]{1,0:T(8,128)(2,1)S(1)}, bf16[72,3840]{1,0:T(8,128)(2,1)S(1)}, u32[]{:S(2)}, u32[]{:S(2)}) collective-permute-start(bf16[72,3840]{1,0:T(8,128)(2,1)S(1)} %collective-permute-done.1.refs_0_), channel_id=1, source_target_pairs={{0,4},{4,0},{8,12},{12,8},{1,5},{5,1},{9,13},{13,9},{2,6},{6,2},{1... | collective-permute-start | bytes 1658888 | tf_op jit(solution)/shard_map/ppermute | solution.py:28
  30.1 40.0 %collective-permute-start.4 = (bf16[72,3840]{1,0:T(8,128)(2,1)S(1)}, bf16[72,3840]{1,0:T(8,128)(2,1)S(1)}, u32[]{:S(2)}, u32[]{:S(2)}) collective-permute-start(bf16[72,3840]{1,0:T(8,128)(2,1)S(1)} %collective-permute-done.3.refs_0_), channel_id=1, source_target_pairs={{0,4},{4,0},{8,12},{12,8},{1,5},{5,1},{9,13},{13,9},{2,6},{6,2},{1... | collective-permute-start | bytes 1658888 | tf_op jit(solution)/shard_map/ppermute | solution.py:28
  41.9 36.3 %collective-permute-start.6 = (bf16[72,3840]{1,0:T(8,128)(2,1)S(1)}, bf16[72,3840]{1,0:T(8,128)(2,1)S(1)}, u32[]{:S(2)}, u32[]{:S(2)}) collective-permute-start(bf16[72,3840]{1,0:T(8,128)(2,1)S(1)} %collective-permute-done.5.refs_0_), channel_id=1, source_target_pairs={{0,4},{4,0},{8,12},{12,8},{1,5},{5,1},{9,13},{13,9},{2,6},{6,2},{1... | collective-permute-start | bytes 1658888 | tf_op jit(solution)/shard_map/ppermute | solution.py:28
  53.5 27.9 %collective-permute-start.10 = (bf16[72,3840]{1,0:T(8,128)(2,1)S(1)}, bf16[72,3840]{1,0:T(8,128)(2,1)S(1)}, u32[]{:S(2)}, u32[]{:S(2)}) collective-permute-start(bf16[72,3840]{1,0:T(8,128)(2,1)S(1)} %collective-permute-done.9.refs_0_), channel_id=1, source_target_pairs={{0,4},{4,0},{8,12},{12,8},{1,5},{5,1},{9,13},{13,9},{2,6},{6,2},{1... | collective-permute-start | bytes 1658888 | tf_op jit(solution)/shard_map/ppermute | solution.py:28
  68.7 12.7 %collective-permute-start.8 = (f32[8,128]{1,0:T(8,128)S(1)}, f32[8,128]{1,0:T(8,128)S(1)}, u32[]{:S(2)}, u32[]{:S(2)}) collective-permute-start(f32[8,128]{1,0:T(8,128)S(1)} %pad_maximum_fusion.1), channel_id=1, source_target_pairs={{1,0},{2,1},{3,2},{5,4},{6,5},{7,6},{9,8},{10,9},{11,10},{13,12},{... | collective-permute-start | bytes 12296 | tf_op jit(solution)/shard_map/ppermute | solution.py:28
  73.2 13.3 %copy-start.1 = (bf16[3,3,128,64]{2,3,1,0:T(8,128)(2,1)S(1)}, bf16[3,3,128,64]{2,3,1,0:T(8,128)(2,1)}, u32[]{:S(2)}) copy-start(bf16[3,3,128,64]{2,3,1,0:T(8,128)(2,1)} %param.22) | copy-start | bytes 442372
  73.3 13.3 %copy-start.2 = (bf16[3,3,64,32]{2,3,1,0:T(8,128)(2,1)S(1)}, bf16[3,3,64,32]{2,3,1,0:T(8,128)(2,1)}, u32[]{:S(2)}) copy-start(bf16[3,3,64,32]{2,3,1,0:T(8,128)(2,1)} %param.20) | copy-start | bytes 110596
  73.3 13.3 %copy-start.3 = (f32[3,3,32]{2,1,0:T(4,128)S(1)}, f32[3,3,32]{2,1,0:T(4,128)}, u32[]{:S(2)}) copy-start(f32[3,3,32]{2,1,0:T(4,128)} %w1_ref.1) | copy-start | bytes 3460
  73.3 13.3 %copy-start.4 = (f32[32]{0:T(128)S(1)}, f32[32]{0:T(128)}, u32[]{:S(2)}) copy-start(f32[32]{0:T(128)} %param.19) | copy-start | bytes 388
  73.3 13.3 %copy-start.5 = (f32[64]{0:T(128)S(1)}, f32[64]{0:T(128)}, u32[]{:S(2)}) copy-start(f32[64]{0:T(128)} %param.21) | copy-start | bytes 772
  73.3 17.6 %copy-start.8 = (s32[2]{0:T(128)S(1)}, s32[2]{0:T(128)}, u32[]{:S(2)}) copy-start(s32[2]{0:T(128)} %len_ref.1) | copy-start | bytes 28
  73.3 8.1 %collective-permute-start.7 = (f32[8,128]{1,0:T(8,128)S(1)}, f32[8,128]{1,0:T(8,128)S(1)}, u32[]{:S(2)}, u32[]{:S(2)}) collective-permute-start(f32[8,128]{1,0:T(8,128)S(1)} %pad_maximum_fusion), channel_id=1, source_target_pairs={{0,1},{1,2},{2,3},{4,5},{5,6},{6,7},{8,9},{9,10},{10,11},{12,13},{... | collective-permute-start | bytes 12296 | tf_op jit(solution)/shard_map/ppermute | solution.py:28
  84.7 6.3 %collective-permute-start.11 = (f32[8,144]{1,0:T(8,128)S(1)}, f32[8,144]{1,0:T(8,128)S(1)}, u32[]{:S(2)}, u32[]{:S(2)}) collective-permute-start(f32[8,144]{1,0:T(8,128)S(1)} %get-tuple-element.29), channel_id=1, source_target_pairs={{0,4},{4,0},{8,12},{12,8},{1,5},{5,1},{9,13},{13,9},{2,6},{6,2},{1... | collective-permute-start | bytes 13832 | tf_op jit(solution)/shard_map/ppermute | solution.py:28
  84.7 6.2 %collective-permute-start.12 = (f32[8,144]{1,0:T(8,128)S(1)}, f32[8,144]{1,0:T(8,128)S(1)}, u32[]{:S(2)}, u32[]{:S(2)}) collective-permute-start(f32[8,144]{1,0:T(8,128)S(1)} %get-tuple-element.30), channel_id=1, source_target_pairs={{4,8},{12,0},{8,4},{0,12},{5,9},{13,1},{9,5},{1,13},{6,10},{14,2},... | collective-permute-start | bytes 13832 | tf_op jit(solution)/shard_map/ppermute | solution.py:28
  94.9 1.2 %collective-permute-start.13 = (f32[2,32]{1,0:T(2,128)S(1)}, f32[2,32]{1,0:T(2,128)S(1)}, u32[]{:S(2)}, u32[]{:S(2)}) collective-permute-start(f32[2,32]{1,0:T(2,128)S(1)} %get-tuple-element.39), channel_id=1, source_target_pairs={{0,4},{4,0},{8,12},{12,8},{1,5},{5,1},{9,13},{13,9},{2,6},{6,2},{1... | collective-permute-start | bytes 776 | tf_op jit(solution)/shard_map/ppermute | solution.py:28
  96.1 1.4 %collective-permute-start.14 = (f32[2,2,32]{2,1,0:T(2,128)S(1)}, f32[2,2,32]{2,1,0:T(2,128)S(1)}, u32[]{:S(2)}, u32[]{:S(2)}) collective-permute-start(f32[2,2,32]{2,1,0:T(2,128)S(1)} %pad_maximum_fusion.2), channel_id=1, source_target_pairs={{0,0},{1,1},{2,2},{3,3},{4,5},{5,4},{6,7},{7,6},{8,8},{9,9},{10,10... | collective-permute-start | bytes 1544 | tf_op jit(solution)/shard_map/ppermute | solution.py:28
  97.5 0.7 collective-permute-start.15
  98.4 0.7 collective-permute-start.16
  99.1 12.0 %collective-permute-start.17 = (f32[2]{0:T(128)S(1)}, f32[2]{0:T(128)S(1)}, u32[]{:S(2)}, u32[]{:S(2)}) collective-permute-start(f32[2]{0:T(128)S(1)} %add.37), channel_id=1, source_target_pairs={{0,4},{4,0},{8,12},{12,8},{1,5},{5,1},{9,13},{13,9},{2,6},{6,2},{1... | collective-permute-start | bytes 32 | tf_op jit(solution)/shard_map/ppermute | solution.py:28
  (3 other events, 27.2 us)

commit v3 on v1

--- a/solution.py
+++ b/solution.py
@@ -540,7 +540,7 @@
     own = jnp.transpose(ref_feats[:, 0], (1, 0, 2))
     chips = senders // 2
     across = [
-        [(i, (i - 2 * step) % senders) for i in range(senders)] for step in range(1, chips)
+        [(i, (i - 2 * step) % senders ^ 1) for i in range(senders)] for step in range(1, chips)
     ]
     beside = [(i, i ^ 1) for i in range(senders)]
 
@@ -595,7 +595,7 @@
             for order, at in enumerate(group):
                 for half in range(2):
                     start = PIECE * (2 * order + half)
-                    segments.append((len(sources), start, PIECE, shard + half, at * PIECE))
+                    segments.append((len(sources), start, PIECE, shard + 1 - half, at * PIECE))
             sources.append(here)
         shard += 2
     if not split:
@@ -632,7 +632,7 @@
     base = assembled(position, sources, segments, block)
     if split:
         for half in range(2):
-            segments.append((len(sources), PIECE * half, PIECE, 2 + half, late * PIECE))
+            segments.append((len(sources), PIECE * half, PIECE, 3 - half, late * PIECE))
         done, core, chip = similarities(query, last, position, pair_table, sources)
         sources.append(done)
     else:
@@ -656,16 +656,28 @@
         block,
         limits,
     )
+    mine, other = peaks, shift(peaks, "qry", beside)
+    peaks = jnp.where(odd == 1, jnp.stack([other, mine]), jnp.stack([mine, other]))
+
+    def swap(array, flip_qry, flip_ref):
+        pairs = [
+            (q * blocks + r, (q ^ flip_qry) * blocks + (r ^ flip_ref))
+            for q in range(senders)
+            for r in range(blocks)
+        ]
+        return shift(array, ("qry", "ref"), pairs)
+
     bit = 1
     while bit < blocks:
-        peaks = jnp.maximum(peaks, shift(peaks, "ref", [(i, i ^ bit) for i in range(blocks)]))
+        peaks = jnp.maximum(peaks, swap(peaks, 1, bit))
         bit *= 2
-    row_ids = qry_index * block + jnp.arange(block, dtype=jnp.int32)
-    total = jnp.sum(jnp.where((row_ids < query_len[0])[None], peaks, 0.0), axis=1)
-    bit = senders // 2
-    while bit >= 1:
-        total = total + shift(total, "qry", [(i, i ^ bit) for i in range(senders)])
-        bit //= 2
+    first_row = (qry_index - odd) * block
+    row_ids = first_row + jnp.arange(2 * block, dtype=jnp.int32).reshape(2, 1, block)
+    total = jnp.sum(jnp.where(row_ids < query_len[0], peaks, 0.0), axis=(0, 2))
+    bit = 2
+    while bit < senders:
+        total = total + swap(total, bit + 1, 0)
+        bit *= 2
     return (score_map, total / query_len[0].astype(F32))
 
 

time: 109 us -> 107 us (0.982)
  waiting for transfers between devices: 51.6 us -> 49 us
    ppermute x17, waiting for transfers between devices: 51.6 us -> 49 us  [shift(): return lax.ppermute(array, axis, pairs)]
where the time goes in v3:
time: 107 us
  waiting for transfers between devices  49 us (46%)
  Pallas kernels  35.2 us (33%)
  starting transfers between devices  18.6 us (17%)
  between operations  2.24 us (2%)
    ppermute x17, waiting for transfers between devices, shift(): return lax.ppermute(array, axis, pairs)  49 us
    pallas_call x5, Pallas kernels, similarities(): pl.pallas_call(functools.partial(sims_kernel, scale, spans, len(done), fe...  24.1 us
    ppermute x17, starting transfers between devices, shift(): return lax.ppermute(array, axis, pairs)  18.6 us
    pallas_call x1, Pallas kernels, network(): pl.pallas_call(functools.partial(network_kernel, limits, padding, starts,...  3.98 us
    pallas_call x2, Pallas kernels, cut(): pl.pallas_call(functools.partial(cut_kernel, order), in_specs=[pl.BlockSp...  3.49 us
    pallas_call x1, Pallas kernels, network_weights(): pl.pallas_call(weights_kernel, out_shape=[jax.ShapeDtypeStruct(shape, dty...  3.09 us
  transfers between devices with their start and end apart: 17, of which 8 were waited for; matrix products, arithmetic and copies ran while one was open for 0% of the time, Pallas kernels for 25%

profile of v3, /device:TPU:0, one launch (start us, length us, event | category | flops | bytes accessed | tf_op | source)
XLA Modules:
  0.0 106.5 jit_solution(14745502963472620974)
XLA Ops:
  0.6 1.1 cut.2
  2.3 2.6 %collective-permute-start.1 = (bf16[72,3840]{1,0:T(8,128)(2,1)S(1)}, bf16[72,3840]{1,0:T(8,128)(2,1)S(1)}, u32[]{:S(2)}, u32[]{:S(2)}) collective-permute-start(bf16[72,3840]{1,0:T(8,128)(2,1)S(1)} %bitcast.32), channel_id=1, source_target_pairs={{0,12},{4,8},{8,4},{12,0},{1,13},{5,9},{9,5},{13,1},{2,14},{6,10},... | collective-permute-start | bytes 1658888 | tf_op jit(solution)/shard_map/ppermute | solution.py:28
  4.8 2.4 %cut.3 = (bf16[9,8,3840]{2,1,0:T(8,128)(2,1)}, bf16[9,8,3840]{2,1,0:T(8,128)(2,1)}, bf16[9,8,3840]{2,1,0:T(8,128)(2,1)S(1)}) custom-call(bf16[9,32,3840]{2,1,0:T(8,128)(2,1)} %bitcast.44), custom_call_target="tpu_custom_call" | custom-call | bytes 4423680 | tf_op jit(solution)/shard_map/cut/pallas_call | solution.py:46
  7.4 1.7 %collective-permute-start.5 = (bf16[72,3840]{1,0:T(8,128)(2,1)}, bf16[72,3840]{1,0:T(8,128)(2,1)S(1)}, u32[]{:S(2)}, u32[]{:S(2)}) collective-permute-start(bf16[72,3840]{1,0:T(8,128)(2,1)} %bitcast.19), channel_id=1, source_target_pairs={{0,12},{4,8},{8,4},{12,0},{1,13},{5,9},{9,5},{13,1},{2,14},{6,10},... | collective-permute-start | bytes 1658888 | tf_op jit(solution)/shard_map/ppermute | solution.py:28
  9.2 8.6 %collective-permute-done.1.refs_0_ = bf16[72,3840]{1,0:T(8,128)(2,1)S(1)} collective-permute-done((bf16[72,3840]{1,0:T(8,128)(2,1)S(1)}, bf16[72,3840]{1,0:T(8,128)(2,1)S(1)}, u32[]{:S(2)}, u32[]{:S(2)}) %collective-permute-start.1) | collective-permute-done | bytes 552992 | tf_op jit(solution)/shard_map/ppermute | solution.py:28
  18.4 11.3 %collective-permute-done.3.refs_0_ = bf16[72,3840]{1,0:T(8,128)(2,1)S(1)} collective-permute-done((bf16[72,3840]{1,0:T(8,128)(2,1)}, bf16[72,3840]{1,0:T(8,128)(2,1)S(1)}, u32[]{:S(2)}, u32[]{:S(2)}) %collective-permute-start.3) | collective-permute-done | bytes 552992 | tf_op jit(solution)/shard_map/ppermute | solution.py:28
  30.2 11.4 %collective-permute-done.5.refs_0_ = bf16[72,3840]{1,0:T(8,128)(2,1)S(1)} collective-permute-done((bf16[72,3840]{1,0:T(8,128)(2,1)}, bf16[72,3840]{1,0:T(8,128)(2,1)S(1)}, u32[]{:S(2)}, u32[]{:S(2)}) %collective-permute-start.5) | collective-permute-done | bytes 552992 | tf_op jit(solution)/shard_map/ppermute | solution.py:28
  42.0 11.2 %collective-permute-done.9.refs_0_ = bf16[72,3840]{1,0:T(8,128)(2,1)S(1)} collective-permute-done((bf16[72,3840]{1,0:T(8,128)(2,1)S(1)}, bf16[72,3840]{1,0:T(8,128)(2,1)S(1)}, u32[]{:S(2)}, u32[]{:S(2)}) %collective-permute-start.9) | collective-permute-done | bytes 552992 | tf_op jit(solution)/shard_map/ppermute | solution.py:28
  54.0 11.3 %similarities.5 = (f32[64,128]{1,0:T(8,128)S(1)}, bf16[9,128,3840]{2,1,0:T(8,128)(2,1)S(1)}) custom-call(s32[14]{0:T(128)S(1)} %stack.67.pos_ref, s32[4,4]{1,0:T(4,128)S(1)} %copy-done, bf16[9,128,3840]{2,1,0:T(8,128)(2,1)} %bitcast.48, bf16[288,3840]{1,0:T(8,128)(2,1)} %bitcast.45, bf16[288,3840]{1,0:T(8,128)(2,1)} %collective-permute-done.refs_1_), custom_call_target="tpu_custom_call" | custom-call | flops 5096079360 | bytes 4423680 | tf_op jit(solution)/shard_map/similarities/pallas_call | solution.py:173
  65.3 3.2 %similarities.6.refs_1_.refs_3_ = f32[16,128]{1,0:T(8,128)S(1)} custom-call(s32[14]{0:T(128)S(1)} %stack.67.pos_ref, s32[4,4]{1,0:T(4,128)S(1)} %copy-done, bf16[9,128,3840]{2,1,0:T(8,128)(2,1)S(1)} %get-tuple-element.23.query_ref, bf16[72,3840]{1,0:T(8,128)(2,1)S(1)} %collective-permute-done.1.refs_0_, bf16[72,3840]{1,0:T(8,128)(2,1)S(1)} %collective-permute-done.2.refs_1_), custom_call_target="tpu_custom_call" | custom-call | flops 1274019840 | bytes 1105920 | tf_op jit(solution)/shard_map/similarities/pallas_call | solution.py:173
  68.5 1.3 %collective-permute-start.8 = (f32[8,128]{1,0:T(8,128)S(1)}, f32[8,128]{1,0:T(8,128)S(1)}, u32[]{:S(2)}, u32[]{:S(2)}) collective-permute-start(f32[8,128]{1,0:T(8,128)S(1)} %pad_maximum_fusion.1), channel_id=1, source_target_pairs={{1,0},{2,1},{3,2},{5,4},{6,5},{7,6},{9,8},{10,9},{11,10},{13,12},{... | collective-permute-start | bytes 12296 | tf_op jit(solution)/shard_map/ppermute | solution.py:28
  69.9 3.2 %similarities.7.refs_2_.refs_4_ = f32[16,128]{1,0:T(8,128)S(1)} custom-call(s32[14]{0:T(128)S(1)} %stack.67.pos_ref, s32[4,4]{1,0:T(4,128)S(1)} %copy-done, bf16[9,128,3840]{2,1,0:T(8,128)(2,1)S(1)} %get-tuple-element.23.query_ref, bf16[72,3840]{1,0:T(8,128)(2,1)S(1)} %collective-permute-done.3.refs_0_, bf16[72,3840]{1,0:T(8,128)(2,1)S(1)} %collective-permute-done.4.refs_1_), custom_call_target="tpu_custom_call" | custom-call | flops 1274019840 | bytes 1105920 | tf_op jit(solution)/shard_map/similarities/pallas_call | solution.py:173
  73.2 4.9 %collective-permute-start.7 = (f32[8,128]{1,0:T(8,128)S(1)}, f32[8,128]{1,0:T(8,128)S(1)}, u32[]{:S(2)}, u32[]{:S(2)}) collective-permute-start(f32[8,128]{1,0:T(8,128)S(1)} %pad_maximum_fusion), channel_id=1, source_target_pairs={{0,1},{1,2},{2,3},{4,5},{5,6},{6,7},{8,9},{9,10},{10,11},{12,13},{... | collective-permute-start | bytes 12296 | tf_op jit(solution)/shard_map/ppermute | solution.py:28
  78.1 3.2 %similarities.8.refs_3_.refs_5_ = f32[16,128]{1,0:T(8,128)S(1)} custom-call(s32[14]{0:T(128)S(1)} %stack.67.pos_ref, s32[4,4]{1,0:T(4,128)S(1)} %copy-done, bf16[9,128,3840]{2,1,0:T(8,128)(2,1)S(1)} %get-tuple-element.23.query_ref, bf16[72,3840]{1,0:T(8,128)(2,1)S(1)} %collective-permute-done.5.refs_0_, bf16[72,3840]{1,0:T(8,128)(2,1)S(1)} %collective-permute-done.6.refs_1_), custom_call_target="tpu_custom_call" | custom-call | flops 1274019840 | bytes 1105920 | tf_op jit(solution)/shard_map/similarities/pallas_call | solution.py:173
  81.3 3.2 %similarities.9 = (f32[16,128]{1,0:T(8,128)S(1)}, f32[8,144]{1,0:T(8,128)S(1)}, f32[8,144]{1,0:T(8,128)S(1)}) custom-call(s32[14]{0:T(128)S(1)} %stack.67.pos_ref, s32[4,4]{1,0:T(4,128)S(1)} %copy-done, bf16[9,128,3840]{2,1,0:T(8,128)(2,1)S(1)} %get-tuple-element.23.query_ref, bf16[72,3840]{1,0:T(8,128)(2,1)S(1)} %collective-permute-done.9.refs_0_, ...), custom_call_target="tpu_custom_call" | custom-call | flops 1274019840 | bytes 1105920 | tf_op jit(solution)/shard_map/similarities/pallas_call | solution.py:173
  84.6 1.8 %collective-permute-start.12 = (f32[8,144]{1,0:T(8,128)S(1)}, f32[8,144]{1,0:T(8,128)S(1)}, u32[]{:S(2)}, u32[]{:S(2)}) collective-permute-start(f32[8,144]{1,0:T(8,128)S(1)} %get-tuple-element.30), channel_id=1, source_target_pairs={{4,8},{12,0},{8,4},{0,12},{5,9},{13,1},{9,5},{1,13},{6,10},{14,2},... | collective-permute-start | bytes 13832 | tf_op jit(solution)/shard_map/ppermute | solution.py:28
  86.4 3.1 %weights.1 = (bf16[256,1536]{1,0:T(8,128)(2,1)S(1)}, f32[1,128]{1,0:T(1,128)S(1)}, bf16[512,256]{1,0:T(8,128)(2,1)S(1)}, f32[1,128]{1,0:T(1,128)S(1)}, bf16[768,...) custom-call(f32[3,3,32]{2,1,0:T(4,128)S(1)} %copy-done.3, f32[1,32]{1,0:T(1,128)S(1)} %bitcast.38, ...), custom_call_target="tpu_custom_call" | custom-call | flops 100000000 | bytes 4000000 | tf_op jit(solution)/shard_map/weights/pallas_call | solution.py:490
  90.7 4.0 %network.1 = (f32[32,32]{1,0:T(8,128)}, f32[2,32]{1,0:T(2,128)S(1)}, f32[4,56,256]{2,1,0:T(8,128)S(1)}) custom-call(s32[14]{0:T(128)S(1)} %stack.67.pos_ref, s32[2]{0:T(128)S(1)} %copy-done.8, f32[4,56,256]{2,1,0:T(8,128)S(1)} %assemble.1.base_ref, f32[16,128]{1,0:T(8,128)S(1)} %get-tuple-element.28.refs_0_, ...), custom_call_target="tpu_custom_call", output_to_operand_aliasing={{2}: (2, {})} | custom-call | flops 6000000000 | bytes 4000000 | tf_op jit(solution)/shard_map/network/pallas_call | solution.py:403
  94.8 1.1 %collective-permute-done.13 = f32[2,32]{1,0:T(2,128)S(1)} collective-permute-done((f32[2,32]{1,0:T(2,128)S(1)}, f32[2,32]{1,0:T(2,128)S(1)}, u32[]{:S(2)}, u32[]{:S(2)}) %collective-permute-start.13) | collective-permute-done | bytes 288 | tf_op jit(solution)/shard_map/ppermute | solution.py:28
  95.9 1.4 %collective-permute-start.14 = (f32[2,2,32]{2,1,0:T(2,128)S(1)}, f32[2,2,32]{2,1,0:T(2,128)S(1)}, u32[]{:S(2)}, u32[]{:S(2)}) collective-permute-start(f32[2,2,32]{2,1,0:T(2,128)S(1)} %maximum_select_fusion), channel_id=1, source_target_pairs={{0,5},{1,4},{2,7},{3,6},{4,1},{5,0},{6,3},{7,2},{8,13},{9,12},{10,... | collective-permute-start | bytes 1544 | tf_op jit(solution)/shard_map/ppermute | solution.py:28
  97.9 1.0 collective-permute-done.14
  98.9 2.4 %collective-permute-start.15 = (f32[2,2,32]{2,1,0:T(2,128)S(1)}, f32[2,2,32]{2,1,0:T(2,128)S(1)}, u32[]{:S(2)}, u32[]{:S(2)}) collective-permute-start(f32[2,2,32]{2,1,0:T(2,128)S(1)} %fusion.3), channel_id=1, source_target_pairs={{0,6},{1,7},{2,4},{3,5},{4,2},{5,3},{6,0},{7,1},{8,14},{9,15},{10,... | collective-permute-start | bytes 1544 | tf_op jit(solution)/shard_map/ppermute | solution.py:28
  101.3 1.5 %collective-permute-done.15 = f32[2,2,32]{2,1,0:T(2,128)S(1)} collective-permute-done((f32[2,2,32]{2,1,0:T(2,128)S(1)}, f32[2,2,32]{2,1,0:T(2,128)S(1)}, u32[]{:S(2)}, u32[]{:S(2)}) %collective-permute-start.15) | collective-permute-done | bytes 544 | tf_op jit(solution)/shard_map/ppermute | solution.py:28
  103.2 2.8 %collective-permute-done.16 = f32[2]{0:T(128)S(1)} collective-permute-done((f32[2]{0:T(128)S(1)}, f32[2]{0:T(128)S(1)}, u32[]{:S(2)}, u32[]{:S(2)}) %collective-permute-start.16) | collective-permute-done | bytes 40 | tf_op jit(solution)/shard_map/ppermute | solution.py:28
  (49 shorter events, 4.7 us)
Async XLA Ops:
  1.7 51.6 %collective-permute-start = (bf16[288,3840]{1,0:T(8,128)(2,1)}, bf16[288,3840]{1,0:T(8,128)(2,1)}, u32[]{:S(2)}, u32[]{:S(2)}) collective-permute-start(bf16[288,3840]{1,0:T(8,128)(2,1)} %bitcast.43), channel_id=1, source_target_pairs={{0,4},{4,0},{8,12},{12,8},{1,5},{5,1},{9,13},{13,9},{2,6},{6,2},{1... | collective-permute-start | bytes 6635528 | tf_op jit(solution)/shard_map/ppermute | solution.py:28
  2.3 15.5 %collective-permute-start.1 = (bf16[72,3840]{1,0:T(8,128)(2,1)S(1)}, bf16[72,3840]{1,0:T(8,128)(2,1)S(1)}, u32[]{:S(2)}, u32[]{:S(2)}) collective-permute-start(bf16[72,3840]{1,0:T(8,128)(2,1)S(1)} %bitcast.32), channel_id=1, source_target_pairs={{0,12},{4,8},{8,4},{12,0},{1,13},{5,9},{9,5},{13,1},{2,14},{6,10},... | collective-permute-start | bytes 1658888 | tf_op jit(solution)/shard_map/ppermute | solution.py:28
  7.3 22.4 %collective-permute-start.3 = (bf16[72,3840]{1,0:T(8,128)(2,1)}, bf16[72,3840]{1,0:T(8,128)(2,1)S(1)}, u32[]{:S(2)}, u32[]{:S(2)}) collective-permute-start(bf16[72,3840]{1,0:T(8,128)(2,1)} %bitcast.18), channel_id=1, source_target_pairs={{0,12},{4,8},{8,4},{12,0},{1,13},{5,9},{9,5},{13,1},{2,14},{6,10},... | collective-permute-start | bytes 1658888 | tf_op jit(solution)/shard_map/ppermute | solution.py:28
  7.4 34.2 %collective-permute-start.5 = (bf16[72,3840]{1,0:T(8,128)(2,1)}, bf16[72,3840]{1,0:T(8,128)(2,1)S(1)}, u32[]{:S(2)}, u32[]{:S(2)}) collective-permute-start(bf16[72,3840]{1,0:T(8,128)(2,1)} %bitcast.19), channel_id=1, source_target_pairs={{0,12},{4,8},{8,4},{12,0},{1,13},{5,9},{9,5},{13,1},{2,14},{6,10},... | collective-permute-start | bytes 1658888 | tf_op jit(solution)/shard_map/ppermute | solution.py:28
  9.1 44.1 %collective-permute-start.9 = (bf16[72,3840]{1,0:T(8,128)(2,1)S(1)}, bf16[72,3840]{1,0:T(8,128)(2,1)S(1)}, u32[]{:S(2)}, u32[]{:S(2)}) collective-permute-start(bf16[72,3840]{1,0:T(8,128)(2,1)S(1)} %bitcast.35), channel_id=1, source_target_pairs={{0,12},{4,8},{8,4},{12,0},{1,13},{5,9},{9,5},{13,1},{2,14},{6,10},... | collective-permute-start | bytes 1658888 | tf_op jit(solution)/shard_map/ppermute | solution.py:28
  17.8 47.5 %collective-permute-start.2 = (bf16[72,3840]{1,0:T(8,128)(2,1)S(1)}, bf16[72,3840]{1,0:T(8,128)(2,1)S(1)}, u32[]{:S(2)}, u32[]{:S(2)}) collective-permute-start(bf16[72,3840]{1,0:T(8,128)(2,1)S(1)} %collective-permute-done.1.refs_0_), channel_id=1, source_target_pairs={{0,4},{4,0},{8,12},{12,8},{1,5},{5,1},{9,13},{13,9},{2,6},{6,2},{1... | collective-permute-start | bytes 1658888 | tf_op jit(solution)/shard_map/ppermute | solution.py:28
  29.7 40.1 %collective-permute-start.4 = (bf16[72,3840]{1,0:T(8,128)(2,1)S(1)}, bf16[72,3840]{1,0:T(8,128)(2,1)S(1)}, u32[]{:S(2)}, u32[]{:S(2)}) collective-permute-start(bf16[72,3840]{1,0:T(8,128)(2,1)S(1)} %collective-permute-done.3.refs_0_), channel_id=1, source_target_pairs={{0,4},{4,0},{8,12},{12,8},{1,5},{5,1},{9,13},{13,9},{2,6},{6,2},{1... | collective-permute-start | bytes 1658888 | tf_op jit(solution)/shard_map/ppermute | solution.py:28
  41.6 36.5 %collective-permute-start.6 = (bf16[72,3840]{1,0:T(8,128)(2,1)S(1)}, bf16[72,3840]{1,0:T(8,128)(2,1)S(1)}, u32[]{:S(2)}, u32[]{:S(2)}) collective-permute-start(bf16[72,3840]{1,0:T(8,128)(2,1)S(1)} %collective-permute-done.5.refs_0_), channel_id=1, source_target_pairs={{0,4},{4,0},{8,12},{12,8},{1,5},{5,1},{9,13},{13,9},{2,6},{6,2},{1... | collective-permute-start | bytes 1658888 | tf_op jit(solution)/shard_map/ppermute | solution.py:28
  53.2 28.0 %collective-permute-start.10 = (bf16[72,3840]{1,0:T(8,128)(2,1)S(1)}, bf16[72,3840]{1,0:T(8,128)(2,1)S(1)}, u32[]{:S(2)}, u32[]{:S(2)}) collective-permute-start(bf16[72,3840]{1,0:T(8,128)(2,1)S(1)} %collective-permute-done.9.refs_0_), channel_id=1, source_target_pairs={{0,4},{4,0},{8,12},{12,8},{1,5},{5,1},{9,13},{13,9},{2,6},{6,2},{1... | collective-permute-start | bytes 1658888 | tf_op jit(solution)/shard_map/ppermute | solution.py:28
  68.5 12.7 %collective-permute-start.8 = (f32[8,128]{1,0:T(8,128)S(1)}, f32[8,128]{1,0:T(8,128)S(1)}, u32[]{:S(2)}, u32[]{:S(2)}) collective-permute-start(f32[8,128]{1,0:T(8,128)S(1)} %pad_maximum_fusion.1), channel_id=1, source_target_pairs={{1,0},{2,1},{3,2},{5,4},{6,5},{7,6},{9,8},{10,9},{11,10},{13,12},{... | collective-permute-start | bytes 12296 | tf_op jit(solution)/shard_map/ppermute | solution.py:28
  73.1 13.3 %copy-start.1 = (bf16[3,3,128,64]{2,3,1,0:T(8,128)(2,1)S(1)}, bf16[3,3,128,64]{2,3,1,0:T(8,128)(2,1)}, u32[]{:S(2)}) copy-start(bf16[3,3,128,64]{2,3,1,0:T(8,128)(2,1)} %param.22) | copy-start | bytes 442372
  73.1 13.3 %copy-start.2 = (bf16[3,3,64,32]{2,3,1,0:T(8,128)(2,1)S(1)}, bf16[3,3,64,32]{2,3,1,0:T(8,128)(2,1)}, u32[]{:S(2)}) copy-start(bf16[3,3,64,32]{2,3,1,0:T(8,128)(2,1)} %param.20) | copy-start | bytes 110596
  73.1 13.3 %copy-start.3 = (f32[3,3,32]{2,1,0:T(4,128)S(1)}, f32[3,3,32]{2,1,0:T(4,128)}, u32[]{:S(2)}) copy-start(f32[3,3,32]{2,1,0:T(4,128)} %w1_ref.1) | copy-start | bytes 3460
  73.1 13.2 %copy-start.4 = (f32[32]{0:T(128)S(1)}, f32[32]{0:T(128)}, u32[]{:S(2)}) copy-start(f32[32]{0:T(128)} %param.19) | copy-start | bytes 388
  73.1 13.2 %copy-start.5 = (f32[64]{0:T(128)S(1)}, f32[64]{0:T(128)}, u32[]{:S(2)}) copy-start(f32[64]{0:T(128)} %param.21) | copy-start | bytes 772
  73.1 13.2 %copy-start.6 = (f32[128]{0:T(128)S(1)}, f32[128]{0:T(128)}, u32[]{:S(2)}) copy-start(f32[128]{0:T(128)} %param.23) | copy-start | bytes 1540
  73.2 17.6 %copy-start.8 = (s32[2]{0:T(128)S(1)}, s32[2]{0:T(128)}, u32[]{:S(2)}) copy-start(s32[2]{0:T(128)} %len_ref.1) | copy-start | bytes 28
  73.2 8.1 %collective-permute-start.7 = (f32[8,128]{1,0:T(8,128)S(1)}, f32[8,128]{1,0:T(8,128)S(1)}, u32[]{:S(2)}, u32[]{:S(2)}) collective-permute-start(f32[8,128]{1,0:T(8,128)S(1)} %pad_maximum_fusion), channel_id=1, source_target_pairs={{0,1},{1,2},{2,3},{4,5},{5,6},{6,7},{8,9},{9,10},{10,11},{12,13},{... | collective-permute-start | bytes 12296 | tf_op jit(solution)/shard_map/ppermute | solution.py:28
  84.5 6.2 %collective-permute-start.11 = (f32[8,144]{1,0:T(8,128)S(1)}, f32[8,144]{1,0:T(8,128)S(1)}, u32[]{:S(2)}, u32[]{:S(2)}) collective-permute-start(f32[8,144]{1,0:T(8,128)S(1)} %get-tuple-element.29), channel_id=1, source_target_pairs={{0,4},{4,0},{8,12},{12,8},{1,5},{5,1},{9,13},{13,9},{2,6},{6,2},{1... | collective-permute-start | bytes 13832 | tf_op jit(solution)/shard_map/ppermute | solution.py:28
  84.6 6.2 %collective-permute-start.12 = (f32[8,144]{1,0:T(8,128)S(1)}, f32[8,144]{1,0:T(8,128)S(1)}, u32[]{:S(2)}, u32[]{:S(2)}) collective-permute-start(f32[8,144]{1,0:T(8,128)S(1)} %get-tuple-element.30), channel_id=1, source_target_pairs={{4,8},{12,0},{8,4},{0,12},{5,9},{13,1},{9,5},{1,13},{6,10},{14,2},... | collective-permute-start | bytes 13832 | tf_op jit(solution)/shard_map/ppermute | solution.py:28
  94.7 1.2 %collective-permute-start.13 = (f32[2,32]{1,0:T(2,128)S(1)}, f32[2,32]{1,0:T(2,128)S(1)}, u32[]{:S(2)}, u32[]{:S(2)}) collective-permute-start(f32[2,32]{1,0:T(2,128)S(1)} %get-tuple-element.39), channel_id=1, source_target_pairs={{0,4},{4,0},{8,12},{12,8},{1,5},{5,1},{9,13},{13,9},{2,6},{6,2},{1... | collective-permute-start | bytes 776 | tf_op jit(solution)/shard_map/ppermute | solution.py:28
  95.9 3.0 %collective-permute-start.14 = (f32[2,2,32]{2,1,0:T(2,128)S(1)}, f32[2,2,32]{2,1,0:T(2,128)S(1)}, u32[]{:S(2)}, u32[]{:S(2)}) collective-permute-start(f32[2,2,32]{2,1,0:T(2,128)S(1)} %maximum_select_fusion), channel_id=1, source_target_pairs={{0,5},{1,4},{2,7},{3,6},{4,1},{5,0},{6,3},{7,2},{8,13},{9,12},{10,... | collective-permute-start | bytes 1544 | tf_op jit(solution)/shard_map/ppermute | solution.py:28
  98.9 3.9 %collective-permute-start.15 = (f32[2,2,32]{2,1,0:T(2,128)S(1)}, f32[2,2,32]{2,1,0:T(2,128)S(1)}, u32[]{:S(2)}, u32[]{:S(2)}) collective-permute-start(f32[2,2,32]{2,1,0:T(2,128)S(1)} %fusion.3), channel_id=1, source_target_pairs={{0,6},{1,7},{2,4},{3,5},{4,2},{5,3},{6,0},{7,1},{8,14},{9,15},{10,... | collective-permute-start | bytes 1544 | tf_op jit(solution)/shard_map/ppermute | solution.py:28
  102.9 3.1 %collective-permute-start.16 = (f32[2]{0:T(128)S(1)}, f32[2]{0:T(128)S(1)}, u32[]{:S(2)}, u32[]{:S(2)}) collective-permute-start(f32[2]{0:T(128)S(1)} %select_reduce_fusion), channel_id=1, source_target_pairs={{0,12},{1,13},{2,14},{3,15},{4,8},{5,9},{6,10},{7,11},{8,4},{9,5},... | collective-permute-start | bytes 32 | tf_op jit(solution)/shard_map/ppermute | solution.py:28
  (2 other events, 13.9 us)

commit v4 on v3

--- a/solution.py
+++ b/solution.py
@@ -193,53 +193,47 @@
     )(position, table, *(map(in_hbm, (query, *pieces)) if fetch else (query, *pieces)), *done)
 
 
-def convolve(sims_ref, weights, scratch, score_ref, pos_ref, block, limits, padding):
-    w1_ref, b1_ref, w2_ref, b2_ref, w3_ref, b3_ref, w4_ref, b4_ref = weights
-    y_ref, first_ref, lhs2_ref, second_ref, lhs3_ref = scratch
-    map_rows, map_cols = limits
-    jf, js, jt = padding
-    rows1 = block + 2 * HALO
-    groups = rows1 // GROUP
-    row0 = pos_ref[0] * block
-    col0 = pos_ref[1] * block
+def inside_columns(pos_ref, block, limits, count, halo):
+    at = lax.broadcasted_iota(jnp.int32, (count, 128), 0) + (pos_ref[1] * block - halo)
+    return jnp.where((at >= 0) & (at < limits[1]), 1.0, 0.0).astype(F32)
+
+
+def inside_rows(pos_ref, block, limits, at):
+    at = pos_ref[0] * block + at
+    return jnp.where((at >= 0) & (at < limits[0]), 1.0, 0.0).astype(F32)
+
+
+def first_map(sims_ref, w1_ref, b1_ref, y_ref, first_ref, pos_ref, block, limits, tiles):
     lanes = sims_ref.shape[2]
-
     sources = [(PHASES - 1, 0)] + [(phase, 1) for phase in range(PHASES)] + [(0, 2)]
-    bases = [sims_ref[phase, at : at + jf, :] for phase, at in sources]
     terms = len(sources) * WINDOW
-    zero = jnp.zeros((jf, 128 - terms), F32)
     reach = PHASES * HALO + 1
-    lane = lax.broadcasted_iota(jnp.int32, (jf, 128), 1)
-    for group in range(groups):
+    spots, start = [], 0
+    for group, first, size in tiles:
         low = PHASES * GROUP * group - reach
         parts = []
-        for base in bases:
+        for phase, at in sources:
+            base = sims_ref[phase, first + at : first + at + size, :]
             if low < 0:
                 parts.append(base[:, lanes + low : lanes])
                 parts.append(base[:, 0 : low + WINDOW])
             else:
                 parts.append(base[:, low : low + WINDOW])
-        window = jnp.concatenate(parts + [zero], axis=1)
+        window = jnp.concatenate(parts + [jnp.zeros((size, 128 - terms), F32)], axis=1)
         high = window.astype(BF).astype(F32)
         rest = pltpu.roll(window - high, terms, 1)
         again = pltpu.roll(high, 2 * terms - 128, 1)
-        row = slice(group * jf, (group + 1) * jf)
+        lane = lax.broadcasted_iota(jnp.int32, (size, 128), 1)
+        row = slice(start, start + size)
         y_ref[row, 0:128] = jnp.where(lane < terms, high, rest).astype(BF)
         y_ref[row, 128:256] = jnp.where(lane < 2 * terms - 128, rest, again).astype(BF)
-
-    cell = lax.broadcasted_iota(jnp.int32, (jf, 128), 0)
-
-    def inside(halo, count):
-        at = cell[0:count] + (col0 - halo)
-        return jnp.where((at >= 0) & (at < map_cols), 1.0, 0.0).astype(F32)
-
-    def row_flag(at):
-        return jnp.where((at >= 0) & (at < map_rows), 1.0, 0.0).astype(F32)
-
-    keep_cols = inside(HALO, jf)
+        spots.append(start)
+        start += size
+
+    keep_cols = inside_columns(pos_ref, block, limits, first_ref.shape[1], HALO)
     for member in range(GROUP):
         result = jnp.dot(
-            y_ref[0 : groups * jf, :],
+            y_ref[0:start, :],
             w1_ref[:, member * 512 : (member + 1) * 512],
             preferred_element_type=F32,
         )
@@ -248,12 +242,37 @@
             jnp.maximum(result[:, 256:384], result[:, 384:512]),
         )
         pooled = jnp.maximum(pooled + b1_ref[...], 0.0)
-        for group in range(groups):
+        for (group, first, size), spot in zip(tiles, spots):
             at = group * GROUP + member
-            keep = keep_cols * row_flag(row0 + at - HALO)
-            first_ref[at, 0:jf, :] = (
-                (pooled[group * jf : (group + 1) * jf] * keep).astype(BF).astype(F32)
+            keep = keep_cols[first : first + size] * inside_rows(
+                pos_ref, block, limits, at - HALO
             )
+            first_ref[at, first : first + size, :] = (
+                (pooled[spot : spot + size] * keep).astype(BF).astype(F32)
+            )
+
+
+def first_tiles(block, frames, jf, late):
+    groups = (block + 2 * HALO) // GROUP
+    reach = PHASES * HALO + 1
+    early, rest, whole = [], [], []
+    for group in range(groups):
+        low = PHASES * GROUP * group - reach
+        if low >= 0 and low + WINDOW <= frames:
+            early += [(group, 0, late)]
+            rest += [(group, late, 2 * PIECE)]
+        else:
+            whole += [(group, 0, jf)]
+    ends = [(group, late + 2 * PIECE, jf - late - 2 * PIECE) for group, _, _ in early]
+    return early + ends, rest + whole
+
+
+def convolve(sims_ref, first_ref, weights, scratch, score_ref, pos_ref, block, limits, padding, tiles):
+    w1_ref, b1_ref, w2_ref, b2_ref, w3_ref, b3_ref, w4_ref, b4_ref = weights
+    y_ref, lhs2_ref, second_ref, lhs3_ref = scratch
+    jf, js, jt = padding
+    first_map(sims_ref, w1_ref, b1_ref, y_ref, first_ref, pos_ref, block, limits, tiles)
+    lane = lax.broadcasted_iota(jnp.int32, (jf, 128), 1)
 
     upper = lane < 64
     left = (lane // 32) % 2 == 0
@@ -271,9 +290,9 @@
     pooled = jnp.maximum(result[:, 0:128], result[:, 128:256])
     pooled = jnp.maximum(pooled, pltpu.roll(pooled, 64, 1))
     pooled = jnp.maximum(pooled + b2_ref[...], 0.0)
-    keep_cols = inside(1, js)
+    keep_cols = inside_columns(pos_ref, block, limits, js, 1)
     for at in range(rows2):
-        keep = keep_cols * row_flag(row0 + at - 1)
+        keep = keep_cols * inside_rows(pos_ref, block, limits, at - 1)
         second_ref[at, 0:js, :] = (pooled[at * js : (at + 1) * js] * keep).astype(BF).astype(F32)
         if js < jt + 8:
             second_ref[at, js : jt + 8, :] = jnp.zeros((jt + 8 - js, 128), F32)
@@ -305,12 +324,10 @@
     return (max(-(-(cells + 4) // 8) * 8, js), js, -(-cells // 16) * 16)
 
 
-def convolve_scratch(block, padding):
-    jf, js, jt = padding
-    rows1 = block + 2 * HALO
+def convolve_scratch(block, padding, tiles):
+    _, js, jt = padding
     return [
-        pltpu.VMEM((rows1 // GROUP * jf, 256), BF),
-        pltpu.VMEM((rows1, jf, 128), F32),
+        pltpu.VMEM((sum(size for _, _, size in tiles), 256), BF),
         pltpu.VMEM(((block + 2) * js, 512), BF),
         pltpu.VMEM((block + 2, max(js, jt + 8), 128), F32),
         pltpu.VMEM((block // 2 * jt, 768), BF),
@@ -337,30 +354,37 @@
             ]
 
 
-def assemble_kernel(segments, pos_ref, *refs):
-    sources, sims_ref = refs[:-1], refs[-1]
+def assemble_kernel(segments, tiles, block, limits, pos_ref, *refs):
+    sources, (w1_ref, b1_ref, sims_ref, first_ref, y_ref) = refs[:-5], refs[-5:]
     sims_ref[...] = jnp.zeros_like(sims_ref)
     place(pos_ref, sims_ref, sources, segments)
-
-
-def assembled(position, sources, segments, block):
+    first_map(sims_ref, w1_ref, b1_ref, y_ref, first_ref, pos_ref, block, limits, tiles)
+
+
+def assembled(position, sources, segments, weights, tiles, block, limits):
     smem = pl.BlockSpec(memory_space=pltpu.SMEM)
     vmem = pl.BlockSpec(memory_space=pltpu.VMEM)
     frames = sources[0].shape[1]
     return pl.pallas_call(
-        functools.partial(assemble_kernel, segments),
-        in_specs=[smem] + [vmem for _ in sources],
-        out_specs=vmem,
-        out_shape=jax.ShapeDtypeStruct((PHASES, block + 24, 2 * frames), F32),
+        functools.partial(assemble_kernel, segments, tiles, block, limits),
+        in_specs=[smem] + [vmem for _ in sources] + [vmem, vmem],
+        out_specs=[vmem, vmem],
+        out_shape=[
+            jax.ShapeDtypeStruct((PHASES, block + 24, 2 * frames), F32),
+            jax.ShapeDtypeStruct((block + 2 * HALO, pad_cells(block)[0], 128), F32),
+        ],
+        scratch_shapes=[pltpu.VMEM((sum(size for _, _, size in tiles), 256), BF)],
         compiler_params=pltpu.CompilerParams(vmem_limit_bytes=GRANT),
-        cost_estimate=pl.CostEstimate(flops=0, bytes_accessed=500_000, transcendentals=0),
+        cost_estimate=pl.CostEstimate(
+            flops=1_000_000_000, bytes_accessed=500_000, transcendentals=0
+        ),
         name="assemble",
-    )(position, *sources)
-
-
-def network_kernel(limits, padding, starts, segments, pos_ref, len_ref, base_ref, *refs):
-    (late_ref, core_ref, chip_ref), refs = refs[:3], refs[3:]
-    weights, (score_ref, peak_ref, sims_ref), scratch = refs[:8], refs[8:11], refs[11:]
+    )(position, *sources, *weights)
+
+
+def network_kernel(limits, padding, starts, segments, tiles, pos_ref, len_ref, *refs):
+    (_, _, late_ref, core_ref, chip_ref), refs = refs[:5], refs[5:]
+    weights, (score_ref, peak_ref, sims_ref, first_ref), scratch = refs[:8], refs[8:12], refs[12:]
     block = score_ref.shape[0]
     last = len(starts) - 1
     place(
@@ -378,7 +402,9 @@
 
     pl.when(pos_ref[0] % 2 == 0)(lambda: edges(below, above))
     pl.when(pos_ref[0] % 2 == 1)(lambda: edges(above, below))
-    convolve(sims_ref, weights, scratch, score_ref, pos_ref, block, limits, padding)
+    convolve(
+        sims_ref, first_ref, weights, scratch, score_ref, pos_ref, block, limits, padding, tiles
+    )
 
     score = score_ref[...]
     videos = len_ref.shape[0]
@@ -395,22 +421,25 @@
     peak_ref[...] = jnp.transpose(peaks)[0:videos]
 
 
-def network(position, lengths, base, late, edges, starts, segments, weights, block, limits):
+def network(
+    position, lengths, base, first, late, edges, starts, segments, tiles, weights, block, limits
+):
     smem = pl.BlockSpec(memory_space=pltpu.SMEM)
     vmem = pl.BlockSpec(memory_space=pltpu.VMEM)
     padding = pad_cells(block)
-    arrays = [base, late, *edges]
-    score, peaks, _ = pl.pallas_call(
-        functools.partial(network_kernel, limits, padding, starts, segments),
+    arrays = [base, first, late, *edges]
+    score, peaks, *_ = pl.pallas_call(
+        functools.partial(network_kernel, limits, padding, starts, segments, tiles),
         in_specs=[smem, smem] + [vmem] * len(arrays) + [vmem] * 7 + [smem],
-        out_specs=[vmem, vmem, vmem],
+        out_specs=[vmem] * 4,
         out_shape=[
             jax.ShapeDtypeStruct((block, block), F32),
             jax.ShapeDtypeStruct((lengths.shape[0], block), F32),
             jax.ShapeDtypeStruct(base.shape, F32),
+            jax.ShapeDtypeStruct(first.shape, F32),
         ],
-        scratch_shapes=convolve_scratch(block, padding),
-        input_output_aliases={2: 2},
+        scratch_shapes=convolve_scratch(block, padding, tiles),
+        input_output_aliases={2: 2, 3: 3},
         cost_estimate=pl.CostEstimate(
             flops=6_000_000_000, bytes_accessed=4_000_000, transcendentals=0
         ),
@@ -540,7 +569,7 @@
     own = jnp.transpose(ref_feats[:, 0], (1, 0, 2))
     chips = senders // 2
     across = [
-        [(i, (i - 2 * step) % senders ^ 1) for i in range(senders)] for step in range(1, chips)
+        [(i, (i - 2 * step) % senders) for i in range(senders)] for step in range(1, chips)
     ]
     beside = [(i, i ^ 1) for i in range(senders)]
 
@@ -595,7 +624,7 @@
             for order, at in enumerate(group):
                 for half in range(2):
                     start = PIECE * (2 * order + half)
-                    segments.append((len(sources), start, PIECE, shard + 1 - half, at * PIECE))
+                    segments.append((len(sources), start, PIECE, shard + half, at * PIECE))
             sources.append(here)
         shard += 2
     if not split:
@@ -629,10 +658,14 @@
     for edge, cell in ((left, -HALO), (right, block)):
         segments += [(len(sources), HALO * k, HALO, k, cell) for k in range(PHASES)]
         sources.append(edge)
-    base = assembled(position, sources, segments, block)
+    jf = pad_cells(block)[0]
+    ready, tiles = first_tiles(block, frames, jf, late * PIECE if split else 2 * PIECE)
+    base, first = assembled(position, sources, segments, weights[:2], ready, block, limits)
+    if not split:
+        tiles = first_tiles(block, 0, jf, 2 * PIECE)[1]
     if split:
         for half in range(2):
-            segments.append((len(sources), PIECE * half, PIECE, 3 - half, late * PIECE))
+            segments.append((len(sources), PIECE * half, PIECE, 2 + half, late * PIECE))
         done, core, chip = similarities(query, last, position, pair_table, sources)
         sources.append(done)
     else:
@@ -648,10 +681,12 @@
         position,
         lengths,
         base,
+        first,
         done,
         (core, chip),
         starts,
         segments,
+        tiles,
         weights,
         block,
         limits,

time: 107 us -> 104 us (0.972)
  waiting for transfers between devices: 49 us -> 39.6 us
  local copies, waits for them, and re-layouts: 0.83 us -> 5.89 us
    ppermute x17, waiting for transfers between devices: 49 us -> 39.6 us  [shift(): return lax.ppermute(array, axis, pairs)]
    unnamed x18, local copies, waits for them, and re-layouts: 0.73 us -> 5.79 us
  transfers between devices with their start and end apart: 17 -> 17, of which waited for: 8 -> 9; matrix products, arithmetic and copies ran while one was open for 0% -> 0% of each run, Pallas kernels for 25% -> 27%
where the time goes in v4:
time: 104 us; the launch traced here: 103 us
  waiting for transfers between devices  39.6 us (38%)
  Pallas kernels  35.4 us (34%)
  starting transfers between devices  19.6 us (19%)
  local copies, waits for them, and re-layouts  5.89 us (6%)
  between operations  2.14 us (2%)
    ppermute x17, waiting for transfers between devices, shift(): return lax.ppermute(array, axis, pairs)  39.6 us
    pallas_call x5, Pallas kernels, similarities(): pl.pallas_call(functools.partial(sims_kernel, scale, spans, len(done), fe...  24.1 us
    ppermute x17, starting transfers between devices, shift(): return lax.ppermute(array, axis, pairs)  19.6 us
    unnamed x18, local copies, waits for them, and re-layouts  5.79 us
    pallas_call x1, Pallas kernels, network(): pl.pallas_call(functools.partial(network_kernel, limits, padding, starts,...  3.54 us
    pallas_call x2, Pallas kernels, cut(): pl.pallas_call(functools.partial(cut_kernel, order), in_specs=[pl.BlockSp...  3.49 us
    pallas_call x1, Pallas kernels, network_weights(): pl.pallas_call(weights_kernel, out_shape=[jax.ShapeDtypeStruct(shape, dty...  3.09 us
  transfers between devices with their start and end apart: 17, of which 9 were waited for; matrix products, arithmetic and copies ran while one was open for 0% of the time, Pallas kernels for 27%

profile of v4, /device:TPU:0, one launch (start us, length us, event | category | flops | bytes accessed | tf_op | source)
XLA Modules:
  0.0 103.3 jit_solution(10731193682942916888)
XLA Ops:
  0.6 1.1 %cut.2 = bf16[9,8,3840]{2,1,0:T(8,128)(2,1)S(1)} custom-call(bf16[9,32,3840]{2,1,0:T(8,128)(2,1)} %bitcast.42), custom_call_target="tpu_custom_call" | custom-call | bytes 4423680 | tf_op jit(solution)/shard_map/cut/pallas_call | solution.py:46
  2.3 2.6 %collective-permute-start.1 = (bf16[72,3840]{1,0:T(8,128)(2,1)S(1)}, bf16[72,3840]{1,0:T(8,128)(2,1)S(1)}, u32[]{:S(2)}, u32[]{:S(2)}) collective-permute-start(bf16[72,3840]{1,0:T(8,128)(2,1)S(1)} %bitcast.32), channel_id=1, source_target_pairs={{0,8},{4,12},{8,0},{12,4},{1,9},{5,13},{9,1},{13,5},{2,10},{6,14},... | collective-permute-start | bytes 1658888 | tf_op jit(solution)/shard_map/ppermute | solution.py:28
  4.8 2.4 %cut.3 = (bf16[9,8,3840]{2,1,0:T(8,128)(2,1)}, bf16[9,8,3840]{2,1,0:T(8,128)(2,1)}, bf16[9,8,3840]{2,1,0:T(8,128)(2,1)S(1)}) custom-call(bf16[9,32,3840]{2,1,0:T(8,128)(2,1)} %bitcast.44), custom_call_target="tpu_custom_call" | custom-call | bytes 4423680 | tf_op jit(solution)/shard_map/cut/pallas_call | solution.py:46
  7.3 2.0 %collective-permute-start.5 = (bf16[72,3840]{1,0:T(8,128)(2,1)}, bf16[72,3840]{1,0:T(8,128)(2,1)S(1)}, u32[]{:S(2)}, u32[]{:S(2)}) collective-permute-start(bf16[72,3840]{1,0:T(8,128)(2,1)} %bitcast.19), channel_id=1, source_target_pairs={{0,8},{4,12},{8,0},{12,4},{1,9},{5,13},{9,1},{13,5},{2,10},{6,14},... | collective-permute-start | bytes 1658888 | tf_op jit(solution)/shard_map/ppermute | solution.py:28
  9.4 8.8 %collective-permute-done.1.refs_0_ = bf16[72,3840]{1,0:T(8,128)(2,1)S(1)} collective-permute-done((bf16[72,3840]{1,0:T(8,128)(2,1)S(1)}, bf16[72,3840]{1,0:T(8,128)(2,1)S(1)}, u32[]{:S(2)}, u32[]{:S(2)}) %collective-permute-start.1) | collective-permute-done | bytes 552992 | tf_op jit(solution)/shard_map/ppermute | solution.py:28
  24.1 3.1 %weights.1 = (bf16[256,1536]{1,0:T(8,128)(2,1)S(1)}, f32[1,128]{1,0:T(1,128)S(1)}, bf16[512,256]{1,0:T(8,128)(2,1)S(1)}, f32[1,128]{1,0:T(1,128)S(1)}, bf16[768,...) custom-call(f32[3,3,32]{2,1,0:T(4,128)S(1)} %copy-done.3, f32[1,32]{1,0:T(1,128)S(1)} %bitcast.38, ...), custom_call_target="tpu_custom_call" | custom-call | flops 100000000 | bytes 4000000 | tf_op jit(solution)/shard_map/weights/pallas_call | solution.py:519
  27.2 2.9 %collective-permute-done.3.refs_0_ = bf16[72,3840]{1,0:T(8,128)(2,1)S(1)} collective-permute-done((bf16[72,3840]{1,0:T(8,128)(2,1)}, bf16[72,3840]{1,0:T(8,128)(2,1)S(1)}, u32[]{:S(2)}, u32[]{:S(2)}) %collective-permute-start.3) | collective-permute-done | bytes 552992 | tf_op jit(solution)/shard_map/ppermute | solution.py:28
  30.1 11.8 %collective-permute-done.5.refs_0_ = bf16[72,3840]{1,0:T(8,128)(2,1)S(1)} collective-permute-done((bf16[72,3840]{1,0:T(8,128)(2,1)}, bf16[72,3840]{1,0:T(8,128)(2,1)S(1)}, u32[]{:S(2)}, u32[]{:S(2)}) %collective-permute-start.5) | collective-permute-done | bytes 552992 | tf_op jit(solution)/shard_map/ppermute | solution.py:28
  41.9 11.6 %collective-permute-done.9.refs_0_ = bf16[72,3840]{1,0:T(8,128)(2,1)S(1)} collective-permute-done((bf16[72,3840]{1,0:T(8,128)(2,1)S(1)}, bf16[72,3840]{1,0:T(8,128)(2,1)S(1)}, u32[]{:S(2)}, u32[]{:S(2)}) %collective-permute-start.9) | collective-permute-done | bytes 552992 | tf_op jit(solution)/shard_map/ppermute | solution.py:28
  54.2 11.3 %similarities.5 = (f32[64,128]{1,0:T(8,128)S(1)}, bf16[9,128,3840]{2,1,0:T(8,128)(2,1)S(1)}) custom-call(s32[14]{0:T(128)S(1)} %stack.67.pos_ref, s32[4,4]{1,0:T(4,128)S(1)} %copy-done, bf16[9,128,3840]{2,1,0:T(8,128)(2,1)} %bitcast.48, bf16[288,3840]{1,0:T(8,128)(2,1)} %bitcast.45, bf16[288,3840]{1,0:T(8,128)(2,1)} %collective-permute-done.refs_1_), custom_call_target="tpu_custom_call" | custom-call | flops 5096079360 | bytes 4423680 | tf_op jit(solution)/shard_map/similarities/pallas_call | solution.py:173
  65.5 3.2 %similarities.6.refs_1_.refs_3_ = f32[16,128]{1,0:T(8,128)S(1)} custom-call(s32[14]{0:T(128)S(1)} %stack.67.pos_ref, s32[4,4]{1,0:T(4,128)S(1)} %copy-done, bf16[9,128,3840]{2,1,0:T(8,128)(2,1)S(1)} %get-tuple-element.25.query_ref, bf16[72,3840]{1,0:T(8,128)(2,1)S(1)} %collective-permute-done.1.refs_0_, bf16[72,3840]{1,0:T(8,128)(2,1)S(1)} %collective-permute-done.2.refs_1_), custom_call_target="tpu_custom_call" | custom-call | flops 1274019840 | bytes 1105920 | tf_op jit(solution)/shard_map/similarities/pallas_call | solution.py:173
  68.7 1.3 %collective-permute-start.8 = (f32[8,128]{1,0:T(8,128)S(1)}, f32[8,128]{1,0:T(8,128)S(1)}, u32[]{:S(2)}, u32[]{:S(2)}) collective-permute-start(f32[8,128]{1,0:T(8,128)S(1)} %pad_maximum_fusion.1), channel_id=1, source_target_pairs={{1,0},{2,1},{3,2},{5,4},{6,5},{7,6},{9,8},{10,9},{11,10},{13,12},{... | collective-permute-start | bytes 12296 | tf_op jit(solution)/shard_map/ppermute | solution.py:28
  70.0 3.2 %similarities.7.refs_2_.refs_4_ = f32[16,128]{1,0:T(8,128)S(1)} custom-call(s32[14]{0:T(128)S(1)} %stack.67.pos_ref, s32[4,4]{1,0:T(4,128)S(1)} %copy-done, bf16[9,128,3840]{2,1,0:T(8,128)(2,1)S(1)} %get-tuple-element.25.query_ref, bf16[72,3840]{1,0:T(8,128)(2,1)S(1)} %collective-permute-done.3.refs_0_, bf16[72,3840]{1,0:T(8,128)(2,1)S(1)} %collective-permute-done.4.refs_1_), custom_call_target="tpu_custom_call" | custom-call | flops 1274019840 | bytes 1105920 | tf_op jit(solution)/shard_map/similarities/pallas_call | solution.py:173
  73.2 4.7 %collective-permute-start.7 = (f32[8,128]{1,0:T(8,128)S(1)}, f32[8,128]{1,0:T(8,128)S(1)}, u32[]{:S(2)}, u32[]{:S(2)}) collective-permute-start(f32[8,128]{1,0:T(8,128)S(1)} %pad_maximum_fusion), channel_id=1, source_target_pairs={{0,1},{1,2},{2,3},{4,5},{5,6},{6,7},{8,9},{9,10},{10,11},{12,13},{... | collective-permute-start | bytes 12296 | tf_op jit(solution)/shard_map/ppermute | solution.py:28
  78.0 3.2 %similarities.8.refs_3_.refs_5_ = f32[16,128]{1,0:T(8,128)S(1)} custom-call(s32[14]{0:T(128)S(1)} %stack.67.pos_ref, s32[4,4]{1,0:T(4,128)S(1)} %copy-done, bf16[9,128,3840]{2,1,0:T(8,128)(2,1)S(1)} %get-tuple-element.25.query_ref, bf16[72,3840]{1,0:T(8,128)(2,1)S(1)} %collective-permute-done.5.refs_0_, bf16[72,3840]{1,0:T(8,128)(2,1)S(1)} %collective-permute-done.6.refs_1_), custom_call_target="tpu_custom_call" | custom-call | flops 1274019840 | bytes 1105920 | tf_op jit(solution)/shard_map/similarities/pallas_call | solution.py:173
  81.2 3.2 %similarities.9 = (f32[16,128]{1,0:T(8,128)S(1)}, f32[8,144]{1,0:T(8,128)S(1)}, f32[8,144]{1,0:T(8,128)S(1)}) custom-call(s32[14]{0:T(128)S(1)} %stack.67.pos_ref, s32[4,4]{1,0:T(4,128)S(1)} %copy-done, bf16[9,128,3840]{2,1,0:T(8,128)(2,1)S(1)} %get-tuple-element.25.query_ref, bf16[72,3840]{1,0:T(8,128)(2,1)S(1)} %collective-permute-done.9.refs_0_, ...), custom_call_target="tpu_custom_call" | custom-call | flops 1274019840 | bytes 1105920 | tf_op jit(solution)/shard_map/similarities/pallas_call | solution.py:173
  84.5 1.8 %collective-permute-start.12 = (f32[8,144]{1,0:T(8,128)S(1)}, f32[8,144]{1,0:T(8,128)S(1)}, u32[]{:S(2)}, u32[]{:S(2)}) collective-permute-start(f32[8,144]{1,0:T(8,128)S(1)} %get-tuple-element.36), channel_id=1, source_target_pairs={{4,8},{12,0},{8,4},{0,12},{5,9},{13,1},{9,5},{1,13},{6,10},{14,2},... | collective-permute-start | bytes 13832 | tf_op jit(solution)/shard_map/ppermute | solution.py:28
  86.3 1.2 %assemble.1 = (f32[4,56,256]{2,1,0:T(8,128)S(1)}, f32[36,40,128]{2,1,0:T(8,128)S(1)}) custom-call(s32[14]{0:T(128)S(1)} %stack.67.pos_ref, f32[64,128]{1,0:T(8,128)S(1)} %get-tuple-element.24.refs_0_.refs_2_, f32[16,128]{1,0:T(8,128)S(1)} %similarities.6.refs_1_.refs_3_, f32[16,128]{1,0:T(8,128)S(1)} %similarities.7.refs_2_.refs_4_, ...), custom_call_target="tpu_custom_call" | custom-call | flops 1000000000 | bytes 500000 | tf_op jit(solution)/shard_map/assemble/pallas_call | solution.py:368
  87.7 3.5 %network.1 = (f32[32,32]{1,0:T(8,128)}, f32[2,32]{1,0:T(2,128)S(1)}, f32[4,56,256]{2,1,0:T(8,128)S(1)}, f32[36,40,128]{2,1,0:T(8,128)S(1)}) custom-call(s32[14]{0:T(128)S(1)} %stack.67.pos_ref, s32[2]{0:T(128)S(1)} %copy-done.8, f32[4,56,256]{2,1,0:T(8,128)S(1)} %get-tuple-element.31.refs_0_, ...), custom_call_target="tpu_custom_call", output_to_operand_aliasing={{2}: (2, {}), {3}: (3, {})} | custom-call | flops 6000000000 | bytes 4000000 | tf_op jit(solution)/shard_map/network/pallas_call | solution.py:431
  92.5 1.8 %collective-permute-start.14 = (f32[2,2,32]{2,1,0:T(2,128)S(1)}, f32[2,2,32]{2,1,0:T(2,128)S(1)}, u32[]{:S(2)}, u32[]{:S(2)}) collective-permute-start(f32[2,2,32]{2,1,0:T(2,128)S(1)} %maximum_select_fusion), channel_id=1, source_target_pairs={{0,5},{1,4},{2,7},{3,6},{4,1},{5,0},{6,3},{7,2},{8,13},{9,12},{10,... | collective-permute-start | bytes 1544 | tf_op jit(solution)/shard_map/ppermute | solution.py:28
  95.5 2.7 %collective-permute-start.15 = (f32[2,2,32]{2,1,0:T(2,128)S(1)}, f32[2,2,32]{2,1,0:T(2,128)S(1)}, u32[]{:S(2)}, u32[]{:S(2)}) collective-permute-start(f32[2,2,32]{2,1,0:T(2,128)S(1)} %fusion.3), channel_id=1, source_target_pairs={{0,6},{1,7},{2,4},{3,5},{4,2},{5,3},{6,0},{7,1},{8,14},{9,15},{10,... | collective-permute-start | bytes 1544 | tf_op jit(solution)/shard_map/ppermute | solution.py:28
  98.3 1.3 %collective-permute-done.15 = f32[2,2,32]{2,1,0:T(2,128)S(1)} collective-permute-done((f32[2,2,32]{2,1,0:T(2,128)S(1)}, f32[2,2,32]{2,1,0:T(2,128)S(1)}, u32[]{:S(2)}, u32[]{:S(2)}) %collective-permute-start.15) | collective-permute-done | bytes 544 | tf_op jit(solution)/shard_map/ppermute | solution.py:28
  99.7 1.5 %collective-permute-start.16 = (f32[2]{0:T(128)S(1)}, f32[2]{0:T(128)S(1)}, u32[]{:S(2)}, u32[]{:S(2)}) collective-permute-start(f32[2]{0:T(128)S(1)} %select_reduce_fusion), channel_id=1, source_target_pairs={{0,12},{1,13},{2,14},{3,15},{4,8},{5,9},{6,10},{7,11},{8,4},{9,5},... | collective-permute-start | bytes 32 | tf_op jit(solution)/shard_map/ppermute | solution.py:28
  101.2 1.5 %collective-permute-done.16 = f32[2]{0:T(128)S(1)} collective-permute-done((f32[2]{0:T(128)S(1)}, f32[2]{0:T(128)S(1)}, u32[]{:S(2)}, u32[]{:S(2)}) %collective-permute-start.16) | collective-permute-done | bytes 40 | tf_op jit(solution)/shard_map/ppermute | solution.py:28
  (49 shorter events, 9.4 us)
Async XLA Ops:
  1.7 51.8 %collective-permute-start = (bf16[288,3840]{1,0:T(8,128)(2,1)}, bf16[288,3840]{1,0:T(8,128)(2,1)}, u32[]{:S(2)}, u32[]{:S(2)}) collective-permute-start(bf16[288,3840]{1,0:T(8,128)(2,1)} %bitcast.43), channel_id=1, source_target_pairs={{0,4},{4,0},{8,12},{12,8},{1,5},{5,1},{9,13},{13,9},{2,6},{6,2},{1... | collective-permute-start | bytes 6635528 | tf_op jit(solution)/shard_map/ppermute | solution.py:28
  2.3 15.9 %collective-permute-start.1 = (bf16[72,3840]{1,0:T(8,128)(2,1)S(1)}, bf16[72,3840]{1,0:T(8,128)(2,1)S(1)}, u32[]{:S(2)}, u32[]{:S(2)}) collective-permute-start(bf16[72,3840]{1,0:T(8,128)(2,1)S(1)} %bitcast.32), channel_id=1, source_target_pairs={{0,8},{4,12},{8,0},{12,4},{1,9},{5,13},{9,1},{13,5},{2,10},{6,14},... | collective-permute-start | bytes 1658888 | tf_op jit(solution)/shard_map/ppermute | solution.py:28
  7.2 22.8 %collective-permute-start.3 = (bf16[72,3840]{1,0:T(8,128)(2,1)}, bf16[72,3840]{1,0:T(8,128)(2,1)S(1)}, u32[]{:S(2)}, u32[]{:S(2)}) collective-permute-start(bf16[72,3840]{1,0:T(8,128)(2,1)} %bitcast.18), channel_id=1, source_target_pairs={{0,8},{4,12},{8,0},{12,4},{1,9},{5,13},{9,1},{13,5},{2,10},{6,14},... | collective-permute-start | bytes 1658888 | tf_op jit(solution)/shard_map/ppermute | solution.py:28
  7.3 34.6 %collective-permute-start.5 = (bf16[72,3840]{1,0:T(8,128)(2,1)}, bf16[72,3840]{1,0:T(8,128)(2,1)S(1)}, u32[]{:S(2)}, u32[]{:S(2)}) collective-permute-start(bf16[72,3840]{1,0:T(8,128)(2,1)} %bitcast.19), channel_id=1, source_target_pairs={{0,8},{4,12},{8,0},{12,4},{1,9},{5,13},{9,1},{13,5},{2,10},{6,14},... | collective-permute-start | bytes 1658888 | tf_op jit(solution)/shard_map/ppermute | solution.py:28
  9.3 44.2 %collective-permute-start.9 = (bf16[72,3840]{1,0:T(8,128)(2,1)S(1)}, bf16[72,3840]{1,0:T(8,128)(2,1)S(1)}, u32[]{:S(2)}, u32[]{:S(2)}) collective-permute-start(bf16[72,3840]{1,0:T(8,128)(2,1)S(1)} %bitcast.35), channel_id=1, source_target_pairs={{0,8},{4,12},{8,0},{12,4},{1,9},{5,13},{9,1},{13,5},{2,10},{6,14},... | collective-permute-start | bytes 1658888 | tf_op jit(solution)/shard_map/ppermute | solution.py:28
  18.2 47.3 %collective-permute-start.2 = (bf16[72,3840]{1,0:T(8,128)(2,1)S(1)}, bf16[72,3840]{1,0:T(8,128)(2,1)S(1)}, u32[]{:S(2)}, u32[]{:S(2)}) collective-permute-start(bf16[72,3840]{1,0:T(8,128)(2,1)S(1)} %collective-permute-done.1.refs_0_), channel_id=1, source_target_pairs={{0,4},{4,0},{8,12},{12,8},{1,5},{5,1},{9,13},{13,9},{2,6},{6,2},{1... | collective-permute-start | bytes 1658888 | tf_op jit(solution)/shard_map/ppermute | solution.py:28
  19.0 0.9 copy-start.1
  19.9 0.9 copy-start.2
  20.8 0.7 copy-start.3
  21.4 0.7 copy-start.4
  22.1 0.7 copy-start.5
  30.1 40.0 %collective-permute-start.4 = (bf16[72,3840]{1,0:T(8,128)(2,1)S(1)}, bf16[72,3840]{1,0:T(8,128)(2,1)S(1)}, u32[]{:S(2)}, u32[]{:S(2)}) collective-permute-start(bf16[72,3840]{1,0:T(8,128)(2,1)S(1)} %collective-permute-done.3.refs_0_), channel_id=1, source_target_pairs={{0,4},{4,0},{8,12},{12,8},{1,5},{5,1},{9,13},{13,9},{2,6},{6,2},{1... | collective-permute-start | bytes 1658888 | tf_op jit(solution)/shard_map/ppermute | solution.py:28
  41.9 36.1 %collective-permute-start.6 = (bf16[72,3840]{1,0:T(8,128)(2,1)S(1)}, bf16[72,3840]{1,0:T(8,128)(2,1)S(1)}, u32[]{:S(2)}, u32[]{:S(2)}) collective-permute-start(bf16[72,3840]{1,0:T(8,128)(2,1)S(1)} %collective-permute-done.5.refs_0_), channel_id=1, source_target_pairs={{0,4},{4,0},{8,12},{12,8},{1,5},{5,1},{9,13},{13,9},{2,6},{6,2},{1... | collective-permute-start | bytes 1658888 | tf_op jit(solution)/shard_map/ppermute | solution.py:28
  53.5 27.7 %collective-permute-start.10 = (bf16[72,3840]{1,0:T(8,128)(2,1)S(1)}, bf16[72,3840]{1,0:T(8,128)(2,1)S(1)}, u32[]{:S(2)}, u32[]{:S(2)}) collective-permute-start(bf16[72,3840]{1,0:T(8,128)(2,1)S(1)} %collective-permute-done.9.refs_0_), channel_id=1, source_target_pairs={{0,4},{4,0},{8,12},{12,8},{1,5},{5,1},{9,13},{13,9},{2,6},{6,2},{1... | collective-permute-start | bytes 1658888 | tf_op jit(solution)/shard_map/ppermute | solution.py:28
  53.5 0.7 copy-start
  68.7 12.5 %collective-permute-start.8 = (f32[8,128]{1,0:T(8,128)S(1)}, f32[8,128]{1,0:T(8,128)S(1)}, u32[]{:S(2)}, u32[]{:S(2)}) collective-permute-start(f32[8,128]{1,0:T(8,128)S(1)} %pad_maximum_fusion.1), channel_id=1, source_target_pairs={{1,0},{2,1},{3,2},{5,4},{6,5},{7,6},{9,8},{10,9},{11,10},{13,12},{... | collective-permute-start | bytes 12296 | tf_op jit(solution)/shard_map/ppermute | solution.py:28
  73.2 8.0 %collective-permute-start.7 = (f32[8,128]{1,0:T(8,128)S(1)}, f32[8,128]{1,0:T(8,128)S(1)}, u32[]{:S(2)}, u32[]{:S(2)}) collective-permute-start(f32[8,128]{1,0:T(8,128)S(1)} %pad_maximum_fusion), channel_id=1, source_target_pairs={{0,1},{1,2},{2,3},{4,5},{5,6},{6,7},{8,9},{9,10},{10,11},{12,13},{... | collective-permute-start | bytes 12296 | tf_op jit(solution)/shard_map/ppermute | solution.py:28
  81.2 6.5 %copy-start.8 = (s32[2]{0:T(128)S(1)}, s32[2]{0:T(128)}, u32[]{:S(2)}) copy-start(s32[2]{0:T(128)} %len_ref.1) | copy-start | bytes 28
  84.5 3.1 %collective-permute-start.11 = (f32[8,144]{1,0:T(8,128)S(1)}, f32[8,144]{1,0:T(8,128)S(1)}, u32[]{:S(2)}, u32[]{:S(2)}) collective-permute-start(f32[8,144]{1,0:T(8,128)S(1)} %get-tuple-element.35), channel_id=1, source_target_pairs={{0,4},{4,0},{8,12},{12,8},{1,5},{5,1},{9,13},{13,9},{2,6},{6,2},{1... | collective-permute-start | bytes 13832 | tf_op jit(solution)/shard_map/ppermute | solution.py:28
  84.5 3.2 %collective-permute-start.12 = (f32[8,144]{1,0:T(8,128)S(1)}, f32[8,144]{1,0:T(8,128)S(1)}, u32[]{:S(2)}, u32[]{:S(2)}) collective-permute-start(f32[8,144]{1,0:T(8,128)S(1)} %get-tuple-element.36), channel_id=1, source_target_pairs={{4,8},{12,0},{8,4},{0,12},{5,9},{13,1},{9,5},{1,13},{6,10},{14,2},... | collective-permute-start | bytes 13832 | tf_op jit(solution)/shard_map/ppermute | solution.py:28
  91.3 1.2 %collective-permute-start.13 = (f32[2,32]{1,0:T(2,128)S(1)}, f32[2,32]{1,0:T(2,128)S(1)}, u32[]{:S(2)}, u32[]{:S(2)}) collective-permute-start(f32[2,32]{1,0:T(2,128)S(1)} %get-tuple-element.43), channel_id=1, source_target_pairs={{0,4},{4,0},{8,12},{12,8},{1,5},{5,1},{9,13},{13,9},{2,6},{6,2},{1... | collective-permute-start | bytes 776 | tf_op jit(solution)/shard_map/ppermute | solution.py:28
  92.5 3.1 %collective-permute-start.14 = (f32[2,2,32]{2,1,0:T(2,128)S(1)}, f32[2,2,32]{2,1,0:T(2,128)S(1)}, u32[]{:S(2)}, u32[]{:S(2)}) collective-permute-start(f32[2,2,32]{2,1,0:T(2,128)S(1)} %maximum_select_fusion), channel_id=1, source_target_pairs={{0,5},{1,4},{2,7},{3,6},{4,1},{5,0},{6,3},{7,2},{8,13},{9,12},{10,... | collective-permute-start | bytes 1544 | tf_op jit(solution)/shard_map/ppermute | solution.py:28
  95.5 4.0 %collective-permute-start.15 = (f32[2,2,32]{2,1,0:T(2,128)S(1)}, f32[2,2,32]{2,1,0:T(2,128)S(1)}, u32[]{:S(2)}, u32[]{:S(2)}) collective-permute-start(f32[2,2,32]{2,1,0:T(2,128)S(1)} %fusion.3), channel_id=1, source_target_pairs={{0,6},{1,7},{2,4},{3,5},{4,2},{5,3},{6,0},{7,1},{8,14},{9,15},{10,... | collective-permute-start | bytes 1544 | tf_op jit(solution)/shard_map/ppermute | solution.py:28
  99.7 3.1 %collective-permute-start.16 = (f32[2]{0:T(128)S(1)}, f32[2]{0:T(128)S(1)}, u32[]{:S(2)}, u32[]{:S(2)}) collective-permute-start(f32[2]{0:T(128)S(1)} %select_reduce_fusion), channel_id=1, source_target_pairs={{0,12},{1,13},{2,14},{3,15},{4,8},{5,9},{6,10},{7,11},{8,4},{9,5},... | collective-permute-start | bytes 32 | tf_op jit(solution)/shard_map/ppermute | solution.py:28
  (2 other events, 1.3 us)

commit v5 on v4

--- a/solution.py
+++ b/solution.py
@@ -96,7 +96,8 @@
     if fetch:
         rows_ref, sems = refs[-2], refs[-1]
     regions, frames, channels = query_ref.shape
-    width = 3 if regions % 3 == 0 else 1
+    width = (3 if regions % 3 == 0 else 1) if fetch else regions
+    blocks = [(at, min(width, regions - at)) for at in range(0, regions, width)]
     if fetch:
         copies, arriving = [], []
         start = 0
@@ -106,8 +107,8 @@
             start += span * regions
         for copy in copies:
             copy.start()
-        for step in range(regions // width):
-            block = pl.ds(step * width, width)
+        for step, (at, size) in enumerate(blocks):
+            block = pl.ds(at, size)
             arriving.append(
                 pltpu.make_async_copy(
                     query_ref.at[block], refs[1].at[block], sems.at[len(spans) + step]
@@ -120,7 +121,7 @@
             copy.wait()
 
     total = None
-    for step in range(regions // width):
+    for step, (at, size) in enumerate(blocks):
         if fetch:
             arriving[step].wait()
         rows = (
@@ -130,7 +131,7 @@
         )
         products = lax.dot_general(
             rows,
-            query_ref[step * width : (step + 1) * width].reshape(-1, channels),
+            query_ref[at : at + size].reshape(-1, channels),
             (((1,), (1,)), ((), ())),
             preferred_element_type=F32,
         )
@@ -143,7 +144,7 @@
                     best, products[start + other * span : start + (other + 1) * span]
                 )
             part = best[:, 0:frames]
-            for other in range(1, width):
+            for other in range(1, size):
                 part = part + best[:, other * frames : (other + 1) * frames]
             parts.append(part)
             start += span * regions

time: 104 us -> 105 us (level)
  Pallas kernels: 35.4 us -> 36.7 us
    pallas_call x5, Pallas kernels: 24.1 us -> 25.3 us  [similarities(): pl.pallas_call(functools.partial(sims_kernel, scale, spans, len(done), fe...]
where the time goes in v5:
time: 105 us
  waiting for transfers between devices  39.6 us (38%)
  Pallas kernels  36.7 us (35%)
  starting transfers between devices  19.6 us (19%)
  local copies, waits for them, and re-layouts  5.89 us (6%)
  between operations  2.14 us (2%)
    ppermute x17, waiting for transfers between devices, shift(): return lax.ppermute(array, axis, pairs)  39.6 us
    pallas_call x5, Pallas kernels, similarities(): pl.pallas_call(functools.partial(sims_kernel, scale, spans, len(done), fe...  25.3 us
    ppermute x17, starting transfers between devices, shift(): return lax.ppermute(array, axis, pairs)  19.6 us
    unnamed x18, local copies, waits for them, and re-layouts  5.79 us
    pallas_call x1, Pallas kernels, network(): pl.pallas_call(functools.partial(network_kernel, limits, padding, starts,...  3.54 us
    pallas_call x2, Pallas kernels, cut(): pl.pallas_call(functools.partial(cut_kernel, order), in_specs=[pl.BlockSp...  3.49 us
    pallas_call x1, Pallas kernels, network_weights(): pl.pallas_call(weights_kernel, out_shape=[jax.ShapeDtypeStruct(shape, dty...  3.09 us
  transfers between devices with their start and end apart: 17, of which 9 were waited for; matrix products, arithmetic and copies ran while one was open for 0% of the time, Pallas kernels for 27%

profile of v5, /device:TPU:0, one launch (start us, length us, event | category | flops | bytes accessed | tf_op | source)
XLA Modules:
  0.0 104.5 jit_solution(4365564282020228822)
XLA Ops:
  0.6 1.1 %cut.2 = bf16[9,8,3840]{2,1,0:T(8,128)(2,1)S(1)} custom-call(bf16[9,32,3840]{2,1,0:T(8,128)(2,1)} %bitcast.42), custom_call_target="tpu_custom_call" | custom-call | bytes 4423680 | tf_op jit(solution)/shard_map/cut/pallas_call | solution.py:46
  2.3 2.6 %collective-permute-start.1 = (bf16[72,3840]{1,0:T(8,128)(2,1)S(1)}, bf16[72,3840]{1,0:T(8,128)(2,1)S(1)}, u32[]{:S(2)}, u32[]{:S(2)}) collective-permute-start(bf16[72,3840]{1,0:T(8,128)(2,1)S(1)} %bitcast.32), channel_id=1, source_target_pairs={{0,8},{4,12},{8,0},{12,4},{1,9},{5,13},{9,1},{13,5},{2,10},{6,14},... | collective-permute-start | bytes 1658888 | tf_op jit(solution)/shard_map/ppermute | solution.py:28
  4.8 2.4 %cut.3 = (bf16[9,8,3840]{2,1,0:T(8,128)(2,1)}, bf16[9,8,3840]{2,1,0:T(8,128)(2,1)}, bf16[9,8,3840]{2,1,0:T(8,128)(2,1)S(1)}) custom-call(bf16[9,32,3840]{2,1,0:T(8,128)(2,1)} %bitcast.44), custom_call_target="tpu_custom_call" | custom-call | bytes 4423680 | tf_op jit(solution)/shard_map/cut/pallas_call | solution.py:46
  7.3 2.0 %collective-permute-start.5 = (bf16[72,3840]{1,0:T(8,128)(2,1)}, bf16[72,3840]{1,0:T(8,128)(2,1)S(1)}, u32[]{:S(2)}, u32[]{:S(2)}) collective-permute-start(bf16[72,3840]{1,0:T(8,128)(2,1)} %bitcast.19), channel_id=1, source_target_pairs={{0,8},{4,12},{8,0},{12,4},{1,9},{5,13},{9,1},{13,5},{2,10},{6,14},... | collective-permute-start | bytes 1658888 | tf_op jit(solution)/shard_map/ppermute | solution.py:28
  9.4 8.8 %collective-permute-done.1.refs_0_ = bf16[72,3840]{1,0:T(8,128)(2,1)S(1)} collective-permute-done((bf16[72,3840]{1,0:T(8,128)(2,1)S(1)}, bf16[72,3840]{1,0:T(8,128)(2,1)S(1)}, u32[]{:S(2)}, u32[]{:S(2)}) %collective-permute-start.1) | collective-permute-done | bytes 552992 | tf_op jit(solution)/shard_map/ppermute | solution.py:28
  24.1 3.1 %weights.1 = (bf16[256,1536]{1,0:T(8,128)(2,1)S(1)}, f32[1,128]{1,0:T(1,128)S(1)}, bf16[512,256]{1,0:T(8,128)(2,1)S(1)}, f32[1,128]{1,0:T(1,128)S(1)}, bf16[768,...) custom-call(f32[3,3,32]{2,1,0:T(4,128)S(1)} %copy-done.3, f32[1,32]{1,0:T(1,128)S(1)} %bitcast.38, ...), custom_call_target="tpu_custom_call" | custom-call | flops 100000000 | bytes 4000000 | tf_op jit(solution)/shard_map/weights/pallas_call | solution.py:520
  27.2 2.9 %collective-permute-done.3.refs_0_ = bf16[72,3840]{1,0:T(8,128)(2,1)S(1)} collective-permute-done((bf16[72,3840]{1,0:T(8,128)(2,1)}, bf16[72,3840]{1,0:T(8,128)(2,1)S(1)}, u32[]{:S(2)}, u32[]{:S(2)}) %collective-permute-start.3) | collective-permute-done | bytes 552992 | tf_op jit(solution)/shard_map/ppermute | solution.py:28
  30.1 11.8 %collective-permute-done.5.refs_0_ = bf16[72,3840]{1,0:T(8,128)(2,1)S(1)} collective-permute-done((bf16[72,3840]{1,0:T(8,128)(2,1)}, bf16[72,3840]{1,0:T(8,128)(2,1)S(1)}, u32[]{:S(2)}, u32[]{:S(2)}) %collective-permute-start.5) | collective-permute-done | bytes 552992 | tf_op jit(solution)/shard_map/ppermute | solution.py:28
  41.9 11.6 %collective-permute-done.9.refs_0_ = bf16[72,3840]{1,0:T(8,128)(2,1)S(1)} collective-permute-done((bf16[72,3840]{1,0:T(8,128)(2,1)S(1)}, bf16[72,3840]{1,0:T(8,128)(2,1)S(1)}, u32[]{:S(2)}, u32[]{:S(2)}) %collective-permute-start.9) | collective-permute-done | bytes 552992 | tf_op jit(solution)/shard_map/ppermute | solution.py:28
  54.2 11.3 %similarities.5 = (f32[64,128]{1,0:T(8,128)S(1)}, bf16[9,128,3840]{2,1,0:T(8,128)(2,1)S(1)}) custom-call(s32[14]{0:T(128)S(1)} %stack.67.pos_ref, s32[4,4]{1,0:T(4,128)S(1)} %copy-done, bf16[9,128,3840]{2,1,0:T(8,128)(2,1)} %bitcast.48, bf16[288,3840]{1,0:T(8,128)(2,1)} %bitcast.45, bf16[288,3840]{1,0:T(8,128)(2,1)} %collective-permute-done.refs_1_), custom_call_target="tpu_custom_call" | custom-call | flops 5096079360 | bytes 4423680 | tf_op jit(solution)/shard_map/similarities/pallas_call | solution.py:174
  65.5 3.5 %similarities.6.refs_1_.refs_3_ = f32[16,128]{1,0:T(8,128)S(1)} custom-call(s32[14]{0:T(128)S(1)} %stack.67.pos_ref, s32[4,4]{1,0:T(4,128)S(1)} %copy-done, bf16[9,128,3840]{2,1,0:T(8,128)(2,1)S(1)} %get-tuple-element.25.query_ref, bf16[72,3840]{1,0:T(8,128)(2,1)S(1)} %collective-permute-done.1.refs_0_, bf16[72,3840]{1,0:T(8,128)(2,1)S(1)} %collective-permute-done.2.refs_1_), custom_call_target="tpu_custom_call" | custom-call | flops 1274019840 | bytes 1105920 | tf_op jit(solution)/shard_map/similarities/pallas_call | solution.py:174
  69.0 1.3 %collective-permute-start.8 = (f32[8,128]{1,0:T(8,128)S(1)}, f32[8,128]{1,0:T(8,128)S(1)}, u32[]{:S(2)}, u32[]{:S(2)}) collective-permute-start(f32[8,128]{1,0:T(8,128)S(1)} %pad_maximum_fusion.1), channel_id=1, source_target_pairs={{1,0},{2,1},{3,2},{5,4},{6,5},{7,6},{9,8},{10,9},{11,10},{13,12},{... | collective-permute-start | bytes 12296 | tf_op jit(solution)/shard_map/ppermute | solution.py:28
  70.3 3.5 %similarities.7.refs_2_.refs_4_ = f32[16,128]{1,0:T(8,128)S(1)} custom-call(s32[14]{0:T(128)S(1)} %stack.67.pos_ref, s32[4,4]{1,0:T(4,128)S(1)} %copy-done, bf16[9,128,3840]{2,1,0:T(8,128)(2,1)S(1)} %get-tuple-element.25.query_ref, bf16[72,3840]{1,0:T(8,128)(2,1)S(1)} %collective-permute-done.3.refs_0_, bf16[72,3840]{1,0:T(8,128)(2,1)S(1)} %collective-permute-done.4.refs_1_), custom_call_target="tpu_custom_call" | custom-call | flops 1274019840 | bytes 1105920 | tf_op jit(solution)/shard_map/similarities/pallas_call | solution.py:174
  73.9 4.7 %collective-permute-start.7 = (f32[8,128]{1,0:T(8,128)S(1)}, f32[8,128]{1,0:T(8,128)S(1)}, u32[]{:S(2)}, u32[]{:S(2)}) collective-permute-start(f32[8,128]{1,0:T(8,128)S(1)} %pad_maximum_fusion), channel_id=1, source_target_pairs={{0,1},{1,2},{2,3},{4,5},{5,6},{6,7},{8,9},{9,10},{10,11},{12,13},{... | collective-permute-start | bytes 12296 | tf_op jit(solution)/shard_map/ppermute | solution.py:28
  78.6 3.5 %similarities.8.refs_3_.refs_5_ = f32[16,128]{1,0:T(8,128)S(1)} custom-call(s32[14]{0:T(128)S(1)} %stack.67.pos_ref, s32[4,4]{1,0:T(4,128)S(1)} %copy-done, bf16[9,128,3840]{2,1,0:T(8,128)(2,1)S(1)} %get-tuple-element.25.query_ref, bf16[72,3840]{1,0:T(8,128)(2,1)S(1)} %collective-permute-done.5.refs_0_, bf16[72,3840]{1,0:T(8,128)(2,1)S(1)} %collective-permute-done.6.refs_1_), custom_call_target="tpu_custom_call" | custom-call | flops 1274019840 | bytes 1105920 | tf_op jit(solution)/shard_map/similarities/pallas_call | solution.py:174
  82.2 3.6 %similarities.9 = (f32[16,128]{1,0:T(8,128)S(1)}, f32[8,144]{1,0:T(8,128)S(1)}, f32[8,144]{1,0:T(8,128)S(1)}) custom-call(s32[14]{0:T(128)S(1)} %stack.67.pos_ref, s32[4,4]{1,0:T(4,128)S(1)} %copy-done, bf16[9,128,3840]{2,1,0:T(8,128)(2,1)S(1)} %get-tuple-element.25.query_ref, bf16[72,3840]{1,0:T(8,128)(2,1)S(1)} %collective-permute-done.9.refs_0_, ...), custom_call_target="tpu_custom_call" | custom-call | flops 1274019840 | bytes 1105920 | tf_op jit(solution)/shard_map/similarities/pallas_call | solution.py:174
  85.8 1.8 %collective-permute-start.12 = (f32[8,144]{1,0:T(8,128)S(1)}, f32[8,144]{1,0:T(8,128)S(1)}, u32[]{:S(2)}, u32[]{:S(2)}) collective-permute-start(f32[8,144]{1,0:T(8,128)S(1)} %get-tuple-element.36), channel_id=1, source_target_pairs={{4,8},{12,0},{8,4},{0,12},{5,9},{13,1},{9,5},{1,13},{6,10},{14,2},... | collective-permute-start | bytes 13832 | tf_op jit(solution)/shard_map/ppermute | solution.py:28
  87.6 1.2 %assemble.1 = (f32[4,56,256]{2,1,0:T(8,128)S(1)}, f32[36,40,128]{2,1,0:T(8,128)S(1)}) custom-call(s32[14]{0:T(128)S(1)} %stack.67.pos_ref, f32[64,128]{1,0:T(8,128)S(1)} %get-tuple-element.24.refs_0_.refs_2_, f32[16,128]{1,0:T(8,128)S(1)} %similarities.6.refs_1_.refs_3_, f32[16,128]{1,0:T(8,128)S(1)} %similarities.7.refs_2_.refs_4_, ...), custom_call_target="tpu_custom_call" | custom-call | flops 1000000000 | bytes 500000 | tf_op jit(solution)/shard_map/assemble/pallas_call | solution.py:369
  89.0 3.5 %network.1 = (f32[32,32]{1,0:T(8,128)}, f32[2,32]{1,0:T(2,128)S(1)}, f32[4,56,256]{2,1,0:T(8,128)S(1)}, f32[36,40,128]{2,1,0:T(8,128)S(1)}) custom-call(s32[14]{0:T(128)S(1)} %stack.67.pos_ref, s32[2]{0:T(128)S(1)} %copy-done.8, f32[4,56,256]{2,1,0:T(8,128)S(1)} %get-tuple-element.31.refs_0_, ...), custom_call_target="tpu_custom_call", output_to_operand_aliasing={{2}: (2, {}), {3}: (3, {})} | custom-call | flops 6000000000 | bytes 4000000 | tf_op jit(solution)/shard_map/network/pallas_call | solution.py:432
  93.7 1.8 %collective-permute-start.14 = (f32[2,2,32]{2,1,0:T(2,128)S(1)}, f32[2,2,32]{2,1,0:T(2,128)S(1)}, u32[]{:S(2)}, u32[]{:S(2)}) collective-permute-start(f32[2,2,32]{2,1,0:T(2,128)S(1)} %maximum_select_fusion), channel_id=1, source_target_pairs={{0,5},{1,4},{2,7},{3,6},{4,1},{5,0},{6,3},{7,2},{8,13},{9,12},{10,... | collective-permute-start | bytes 1544 | tf_op jit(solution)/shard_map/ppermute | solution.py:28
  96.8 2.7 %collective-permute-start.15 = (f32[2,2,32]{2,1,0:T(2,128)S(1)}, f32[2,2,32]{2,1,0:T(2,128)S(1)}, u32[]{:S(2)}, u32[]{:S(2)}) collective-permute-start(f32[2,2,32]{2,1,0:T(2,128)S(1)} %fusion.3), channel_id=1, source_target_pairs={{0,6},{1,7},{2,4},{3,5},{4,2},{5,3},{6,0},{7,1},{8,14},{9,15},{10,... | collective-permute-start | bytes 1544 | tf_op jit(solution)/shard_map/ppermute | solution.py:28
  99.5 1.3 %collective-permute-done.15 = f32[2,2,32]{2,1,0:T(2,128)S(1)} collective-permute-done((f32[2,2,32]{2,1,0:T(2,128)S(1)}, f32[2,2,32]{2,1,0:T(2,128)S(1)}, u32[]{:S(2)}, u32[]{:S(2)}) %collective-permute-start.15) | collective-permute-done | bytes 544 | tf_op jit(solution)/shard_map/ppermute | solution.py:28
  101.0 1.6 %collective-permute-start.16 = (f32[2]{0:T(128)S(1)}, f32[2]{0:T(128)S(1)}, u32[]{:S(2)}, u32[]{:S(2)}) collective-permute-start(f32[2]{0:T(128)S(1)} %select_reduce_fusion), channel_id=1, source_target_pairs={{0,12},{1,13},{2,14},{3,15},{4,8},{5,9},{6,10},{7,11},{8,4},{9,5},... | collective-permute-start | bytes 32 | tf_op jit(solution)/shard_map/ppermute | solution.py:28
  102.5 1.5 %collective-permute-done.16 = f32[2]{0:T(128)S(1)} collective-permute-done((f32[2]{0:T(128)S(1)}, f32[2]{0:T(128)S(1)}, u32[]{:S(2)}, u32[]{:S(2)}) %collective-permute-start.16) | collective-permute-done | bytes 40 | tf_op jit(solution)/shard_map/ppermute | solution.py:28
  (49 shorter events, 9.4 us)
Async XLA Ops:
  1.7 51.8 %collective-permute-start = (bf16[288,3840]{1,0:T(8,128)(2,1)}, bf16[288,3840]{1,0:T(8,128)(2,1)}, u32[]{:S(2)}, u32[]{:S(2)}) collective-permute-start(bf16[288,3840]{1,0:T(8,128)(2,1)} %bitcast.43), channel_id=1, source_target_pairs={{0,4},{4,0},{8,12},{12,8},{1,5},{5,1},{9,13},{13,9},{2,6},{6,2},{1... | collective-permute-start | bytes 6635528 | tf_op jit(solution)/shard_map/ppermute | solution.py:28
  2.3 15.9 %collective-permute-start.1 = (bf16[72,3840]{1,0:T(8,128)(2,1)S(1)}, bf16[72,3840]{1,0:T(8,128)(2,1)S(1)}, u32[]{:S(2)}, u32[]{:S(2)}) collective-permute-start(bf16[72,3840]{1,0:T(8,128)(2,1)S(1)} %bitcast.32), channel_id=1, source_target_pairs={{0,8},{4,12},{8,0},{12,4},{1,9},{5,13},{9,1},{13,5},{2,10},{6,14},... | collective-permute-start | bytes 1658888 | tf_op jit(solution)/shard_map/ppermute | solution.py:28
  7.2 22.8 %collective-permute-start.3 = (bf16[72,3840]{1,0:T(8,128)(2,1)}, bf16[72,3840]{1,0:T(8,128)(2,1)S(1)}, u32[]{:S(2)}, u32[]{:S(2)}) collective-permute-start(bf16[72,3840]{1,0:T(8,128)(2,1)} %bitcast.18), channel_id=1, source_target_pairs={{0,8},{4,12},{8,0},{12,4},{1,9},{5,13},{9,1},{13,5},{2,10},{6,14},... | collective-permute-start | bytes 1658888 | tf_op jit(solution)/shard_map/ppermute | solution.py:28
  7.3 34.6 %collective-permute-start.5 = (bf16[72,3840]{1,0:T(8,128)(2,1)}, bf16[72,3840]{1,0:T(8,128)(2,1)S(1)}, u32[]{:S(2)}, u32[]{:S(2)}) collective-permute-start(bf16[72,3840]{1,0:T(8,128)(2,1)} %bitcast.19), channel_id=1, source_target_pairs={{0,8},{4,12},{8,0},{12,4},{1,9},{5,13},{9,1},{13,5},{2,10},{6,14},... | collective-permute-start | bytes 1658888 | tf_op jit(solution)/shard_map/ppermute | solution.py:28
  9.3 44.2 %collective-permute-start.9 = (bf16[72,3840]{1,0:T(8,128)(2,1)S(1)}, bf16[72,3840]{1,0:T(8,128)(2,1)S(1)}, u32[]{:S(2)}, u32[]{:S(2)}) collective-permute-start(bf16[72,3840]{1,0:T(8,128)(2,1)S(1)} %bitcast.35), channel_id=1, source_target_pairs={{0,8},{4,12},{8,0},{12,4},{1,9},{5,13},{9,1},{13,5},{2,10},{6,14},... | collective-permute-start | bytes 1658888 | tf_op jit(solution)/shard_map/ppermute | solution.py:28
  18.2 47.3 %collective-permute-start.2 = (bf16[72,3840]{1,0:T(8,128)(2,1)S(1)}, bf16[72,3840]{1,0:T(8,128)(2,1)S(1)}, u32[]{:S(2)}, u32[]{:S(2)}) collective-permute-start(bf16[72,3840]{1,0:T(8,128)(2,1)S(1)} %collective-permute-done.1.refs_0_), channel_id=1, source_target_pairs={{0,4},{4,0},{8,12},{12,8},{1,5},{5,1},{9,13},{13,9},{2,6},{6,2},{1... | collective-permute-start | bytes 1658888 | tf_op jit(solution)/shard_map/ppermute | solution.py:28
  19.0 0.9 copy-start.1
  19.9 0.9 copy-start.2
  20.8 0.7 copy-start.3
  21.4 0.7 copy-start.4
  22.1 0.7 copy-start.5
  30.1 40.3 %collective-permute-start.4 = (bf16[72,3840]{1,0:T(8,128)(2,1)S(1)}, bf16[72,3840]{1,0:T(8,128)(2,1)S(1)}, u32[]{:S(2)}, u32[]{:S(2)}) collective-permute-start(bf16[72,3840]{1,0:T(8,128)(2,1)S(1)} %collective-permute-done.3.refs_0_), channel_id=1, source_target_pairs={{0,4},{4,0},{8,12},{12,8},{1,5},{5,1},{9,13},{13,9},{2,6},{6,2},{1... | collective-permute-start | bytes 1658888 | tf_op jit(solution)/shard_map/ppermute | solution.py:28
  41.9 36.7 %collective-permute-start.6 = (bf16[72,3840]{1,0:T(8,128)(2,1)S(1)}, bf16[72,3840]{1,0:T(8,128)(2,1)S(1)}, u32[]{:S(2)}, u32[]{:S(2)}) collective-permute-start(bf16[72,3840]{1,0:T(8,128)(2,1)S(1)} %collective-permute-done.5.refs_0_), channel_id=1, source_target_pairs={{0,4},{4,0},{8,12},{12,8},{1,5},{5,1},{9,13},{13,9},{2,6},{6,2},{1... | collective-permute-start | bytes 1658888 | tf_op jit(solution)/shard_map/ppermute | solution.py:28
  53.5 28.7 %collective-permute-start.10 = (bf16[72,3840]{1,0:T(8,128)(2,1)S(1)}, bf16[72,3840]{1,0:T(8,128)(2,1)S(1)}, u32[]{:S(2)}, u32[]{:S(2)}) collective-permute-start(bf16[72,3840]{1,0:T(8,128)(2,1)S(1)} %collective-permute-done.9.refs_0_), channel_id=1, source_target_pairs={{0,4},{4,0},{8,12},{12,8},{1,5},{5,1},{9,13},{13,9},{2,6},{6,2},{1... | collective-permute-start | bytes 1658888 | tf_op jit(solution)/shard_map/ppermute | solution.py:28
  53.5 0.7 copy-start
  69.0 13.1 %collective-permute-start.8 = (f32[8,128]{1,0:T(8,128)S(1)}, f32[8,128]{1,0:T(8,128)S(1)}, u32[]{:S(2)}, u32[]{:S(2)}) collective-permute-start(f32[8,128]{1,0:T(8,128)S(1)} %pad_maximum_fusion.1), channel_id=1, source_target_pairs={{1,0},{2,1},{3,2},{5,4},{6,5},{7,6},{9,8},{10,9},{11,10},{13,12},{... | collective-permute-start | bytes 12296 | tf_op jit(solution)/shard_map/ppermute | solution.py:28
  73.9 8.3 %collective-permute-start.7 = (f32[8,128]{1,0:T(8,128)S(1)}, f32[8,128]{1,0:T(8,128)S(1)}, u32[]{:S(2)}, u32[]{:S(2)}) collective-permute-start(f32[8,128]{1,0:T(8,128)S(1)} %pad_maximum_fusion), channel_id=1, source_target_pairs={{0,1},{1,2},{2,3},{4,5},{5,6},{6,7},{8,9},{9,10},{10,11},{12,13},{... | collective-permute-start | bytes 12296 | tf_op jit(solution)/shard_map/ppermute | solution.py:28
  82.1 6.8 %copy-start.8 = (s32[2]{0:T(128)S(1)}, s32[2]{0:T(128)}, u32[]{:S(2)}) copy-start(s32[2]{0:T(128)} %len_ref.1) | copy-start | bytes 28
  85.7 3.1 %collective-permute-start.11 = (f32[8,144]{1,0:T(8,128)S(1)}, f32[8,144]{1,0:T(8,128)S(1)}, u32[]{:S(2)}, u32[]{:S(2)}) collective-permute-start(f32[8,144]{1,0:T(8,128)S(1)} %get-tuple-element.35), channel_id=1, source_target_pairs={{0,4},{4,0},{8,12},{12,8},{1,5},{5,1},{9,13},{13,9},{2,6},{6,2},{1... | collective-permute-start | bytes 13832 | tf_op jit(solution)/shard_map/ppermute | solution.py:28
  85.8 3.2 %collective-permute-start.12 = (f32[8,144]{1,0:T(8,128)S(1)}, f32[8,144]{1,0:T(8,128)S(1)}, u32[]{:S(2)}, u32[]{:S(2)}) collective-permute-start(f32[8,144]{1,0:T(8,128)S(1)} %get-tuple-element.36), channel_id=1, source_target_pairs={{4,8},{12,0},{8,4},{0,12},{5,9},{13,1},{9,5},{1,13},{6,10},{14,2},... | collective-permute-start | bytes 13832 | tf_op jit(solution)/shard_map/ppermute | solution.py:28
  92.5 1.2 %collective-permute-start.13 = (f32[2,32]{1,0:T(2,128)S(1)}, f32[2,32]{1,0:T(2,128)S(1)}, u32[]{:S(2)}, u32[]{:S(2)}) collective-permute-start(f32[2,32]{1,0:T(2,128)S(1)} %get-tuple-element.43), channel_id=1, source_target_pairs={{0,4},{4,0},{8,12},{12,8},{1,5},{5,1},{9,13},{13,9},{2,6},{6,2},{1... | collective-permute-start | bytes 776 | tf_op jit(solution)/shard_map/ppermute | solution.py:28
  93.7 3.1 %collective-permute-start.14 = (f32[2,2,32]{2,1,0:T(2,128)S(1)}, f32[2,2,32]{2,1,0:T(2,128)S(1)}, u32[]{:S(2)}, u32[]{:S(2)}) collective-permute-start(f32[2,2,32]{2,1,0:T(2,128)S(1)} %maximum_select_fusion), channel_id=1, source_target_pairs={{0,5},{1,4},{2,7},{3,6},{4,1},{5,0},{6,3},{7,2},{8,13},{9,12},{10,... | collective-permute-start | bytes 1544 | tf_op jit(solution)/shard_map/ppermute | solution.py:28
  96.8 4.0 %collective-permute-start.15 = (f32[2,2,32]{2,1,0:T(2,128)S(1)}, f32[2,2,32]{2,1,0:T(2,128)S(1)}, u32[]{:S(2)}, u32[]{:S(2)}) collective-permute-start(f32[2,2,32]{2,1,0:T(2,128)S(1)} %fusion.3), channel_id=1, source_target_pairs={{0,6},{1,7},{2,4},{3,5},{4,2},{5,3},{6,0},{7,1},{8,14},{9,15},{10,... | collective-permute-start | bytes 1544 | tf_op jit(solution)/shard_map/ppermute | solution.py:28
  101.0 3.1 %collective-permute-start.16 = (f32[2]{0:T(128)S(1)}, f32[2]{0:T(128)S(1)}, u32[]{:S(2)}, u32[]{:S(2)}) collective-permute-start(f32[2]{0:T(128)S(1)} %select_reduce_fusion), channel_id=1, source_target_pairs={{0,12},{1,13},{2,14},{3,15},{4,8},{5,9},{6,10},{7,11},{8,4},{9,5},... | collective-permute-start | bytes 32 | tf_op jit(solution)/shard_map/ppermute | solution.py:28
  (2 other events, 1.3 us)

commit v6 on v4

--- a/solution.py
+++ b/solution.py
@@ -267,37 +267,56 @@
     return early + ends, rest + whole
 
 
-def convolve(sims_ref, first_ref, weights, scratch, score_ref, pos_ref, block, limits, padding, tiles):
-    w1_ref, b1_ref, w2_ref, b2_ref, w3_ref, b3_ref, w4_ref, b4_ref = weights
-    y_ref, lhs2_ref, second_ref, lhs3_ref = scratch
-    jf, js, jt = padding
-    first_map(sims_ref, w1_ref, b1_ref, y_ref, first_ref, pos_ref, block, limits, tiles)
+def second_map(first_ref, w2_ref, b2_ref, lhs_ref, second_ref, pos_ref, block, limits, tiles):
+    jf = first_ref.shape[1]
     lane = lax.broadcasted_iota(jnp.int32, (jf, 128), 1)
-
     upper = lane < 64
     left = (lane // 32) % 2 == 0
-    rows2 = block + 2
-    for at in range(rows2):
-        centre = first_ref[at + 1, 0:jf, :]
-        across = jnp.where(upper, first_ref[at + 2, 0:jf, :], first_ref[at, 0:jf, :])
-        row = slice(at * js, (at + 1) * js)
+    start, spots = 0, []
+    for at, first, size in tiles:
+        centre = first_ref[at + 1]
+        across = jnp.where(upper, first_ref[at + 2], first_ref[at])
+        row, cells = slice(start, start + size), slice(first, first + size)
         for index, value in enumerate((centre, across)):
             here = pltpu.roll(value, jf - 1, 0)
             beside = jnp.where(left, pltpu.roll(value, jf - 2, 0), value)
-            lhs2_ref[row, index * 256 : index * 256 + 128] = here[0:js].astype(BF)
-            lhs2_ref[row, index * 256 + 128 : index * 256 + 256] = beside[0:js].astype(BF)
-    result = jnp.dot(lhs2_ref[0 : rows2 * js, :], w2_ref[...], preferred_element_type=F32)
+            lhs_ref[row, index * 256 : index * 256 + 128] = here[cells].astype(BF)
+            lhs_ref[row, index * 256 + 128 : index * 256 + 256] = beside[cells].astype(BF)
+        spots.append(start)
+        start += size
+    result = jnp.dot(lhs_ref[0:start, :], w2_ref[...], preferred_element_type=F32)
     pooled = jnp.maximum(result[:, 0:128], result[:, 128:256])
     pooled = jnp.maximum(pooled, pltpu.roll(pooled, 64, 1))
     pooled = jnp.maximum(pooled + b2_ref[...], 0.0)
-    keep_cols = inside_columns(pos_ref, block, limits, js, 1)
-    for at in range(rows2):
-        keep = keep_cols * inside_rows(pos_ref, block, limits, at - 1)
-        second_ref[at, 0:js, :] = (pooled[at * js : (at + 1) * js] * keep).astype(BF).astype(F32)
-        if js < jt + 8:
-            second_ref[at, js : jt + 8, :] = jnp.zeros((jt + 8 - js, 128), F32)
-
-    upper = upper[0:jt]
+    keep_cols = inside_columns(pos_ref, block, limits, second_ref.shape[1], 1)
+    for (at, first, size), spot in zip(tiles, spots):
+        cells = slice(first, first + size)
+        keep = keep_cols[cells] * inside_rows(pos_ref, block, limits, at - 1)
+        second_ref[at, cells, :] = (pooled[spot : spot + size] * keep).astype(BF).astype(F32)
+
+
+def second_tiles(block, js, late, split):
+    early, rest, whole = [], [], []
+    for at in range(block + 2):
+        if split and GROUP <= at < block + 2 - GROUP:
+            early += [(at, 0, late - PIECE), (at, late + 2 * PIECE, js - late - 2 * PIECE)]
+            rest += [(at, late - PIECE, 3 * PIECE)]
+        else:
+            whole += [(at, 0, js)]
+    return early, rest + whole
+
+
+def convolve(
+    sims_ref, maps, weights, scratch, score_ref, pos_ref, block, limits, padding, tiles
+):
+    w1_ref, b1_ref, w2_ref, b2_ref, w3_ref, b3_ref, w4_ref, b4_ref = weights
+    first_ref, second_ref = maps
+    y_ref, lhs2_ref, lhs3_ref = scratch
+    _, _, jt = padding
+    first_map(sims_ref, w1_ref, b1_ref, y_ref, first_ref, pos_ref, block, limits, tiles[0])
+    second_map(first_ref, w2_ref, b2_ref, lhs2_ref, second_ref, pos_ref, block, limits, tiles[1])
+
+    upper = lax.broadcasted_iota(jnp.int32, (jt, 128), 1) < 64
     for at in range(block // 2):
         row = slice(at * jt, (at + 1) * jt)
         rows = [second_ref.at[2 * at + down] for down in range(4)]
@@ -325,11 +344,10 @@
 
 
 def convolve_scratch(block, padding, tiles):
-    _, js, jt = padding
+    _, _, jt = padding
     return [
-        pltpu.VMEM((sum(size for _, _, size in tiles), 256), BF),
-        pltpu.VMEM(((block + 2) * js, 512), BF),
-        pltpu.VMEM((block + 2, max(js, jt + 8), 128), F32),
+        pltpu.VMEM((sum(size for _, _, size in tiles[0]), 256), BF),
+        pltpu.VMEM((sum(size for _, _, size in tiles[1]), 512), BF),
         pltpu.VMEM((block // 2 * jt, 768), BF),
     ]
 
@@ -355,25 +373,33 @@
 
 
 def assemble_kernel(segments, tiles, block, limits, pos_ref, *refs):
-    sources, (w1_ref, b1_ref, sims_ref, first_ref, y_ref) = refs[:-5], refs[-5:]
+    sources, refs = refs[:-9], refs[-9:]
+    w1_ref, b1_ref, w2_ref, b2_ref, sims_ref, first_ref, second_ref, y_ref, lhs_ref = refs
     sims_ref[...] = jnp.zeros_like(sims_ref)
     place(pos_ref, sims_ref, sources, segments)
-    first_map(sims_ref, w1_ref, b1_ref, y_ref, first_ref, pos_ref, block, limits, tiles)
+    first_map(sims_ref, w1_ref, b1_ref, y_ref, first_ref, pos_ref, block, limits, tiles[0])
+    if tiles[1]:
+        second_map(first_ref, w2_ref, b2_ref, lhs_ref, second_ref, pos_ref, block, limits, tiles[1])
 
 
 def assembled(position, sources, segments, weights, tiles, block, limits):
     smem = pl.BlockSpec(memory_space=pltpu.SMEM)
     vmem = pl.BlockSpec(memory_space=pltpu.VMEM)
     frames = sources[0].shape[1]
+    jf, js, jt = pad_cells(block)
     return pl.pallas_call(
         functools.partial(assemble_kernel, segments, tiles, block, limits),
-        in_specs=[smem] + [vmem for _ in sources] + [vmem, vmem],
-        out_specs=[vmem, vmem],
+        in_specs=[smem] + [vmem for _ in sources] + [vmem] * 4,
+        out_specs=[vmem] * 3,
         out_shape=[
             jax.ShapeDtypeStruct((PHASES, block + 24, 2 * frames), F32),
-            jax.ShapeDtypeStruct((block + 2 * HALO, pad_cells(block)[0], 128), F32),
+            jax.ShapeDtypeStruct((block + 2 * HALO, jf, 128), F32),
+            jax.ShapeDtypeStruct((block + 2, max(js, jt + 8), 128), F32),
         ],
-        scratch_shapes=[pltpu.VMEM((sum(size for _, _, size in tiles), 256), BF)],
+        scratch_shapes=[
+            pltpu.VMEM((max(8, sum(size for _, _, size in part)), lanes), BF)
+            for part, lanes in zip(tiles, (256, 512))
+        ],
         compiler_params=pltpu.CompilerParams(vmem_limit_bytes=GRANT),
         cost_estimate=pl.CostEstimate(
             flops=1_000_000_000, bytes_accessed=500_000, transcendentals=0
@@ -383,8 +409,9 @@
 
 
 def network_kernel(limits, padding, starts, segments, tiles, pos_ref, len_ref, *refs):
-    (_, _, late_ref, core_ref, chip_ref), refs = refs[:5], refs[5:]
-    weights, (score_ref, peak_ref, sims_ref, first_ref), scratch = refs[:8], refs[8:12], refs[12:]
+    (_, _, _, late_ref, core_ref, chip_ref), refs = refs[:6], refs[6:]
+    weights, outs, scratch = refs[:8], refs[8:13], refs[13:]
+    score_ref, peak_ref, sims_ref, *maps = outs
     block = score_ref.shape[0]
     last = len(starts) - 1
     place(
@@ -403,7 +430,7 @@
     pl.when(pos_ref[0] % 2 == 0)(lambda: edges(below, above))
     pl.when(pos_ref[0] % 2 == 1)(lambda: edges(above, below))
     convolve(
-        sims_ref, first_ref, weights, scratch, score_ref, pos_ref, block, limits, padding, tiles
+        sims_ref, maps, weights, scratch, score_ref, pos_ref, block, limits, padding, tiles
     )
 
     score = score_ref[...]
@@ -422,24 +449,23 @@
 
 
 def network(
-    position, lengths, base, first, late, edges, starts, segments, tiles, weights, block, limits
+    position, lengths, maps, late, edges, starts, segments, tiles, weights, block, limits
 ):
     smem = pl.BlockSpec(memory_space=pltpu.SMEM)
     vmem = pl.BlockSpec(memory_space=pltpu.VMEM)
     padding = pad_cells(block)
-    arrays = [base, first, late, *edges]
+    arrays = [*maps, late, *edges]
     score, peaks, *_ = pl.pallas_call(
         functools.partial(network_kernel, limits, padding, starts, segments, tiles),
         in_specs=[smem, smem] + [vmem] * len(arrays) + [vmem] * 7 + [smem],
-        out_specs=[vmem] * 4,
+        out_specs=[vmem] * 5,
         out_shape=[
             jax.ShapeDtypeStruct((block, block), F32),
             jax.ShapeDtypeStruct((lengths.shape[0], block), F32),
-            jax.ShapeDtypeStruct(base.shape, F32),
-            jax.ShapeDtypeStruct(first.shape, F32),
+            *[jax.ShapeDtypeStruct(array.shape, F32) for array in maps],
         ],
         scratch_shapes=convolve_scratch(block, padding, tiles),
-        input_output_aliases={2: 2, 3: 3},
+        input_output_aliases={2: 2, 3: 3, 4: 4},
         cost_estimate=pl.CostEstimate(
             flops=6_000_000_000, bytes_accessed=4_000_000, transcendentals=0
         ),
@@ -658,11 +684,16 @@
     for edge, cell in ((left, -HALO), (right, block)):
         segments += [(len(sources), HALO * k, HALO, k, cell) for k in range(PHASES)]
         sources.append(edge)
-    jf = pad_cells(block)[0]
-    ready, tiles = first_tiles(block, frames, jf, late * PIECE if split else 2 * PIECE)
-    base, first = assembled(position, sources, segments, weights[:2], ready, block, limits)
+    jf, js, _ = pad_cells(block)
+    spot = late * PIECE if split else 2 * PIECE
+    firsts = first_tiles(block, frames, jf, spot)
+    seconds = second_tiles(block, js, spot, split)
+    maps = assembled(
+        position, sources, segments, weights[:4], (firsts[0], seconds[0]), block, limits
+    )
     if not split:
-        tiles = first_tiles(block, 0, jf, 2 * PIECE)[1]
+        firsts = first_tiles(block, 0, jf, spot)
+    tiles = (firsts[1], seconds[1])
     if split:
         for half in range(2):
             segments.append((len(sources), PIECE * half, PIECE, 2 + half, late * PIECE))
@@ -680,8 +711,7 @@
     score_map, peaks = network(
         position,
         lengths,
-        base,
-        first,
+        maps,
         done,
         (core, chip),
         starts,

time: 104 us -> 104 us (level)
  transfers between devices with their start and end apart: 17 -> 17, of which waited for: 9 -> 8; matrix products, arithmetic and copies ran while one was open for 0% -> 0% of each run, Pallas kernels for 27% -> 27%
where the time goes in v6:
time: 104 us; the launch traced here: 103 us
  waiting for transfers between devices  39.7 us (38%)
  Pallas kernels  35.6 us (34%)
  starting transfers between devices  19.1 us (18%)
  local copies, waits for them, and re-layouts  5.89 us (6%)
  between operations  2.15 us (2%)
    ppermute x17, waiting for transfers between devices, shift(): return lax.ppermute(array, axis, pairs)  39.7 us
    pallas_call x5, Pallas kernels, similarities(): pl.pallas_call(functools.partial(sims_kernel, scale, spans, len(done), fe...  24.1 us
    ppermute x17, starting transfers between devices, shift(): return lax.ppermute(array, axis, pairs)  19.1 us
    unnamed x18, local copies, waits for them, and re-layouts  5.79 us
    pallas_call x2, Pallas kernels, cut(): pl.pallas_call(functools.partial(cut_kernel, order), in_specs=[pl.BlockSp...  3.49 us
    pallas_call x1, Pallas kernels, network(): pl.pallas_call(functools.partial(network_kernel, limits, padding, starts,...  3.45 us
    pallas_call x1, Pallas kernels, network_weights(): pl.pallas_call(weights_kernel, out_shape=[jax.ShapeDtypeStruct(shape, dty...  3.09 us
  transfers between devices with their start and end apart: 17, of which 8 were waited for; matrix products, arithmetic and copies ran while one was open for 0% of the time, Pallas kernels for 27%

profile of v6, /device:TPU:0, one launch (start us, length us, event | category | flops | bytes accessed | tf_op | source)
XLA Modules:
  0.0 103.2 jit_solution(10824210581867863136)
XLA Ops:
  0.6 1.1 %cut.2 = bf16[9,8,3840]{2,1,0:T(8,128)(2,1)S(1)} custom-call(bf16[9,32,3840]{2,1,0:T(8,128)(2,1)} %bitcast.42), custom_call_target="tpu_custom_call" | custom-call | bytes 4423680 | tf_op jit(solution)/shard_map/cut/pallas_call | solution.py:46
  2.3 2.6 %collective-permute-start.1 = (bf16[72,3840]{1,0:T(8,128)(2,1)S(1)}, bf16[72,3840]{1,0:T(8,128)(2,1)S(1)}, u32[]{:S(2)}, u32[]{:S(2)}) collective-permute-start(bf16[72,3840]{1,0:T(8,128)(2,1)S(1)} %bitcast.32), channel_id=1, source_target_pairs={{0,8},{4,12},{8,0},{12,4},{1,9},{5,13},{9,1},{13,5},{2,10},{6,14},... | collective-permute-start | bytes 1658888 | tf_op jit(solution)/shard_map/ppermute | solution.py:28
  4.8 2.4 %cut.3 = (bf16[9,8,3840]{2,1,0:T(8,128)(2,1)}, bf16[9,8,3840]{2,1,0:T(8,128)(2,1)}, bf16[9,8,3840]{2,1,0:T(8,128)(2,1)S(1)}) custom-call(bf16[9,32,3840]{2,1,0:T(8,128)(2,1)} %bitcast.44), custom_call_target="tpu_custom_call" | custom-call | bytes 4423680 | tf_op jit(solution)/shard_map/cut/pallas_call | solution.py:46
  7.3 2.0 %collective-permute-start.5 = (bf16[72,3840]{1,0:T(8,128)(2,1)}, bf16[72,3840]{1,0:T(8,128)(2,1)S(1)}, u32[]{:S(2)}, u32[]{:S(2)}) collective-permute-start(bf16[72,3840]{1,0:T(8,128)(2,1)} %bitcast.19), channel_id=1, source_target_pairs={{0,8},{4,12},{8,0},{12,4},{1,9},{5,13},{9,1},{13,5},{2,10},{6,14},... | collective-permute-start | bytes 1658888 | tf_op jit(solution)/shard_map/ppermute | solution.py:28
  9.4 8.8 %collective-permute-done.1.refs_0_ = bf16[72,3840]{1,0:T(8,128)(2,1)S(1)} collective-permute-done((bf16[72,3840]{1,0:T(8,128)(2,1)S(1)}, bf16[72,3840]{1,0:T(8,128)(2,1)S(1)}, u32[]{:S(2)}, u32[]{:S(2)}) %collective-permute-start.1) | collective-permute-done | bytes 552992 | tf_op jit(solution)/shard_map/ppermute | solution.py:28
  24.1 3.1 %weights.1 = (bf16[256,1536]{1,0:T(8,128)(2,1)S(1)}, f32[1,128]{1,0:T(1,128)S(1)}, bf16[512,256]{1,0:T(8,128)(2,1)S(1)}, f32[1,128]{1,0:T(1,128)S(1)}, bf16[768,...) custom-call(f32[3,3,32]{2,1,0:T(4,128)S(1)} %copy-done.3, f32[1,32]{1,0:T(1,128)S(1)} %bitcast.38, ...), custom_call_target="tpu_custom_call" | custom-call | flops 100000000 | bytes 4000000 | tf_op jit(solution)/shard_map/weights/pallas_call | solution.py:545
  27.2 2.9 %collective-permute-done.3.refs_0_ = bf16[72,3840]{1,0:T(8,128)(2,1)S(1)} collective-permute-done((bf16[72,3840]{1,0:T(8,128)(2,1)}, bf16[72,3840]{1,0:T(8,128)(2,1)S(1)}, u32[]{:S(2)}, u32[]{:S(2)}) %collective-permute-start.3) | collective-permute-done | bytes 552992 | tf_op jit(solution)/shard_map/ppermute | solution.py:28
  30.1 11.8 %collective-permute-done.5.refs_0_ = bf16[72,3840]{1,0:T(8,128)(2,1)S(1)} collective-permute-done((bf16[72,3840]{1,0:T(8,128)(2,1)}, bf16[72,3840]{1,0:T(8,128)(2,1)S(1)}, u32[]{:S(2)}, u32[]{:S(2)}) %collective-permute-start.5) | collective-permute-done | bytes 552992 | tf_op jit(solution)/shard_map/ppermute | solution.py:28
  41.9 11.6 %collective-permute-done.9.refs_0_ = bf16[72,3840]{1,0:T(8,128)(2,1)S(1)} collective-permute-done((bf16[72,3840]{1,0:T(8,128)(2,1)S(1)}, bf16[72,3840]{1,0:T(8,128)(2,1)S(1)}, u32[]{:S(2)}, u32[]{:S(2)}) %collective-permute-start.9) | collective-permute-done | bytes 552992 | tf_op jit(solution)/shard_map/ppermute | solution.py:28
  54.2 11.3 %similarities.5 = (f32[64,128]{1,0:T(8,128)S(1)}, bf16[9,128,3840]{2,1,0:T(8,128)(2,1)S(1)}) custom-call(s32[14]{0:T(128)S(1)} %stack.67.pos_ref, s32[4,4]{1,0:T(4,128)S(1)} %copy-done, bf16[9,128,3840]{2,1,0:T(8,128)(2,1)} %bitcast.48, bf16[288,3840]{1,0:T(8,128)(2,1)} %bitcast.45, bf16[288,3840]{1,0:T(8,128)(2,1)} %collective-permute-done.refs_1_), custom_call_target="tpu_custom_call" | custom-call | flops 5096079360 | bytes 4423680 | tf_op jit(solution)/shard_map/similarities/pallas_call | solution.py:173
  65.5 3.2 %similarities.6.refs_1_.refs_3_ = f32[16,128]{1,0:T(8,128)S(1)} custom-call(s32[14]{0:T(128)S(1)} %stack.67.pos_ref, s32[4,4]{1,0:T(4,128)S(1)} %copy-done, bf16[9,128,3840]{2,1,0:T(8,128)(2,1)S(1)} %get-tuple-element.26.query_ref, bf16[72,3840]{1,0:T(8,128)(2,1)S(1)} %collective-permute-done.1.refs_0_, bf16[72,3840]{1,0:T(8,128)(2,1)S(1)} %collective-permute-done.2.refs_1_), custom_call_target="tpu_custom_call" | custom-call | flops 1274019840 | bytes 1105920 | tf_op jit(solution)/shard_map/similarities/pallas_call | solution.py:173
  68.7 1.3 %collective-permute-start.8 = (f32[8,128]{1,0:T(8,128)S(1)}, f32[8,128]{1,0:T(8,128)S(1)}, u32[]{:S(2)}, u32[]{:S(2)}) collective-permute-start(f32[8,128]{1,0:T(8,128)S(1)} %pad_maximum_fusion.1), channel_id=1, source_target_pairs={{1,0},{2,1},{3,2},{5,4},{6,5},{7,6},{9,8},{10,9},{11,10},{13,12},{... | collective-permute-start | bytes 12296 | tf_op jit(solution)/shard_map/ppermute | solution.py:28
  70.0 3.2 %similarities.7.refs_2_.refs_4_ = f32[16,128]{1,0:T(8,128)S(1)} custom-call(s32[14]{0:T(128)S(1)} %stack.67.pos_ref, s32[4,4]{1,0:T(4,128)S(1)} %copy-done, bf16[9,128,3840]{2,1,0:T(8,128)(2,1)S(1)} %get-tuple-element.26.query_ref, bf16[72,3840]{1,0:T(8,128)(2,1)S(1)} %collective-permute-done.3.refs_0_, bf16[72,3840]{1,0:T(8,128)(2,1)S(1)} %collective-permute-done.4.refs_1_), custom_call_target="tpu_custom_call" | custom-call | flops 1274019840 | bytes 1105920 | tf_op jit(solution)/shard_map/similarities/pallas_call | solution.py:173
  73.2 4.7 %collective-permute-start.7 = (f32[8,128]{1,0:T(8,128)S(1)}, f32[8,128]{1,0:T(8,128)S(1)}, u32[]{:S(2)}, u32[]{:S(2)}) collective-permute-start(f32[8,128]{1,0:T(8,128)S(1)} %pad_maximum_fusion), channel_id=1, source_target_pairs={{0,1},{1,2},{2,3},{4,5},{5,6},{6,7},{8,9},{9,10},{10,11},{12,13},{... | collective-permute-start | bytes 12296 | tf_op jit(solution)/shard_map/ppermute | solution.py:28
  78.0 3.2 %similarities.8.refs_3_.refs_5_ = f32[16,128]{1,0:T(8,128)S(1)} custom-call(s32[14]{0:T(128)S(1)} %stack.67.pos_ref, s32[4,4]{1,0:T(4,128)S(1)} %copy-done, bf16[9,128,3840]{2,1,0:T(8,128)(2,1)S(1)} %get-tuple-element.26.query_ref, bf16[72,3840]{1,0:T(8,128)(2,1)S(1)} %collective-permute-done.5.refs_0_, bf16[72,3840]{1,0:T(8,128)(2,1)S(1)} %collective-permute-done.6.refs_1_), custom_call_target="tpu_custom_call" | custom-call | flops 1274019840 | bytes 1105920 | tf_op jit(solution)/shard_map/similarities/pallas_call | solution.py:173
  81.2 3.2 %similarities.9 = (f32[16,128]{1,0:T(8,128)S(1)}, f32[8,144]{1,0:T(8,128)S(1)}, f32[8,144]{1,0:T(8,128)S(1)}) custom-call(s32[14]{0:T(128)S(1)} %stack.67.pos_ref, s32[4,4]{1,0:T(4,128)S(1)} %copy-done, bf16[9,128,3840]{2,1,0:T(8,128)(2,1)S(1)} %get-tuple-element.26.query_ref, bf16[72,3840]{1,0:T(8,128)(2,1)S(1)} %collective-permute-done.9.refs_0_, ...), custom_call_target="tpu_custom_call" | custom-call | flops 1274019840 | bytes 1105920 | tf_op jit(solution)/shard_map/similarities/pallas_call | solution.py:173
  84.5 1.8 %collective-permute-start.12 = (f32[8,144]{1,0:T(8,128)S(1)}, f32[8,144]{1,0:T(8,128)S(1)}, u32[]{:S(2)}, u32[]{:S(2)}) collective-permute-start(f32[8,144]{1,0:T(8,128)S(1)} %get-tuple-element.40), channel_id=1, source_target_pairs={{4,8},{12,0},{8,4},{0,12},{5,9},{13,1},{9,5},{1,13},{6,10},{14,2},... | collective-permute-start | bytes 13832 | tf_op jit(solution)/shard_map/ppermute | solution.py:28
  86.3 1.5 %assemble.1 = (f32[4,56,256]{2,1,0:T(8,128)S(1)}, f32[36,40,128]{2,1,0:T(8,128)S(1)}, f32[34,40,128]{2,1,0:T(8,128)S(1)}) custom-call(s32[14]{0:T(128)S(1)} %stack.67.pos_ref, f32[64,128]{1,0:T(8,128)S(1)} %get-tuple-element.25.refs_0_.refs_2_, f32[16,128]{1,0:T(8,128)S(1)} %similarities.6.refs_1_.refs_3_, f32[16,128]{1,0:T(8,128)S(1)} %similarities.7.refs_2_.refs_4_, ...), custom_call_target="tpu_custom_call" | custom-call | flops 1000000000 | bytes 500000 | tf_op jit(solution)/shard_map/assemble/pallas_call | solution.py:390
  87.9 3.5 %network.1 = (f32[32,32]{1,0:T(8,128)}, f32[2,32]{1,0:T(2,128)S(1)}, f32[4,56,256]{2,1,0:T(8,128)S(1)}, f32[36,40,128]{2,1,0:T(8,128)S(1)}, f32[34,40,128]{2,1,0:T(8,128)S(1)}) custom-call(s32[14]{0:T(128)S(1)} %stack.67.pos_ref, s32[2]{0:T(128)S(1)} %copy-done.8, ...), custom_call_target="tpu_custom_call", output_to_operand_aliasing={{2}: (2, {}), {3}: (3, {}), {4}: (4, {})} | custom-call | flops 6000000000 | bytes 4000000 | tf_op jit(solution)/shard_map/network/pallas_call | solution.py:458
  92.5 1.6 %collective-permute-start.14 = (f32[2,2,32]{2,1,0:T(2,128)S(1)}, f32[2,2,32]{2,1,0:T(2,128)S(1)}, u32[]{:S(2)}, u32[]{:S(2)}) collective-permute-start(f32[2,2,32]{2,1,0:T(2,128)S(1)} %maximum_select_fusion), channel_id=1, source_target_pairs={{0,5},{1,4},{2,7},{3,6},{4,1},{5,0},{6,3},{7,2},{8,13},{9,12},{10,... | collective-permute-start | bytes 1544 | tf_op jit(solution)/shard_map/ppermute | solution.py:28
  95.5 2.6 %collective-permute-start.15 = (f32[2,2,32]{2,1,0:T(2,128)S(1)}, f32[2,2,32]{2,1,0:T(2,128)S(1)}, u32[]{:S(2)}, u32[]{:S(2)}) collective-permute-start(f32[2,2,32]{2,1,0:T(2,128)S(1)} %fusion.3), channel_id=1, source_target_pairs={{0,6},{1,7},{2,4},{3,5},{4,2},{5,3},{6,0},{7,1},{8,14},{9,15},{10,... | collective-permute-start | bytes 1544 | tf_op jit(solution)/shard_map/ppermute | solution.py:28
  98.2 1.3 %collective-permute-done.15 = f32[2,2,32]{2,1,0:T(2,128)S(1)} collective-permute-done((f32[2,2,32]{2,1,0:T(2,128)S(1)}, f32[2,2,32]{2,1,0:T(2,128)S(1)}, u32[]{:S(2)}, u32[]{:S(2)}) %collective-permute-start.15) | collective-permute-done | bytes 544 | tf_op jit(solution)/shard_map/ppermute | solution.py:28
  99.6 1.5 %collective-permute-start.16 = (f32[2]{0:T(128)S(1)}, f32[2]{0:T(128)S(1)}, u32[]{:S(2)}, u32[]{:S(2)}) collective-permute-start(f32[2]{0:T(128)S(1)} %select_reduce_fusion), channel_id=1, source_target_pairs={{0,12},{1,13},{2,14},{3,15},{4,8},{5,9},{6,10},{7,11},{8,4},{9,5},... | collective-permute-start | bytes 32 | tf_op jit(solution)/shard_map/ppermute | solution.py:28
  101.1 1.5 %collective-permute-done.16 = f32[2]{0:T(128)S(1)} collective-permute-done((f32[2]{0:T(128)S(1)}, f32[2]{0:T(128)S(1)}, u32[]{:S(2)}, u32[]{:S(2)}) %collective-permute-start.16) | collective-permute-done | bytes 40 | tf_op jit(solution)/shard_map/ppermute | solution.py:28
  (49 shorter events, 9.3 us)
Async XLA Ops:
  1.7 51.8 %collective-permute-start = (bf16[288,3840]{1,0:T(8,128)(2,1)}, bf16[288,3840]{1,0:T(8,128)(2,1)}, u32[]{:S(2)}, u32[]{:S(2)}) collective-permute-start(bf16[288,3840]{1,0:T(8,128)(2,1)} %bitcast.43), channel_id=1, source_target_pairs={{0,4},{4,0},{8,12},{12,8},{1,5},{5,1},{9,13},{13,9},{2,6},{6,2},{1... | collective-permute-start | bytes 6635528 | tf_op jit(solution)/shard_map/ppermute | solution.py:28
  2.3 15.9 %collective-permute-start.1 = (bf16[72,3840]{1,0:T(8,128)(2,1)S(1)}, bf16[72,3840]{1,0:T(8,128)(2,1)S(1)}, u32[]{:S(2)}, u32[]{:S(2)}) collective-permute-start(bf16[72,3840]{1,0:T(8,128)(2,1)S(1)} %bitcast.32), channel_id=1, source_target_pairs={{0,8},{4,12},{8,0},{12,4},{1,9},{5,13},{9,1},{13,5},{2,10},{6,14},... | collective-permute-start | bytes 1658888 | tf_op jit(solution)/shard_map/ppermute | solution.py:28
  7.2 22.8 %collective-permute-start.3 = (bf16[72,3840]{1,0:T(8,128)(2,1)}, bf16[72,3840]{1,0:T(8,128)(2,1)S(1)}, u32[]{:S(2)}, u32[]{:S(2)}) collective-permute-start(bf16[72,3840]{1,0:T(8,128)(2,1)} %bitcast.18), channel_id=1, source_target_pairs={{0,8},{4,12},{8,0},{12,4},{1,9},{5,13},{9,1},{13,5},{2,10},{6,14},... | collective-permute-start | bytes 1658888 | tf_op jit(solution)/shard_map/ppermute | solution.py:28
  7.3 34.6 %collective-permute-start.5 = (bf16[72,3840]{1,0:T(8,128)(2,1)}, bf16[72,3840]{1,0:T(8,128)(2,1)S(1)}, u32[]{:S(2)}, u32[]{:S(2)}) collective-permute-start(bf16[72,3840]{1,0:T(8,128)(2,1)} %bitcast.19), channel_id=1, source_target_pairs={{0,8},{4,12},{8,0},{12,4},{1,9},{5,13},{9,1},{13,5},{2,10},{6,14},... | collective-permute-start | bytes 1658888 | tf_op jit(solution)/shard_map/ppermute | solution.py:28
  9.3 44.2 %collective-permute-start.9 = (bf16[72,3840]{1,0:T(8,128)(2,1)S(1)}, bf16[72,3840]{1,0:T(8,128)(2,1)S(1)}, u32[]{:S(2)}, u32[]{:S(2)}) collective-permute-start(bf16[72,3840]{1,0:T(8,128)(2,1)S(1)} %bitcast.35), channel_id=1, source_target_pairs={{0,8},{4,12},{8,0},{12,4},{1,9},{5,13},{9,1},{13,5},{2,10},{6,14},... | collective-permute-start | bytes 1658888 | tf_op jit(solution)/shard_map/ppermute | solution.py:28
  18.2 47.3 %collective-permute-start.2 = (bf16[72,3840]{1,0:T(8,128)(2,1)S(1)}, bf16[72,3840]{1,0:T(8,128)(2,1)S(1)}, u32[]{:S(2)}, u32[]{:S(2)}) collective-permute-start(bf16[72,3840]{1,0:T(8,128)(2,1)S(1)} %collective-permute-done.1.refs_0_), channel_id=1, source_target_pairs={{0,4},{4,0},{8,12},{12,8},{1,5},{5,1},{9,13},{13,9},{2,6},{6,2},{1... | collective-permute-start | bytes 1658888 | tf_op jit(solution)/shard_map/ppermute | solution.py:28
  19.0 0.9 copy-start.1
  19.9 0.9 copy-start.2
  20.8 0.7 copy-start.3
  21.4 0.7 copy-start.4
  22.1 0.7 copy-start.5
  30.1 40.0 %collective-permute-start.4 = (bf16[72,3840]{1,0:T(8,128)(2,1)S(1)}, bf16[72,3840]{1,0:T(8,128)(2,1)S(1)}, u32[]{:S(2)}, u32[]{:S(2)}) collective-permute-start(bf16[72,3840]{1,0:T(8,128)(2,1)S(1)} %collective-permute-done.3.refs_0_), channel_id=1, source_target_pairs={{0,4},{4,0},{8,12},{12,8},{1,5},{5,1},{9,13},{13,9},{2,6},{6,2},{1... | collective-permute-start | bytes 1658888 | tf_op jit(solution)/shard_map/ppermute | solution.py:28
  41.9 36.1 %collective-permute-start.6 = (bf16[72,3840]{1,0:T(8,128)(2,1)S(1)}, bf16[72,3840]{1,0:T(8,128)(2,1)S(1)}, u32[]{:S(2)}, u32[]{:S(2)}) collective-permute-start(bf16[72,3840]{1,0:T(8,128)(2,1)S(1)} %collective-permute-done.5.refs_0_), channel_id=1, source_target_pairs={{0,4},{4,0},{8,12},{12,8},{1,5},{5,1},{9,13},{13,9},{2,6},{6,2},{1... | collective-permute-start | bytes 1658888 | tf_op jit(solution)/shard_map/ppermute | solution.py:28
  53.5 27.7 %collective-permute-start.10 = (bf16[72,3840]{1,0:T(8,128)(2,1)S(1)}, bf16[72,3840]{1,0:T(8,128)(2,1)S(1)}, u32[]{:S(2)}, u32[]{:S(2)}) collective-permute-start(bf16[72,3840]{1,0:T(8,128)(2,1)S(1)} %collective-permute-done.9.refs_0_), channel_id=1, source_target_pairs={{0,4},{4,0},{8,12},{12,8},{1,5},{5,1},{9,13},{13,9},{2,6},{6,2},{1... | collective-permute-start | bytes 1658888 | tf_op jit(solution)/shard_map/ppermute | solution.py:28
  53.5 0.7 copy-start
  68.7 12.5 %collective-permute-start.8 = (f32[8,128]{1,0:T(8,128)S(1)}, f32[8,128]{1,0:T(8,128)S(1)}, u32[]{:S(2)}, u32[]{:S(2)}) collective-permute-start(f32[8,128]{1,0:T(8,128)S(1)} %pad_maximum_fusion.1), channel_id=1, source_target_pairs={{1,0},{2,1},{3,2},{5,4},{6,5},{7,6},{9,8},{10,9},{11,10},{13,12},{... | collective-permute-start | bytes 12296 | tf_op jit(solution)/shard_map/ppermute | solution.py:28
  73.2 8.0 %collective-permute-start.7 = (f32[8,128]{1,0:T(8,128)S(1)}, f32[8,128]{1,0:T(8,128)S(1)}, u32[]{:S(2)}, u32[]{:S(2)}) collective-permute-start(f32[8,128]{1,0:T(8,128)S(1)} %pad_maximum_fusion), channel_id=1, source_target_pairs={{0,1},{1,2},{2,3},{4,5},{5,6},{6,7},{8,9},{9,10},{10,11},{12,13},{... | collective-permute-start | bytes 12296 | tf_op jit(solution)/shard_map/ppermute | solution.py:28
  81.2 6.7 %copy-start.8 = (s32[2]{0:T(128)S(1)}, s32[2]{0:T(128)}, u32[]{:S(2)}) copy-start(s32[2]{0:T(128)} %len_ref.1) | copy-start | bytes 28
  84.5 3.4 %collective-permute-start.11 = (f32[8,144]{1,0:T(8,128)S(1)}, f32[8,144]{1,0:T(8,128)S(1)}, u32[]{:S(2)}, u32[]{:S(2)}) collective-permute-start(f32[8,144]{1,0:T(8,128)S(1)} %get-tuple-element.39), channel_id=1, source_target_pairs={{0,4},{4,0},{8,12},{12,8},{1,5},{5,1},{9,13},{13,9},{2,6},{6,2},{1... | collective-permute-start | bytes 13832 | tf_op jit(solution)/shard_map/ppermute | solution.py:28
  84.5 3.4 %collective-permute-start.12 = (f32[8,144]{1,0:T(8,128)S(1)}, f32[8,144]{1,0:T(8,128)S(1)}, u32[]{:S(2)}, u32[]{:S(2)}) collective-permute-start(f32[8,144]{1,0:T(8,128)S(1)} %get-tuple-element.40), channel_id=1, source_target_pairs={{4,8},{12,0},{8,4},{0,12},{5,9},{13,1},{9,5},{1,13},{6,10},{14,2},... | collective-permute-start | bytes 13832 | tf_op jit(solution)/shard_map/ppermute | solution.py:28
  91.3 1.2 %collective-permute-start.13 = (f32[2,32]{1,0:T(2,128)S(1)}, f32[2,32]{1,0:T(2,128)S(1)}, u32[]{:S(2)}, u32[]{:S(2)}) collective-permute-start(f32[2,32]{1,0:T(2,128)S(1)} %get-tuple-element.45), channel_id=1, source_target_pairs={{0,4},{4,0},{8,12},{12,8},{1,5},{5,1},{9,13},{13,9},{2,6},{6,2},{1... | collective-permute-start | bytes 776 | tf_op jit(solution)/shard_map/ppermute | solution.py:28
  92.5 3.0 %collective-permute-start.14 = (f32[2,2,32]{2,1,0:T(2,128)S(1)}, f32[2,2,32]{2,1,0:T(2,128)S(1)}, u32[]{:S(2)}, u32[]{:S(2)}) collective-permute-start(f32[2,2,32]{2,1,0:T(2,128)S(1)} %maximum_select_fusion), channel_id=1, source_target_pairs={{0,5},{1,4},{2,7},{3,6},{4,1},{5,0},{6,3},{7,2},{8,13},{9,12},{10,... | collective-permute-start | bytes 1544 | tf_op jit(solution)/shard_map/ppermute | solution.py:28
  95.5 3.9 %collective-permute-start.15 = (f32[2,2,32]{2,1,0:T(2,128)S(1)}, f32[2,2,32]{2,1,0:T(2,128)S(1)}, u32[]{:S(2)}, u32[]{:S(2)}) collective-permute-start(f32[2,2,32]{2,1,0:T(2,128)S(1)} %fusion.3), channel_id=1, source_target_pairs={{0,6},{1,7},{2,4},{3,5},{4,2},{5,3},{6,0},{7,1},{8,14},{9,15},{10,... | collective-permute-start | bytes 1544 | tf_op jit(solution)/shard_map/ppermute | solution.py:28
  99.6 3.1 %collective-permute-start.16 = (f32[2]{0:T(128)S(1)}, f32[2]{0:T(128)S(1)}, u32[]{:S(2)}, u32[]{:S(2)}) collective-permute-start(f32[2]{0:T(128)S(1)} %select_reduce_fusion), channel_id=1, source_target_pairs={{0,12},{1,13},{2,14},{3,15},{4,8},{5,9},{6,10},{7,11},{8,4},{9,5},... | collective-permute-start | bytes 32 | tf_op jit(solution)/shard_map/ppermute | solution.py:28
  (2 other events, 1.3 us)

commit v7 on v6

--- a/solution.py
+++ b/solution.py
@@ -31,9 +31,10 @@
 def cut_kernel(order, source_ref, *refs):
     outs, sems = refs[:-1], refs[-1]
     copies = []
-    for index, (at, out) in enumerate(zip(order, outs)):
-        piece = source_ref.at[:, pl.ds(at * PIECE, PIECE), :]
-        copies.append(pltpu.make_async_copy(piece, out, sems.at[index]))
+    for at, out in zip(order, outs):
+        for region in range(source_ref.shape[0]):
+            piece = source_ref.at[region, pl.ds(at * PIECE, PIECE), :]
+            copies.append(pltpu.make_async_copy(piece, out.at[region], sems.at[len(copies)]))
     for copy in copies:
         copy.start()
     for copy in copies:
@@ -48,7 +49,7 @@
         in_specs=[pl.BlockSpec(memory_space=pltpu.HBM)],
         out_specs=[pl.BlockSpec(memory_space=pltpu.VMEM) for _ in order],
         out_shape=[jax.ShapeDtypeStruct(shape, source.dtype) for _ in order],
-        scratch_shapes=[pltpu.SemaphoreType.DMA((len(order),))],
+        scratch_shapes=[pltpu.SemaphoreType.DMA((len(order) * regions,))],
         compiler_params=pltpu.CompilerParams(vmem_limit_bytes=GRANT),
         cost_estimate=pl.CostEstimate(
             flops=0, bytes_accessed=4 * source.size, transcendentals=0

time: 104 us -> 104 us (level)
  no operation moved by 1% of the time
where the time goes in v7:
time: 104 us; the launch traced here: 103 us
  waiting for transfers between devices  39.4 us (38%)
  Pallas kernels  35.9 us (35%)
  starting transfers between devices  19.1 us (18%)
  local copies, waits for them, and re-layouts  5.89 us (6%)
  between operations  2.15 us (2%)
    ppermute x17, waiting for transfers between devices, shift(): return lax.ppermute(array, axis, pairs)  39.4 us
    pallas_call x5, Pallas kernels, similarities(): pl.pallas_call(functools.partial(sims_kernel, scale, spans, len(done), fe...  24.1 us
    ppermute x17, starting transfers between devices, shift(): return lax.ppermute(array, axis, pairs)  19.1 us
    unnamed x18, local copies, waits for them, and re-layouts  5.79 us
    pallas_call x2, Pallas kernels, cut(): pl.pallas_call(functools.partial(cut_kernel, order), in_specs=[pl.BlockSp...  3.81 us
    pallas_call x1, Pallas kernels, network(): pl.pallas_call(functools.partial(network_kernel, limits, padding, starts,...  3.45 us
    pallas_call x1, Pallas kernels, network_weights(): pl.pallas_call(weights_kernel, out_shape=[jax.ShapeDtypeStruct(shape, dty...  3.09 us
  transfers between devices with their start and end apart: 17, of which 8 were waited for; matrix products, arithmetic and copies ran while one was open for 0% of the time, Pallas kernels for 27%

profile of v7, /device:TPU:0, one launch (start us, length us, event | category | flops | bytes accessed | tf_op | source)
XLA Modules:
  0.0 103.2 jit_solution(5632473303001653679)
XLA Ops:
  0.6 1.1 %cut.2 = bf16[9,8,3840]{2,1,0:T(8,128)(2,1)S(1)} custom-call(bf16[9,32,3840]{2,1,0:T(8,128)(2,1)} %bitcast.42), custom_call_target="tpu_custom_call" | custom-call | bytes 4423680 | tf_op jit(solution)/shard_map/cut/pallas_call | solution.py:47
  2.3 2.6 %collective-permute-start.1 = (bf16[72,3840]{1,0:T(8,128)(2,1)S(1)}, bf16[72,3840]{1,0:T(8,128)(2,1)S(1)}, u32[]{:S(2)}, u32[]{:S(2)}) collective-permute-start(bf16[72,3840]{1,0:T(8,128)(2,1)S(1)} %bitcast.32), channel_id=1, source_target_pairs={{0,8},{4,12},{8,0},{12,4},{1,9},{5,13},{9,1},{13,5},{2,10},{6,14},... | collective-permute-start | bytes 1658888 | tf_op jit(solution)/shard_map/ppermute | solution.py:28
  4.9 2.7 %cut.3 = (bf16[9,8,3840]{2,1,0:T(8,128)(2,1)}, bf16[9,8,3840]{2,1,0:T(8,128)(2,1)}, bf16[9,8,3840]{2,1,0:T(8,128)(2,1)S(1)}) custom-call(bf16[9,32,3840]{2,1,0:T(8,128)(2,1)} %bitcast.44), custom_call_target="tpu_custom_call" | custom-call | bytes 4423680 | tf_op jit(solution)/shard_map/cut/pallas_call | solution.py:47
  7.7 2.0 %collective-permute-start.5 = (bf16[72,3840]{1,0:T(8,128)(2,1)}, bf16[72,3840]{1,0:T(8,128)(2,1)S(1)}, u32[]{:S(2)}, u32[]{:S(2)}) collective-permute-start(bf16[72,3840]{1,0:T(8,128)(2,1)} %bitcast.19), channel_id=1, source_target_pairs={{0,8},{4,12},{8,0},{12,4},{1,9},{5,13},{9,1},{13,5},{2,10},{6,14},... | collective-permute-start | bytes 1658888 | tf_op jit(solution)/shard_map/ppermute | solution.py:28
  9.7 8.5 %collective-permute-done.1.refs_0_ = bf16[72,3840]{1,0:T(8,128)(2,1)S(1)} collective-permute-done((bf16[72,3840]{1,0:T(8,128)(2,1)S(1)}, bf16[72,3840]{1,0:T(8,128)(2,1)S(1)}, u32[]{:S(2)}, u32[]{:S(2)}) %collective-permute-start.1) | collective-permute-done | bytes 552992 | tf_op jit(solution)/shard_map/ppermute | solution.py:28
  24.2 3.1 %weights.1 = (bf16[256,1536]{1,0:T(8,128)(2,1)S(1)}, f32[1,128]{1,0:T(1,128)S(1)}, bf16[512,256]{1,0:T(8,128)(2,1)S(1)}, f32[1,128]{1,0:T(1,128)S(1)}, bf16[768,...) custom-call(f32[3,3,32]{2,1,0:T(4,128)S(1)} %copy-done.3, f32[1,32]{1,0:T(1,128)S(1)} %bitcast.38, ...), custom_call_target="tpu_custom_call" | custom-call | flops 100000000 | bytes 4000000 | tf_op jit(solution)/shard_map/weights/pallas_call | solution.py:546
  27.2 2.9 %collective-permute-done.3.refs_0_ = bf16[72,3840]{1,0:T(8,128)(2,1)S(1)} collective-permute-done((bf16[72,3840]{1,0:T(8,128)(2,1)}, bf16[72,3840]{1,0:T(8,128)(2,1)S(1)}, u32[]{:S(2)}, u32[]{:S(2)}) %collective-permute-start.3) | collective-permute-done | bytes 552992 | tf_op jit(solution)/shard_map/ppermute | solution.py:28
  30.1 11.8 %collective-permute-done.5.refs_0_ = bf16[72,3840]{1,0:T(8,128)(2,1)S(1)} collective-permute-done((bf16[72,3840]{1,0:T(8,128)(2,1)}, bf16[72,3840]{1,0:T(8,128)(2,1)S(1)}, u32[]{:S(2)}, u32[]{:S(2)}) %collective-permute-start.5) | collective-permute-done | bytes 552992 | tf_op jit(solution)/shard_map/ppermute | solution.py:28
  42.0 11.6 %collective-permute-done.9.refs_0_ = bf16[72,3840]{1,0:T(8,128)(2,1)S(1)} collective-permute-done((bf16[72,3840]{1,0:T(8,128)(2,1)S(1)}, bf16[72,3840]{1,0:T(8,128)(2,1)S(1)}, u32[]{:S(2)}, u32[]{:S(2)}) %collective-permute-start.9) | collective-permute-done | bytes 552992 | tf_op jit(solution)/shard_map/ppermute | solution.py:28
  54.3 11.3 %similarities.5 = (f32[64,128]{1,0:T(8,128)S(1)}, bf16[9,128,3840]{2,1,0:T(8,128)(2,1)S(1)}) custom-call(s32[14]{0:T(128)S(1)} %stack.67.pos_ref, s32[4,4]{1,0:T(4,128)S(1)} %copy-done, bf16[9,128,3840]{2,1,0:T(8,128)(2,1)} %bitcast.48, bf16[288,3840]{1,0:T(8,128)(2,1)} %bitcast.45, bf16[288,3840]{1,0:T(8,128)(2,1)} %collective-permute-done.refs_1_), custom_call_target="tpu_custom_call" | custom-call | flops 5096079360 | bytes 4423680 | tf_op jit(solution)/shard_map/similarities/pallas_call | solution.py:174
  65.5 3.2 %similarities.6.refs_1_.refs_3_ = f32[16,128]{1,0:T(8,128)S(1)} custom-call(s32[14]{0:T(128)S(1)} %stack.67.pos_ref, s32[4,4]{1,0:T(4,128)S(1)} %copy-done, bf16[9,128,3840]{2,1,0:T(8,128)(2,1)S(1)} %get-tuple-element.26.query_ref, bf16[72,3840]{1,0:T(8,128)(2,1)S(1)} %collective-permute-done.1.refs_0_, bf16[72,3840]{1,0:T(8,128)(2,1)S(1)} %collective-permute-done.2.refs_1_), custom_call_target="tpu_custom_call" | custom-call | flops 1274019840 | bytes 1105920 | tf_op jit(solution)/shard_map/similarities/pallas_call | solution.py:174
  68.8 1.3 %collective-permute-start.8 = (f32[8,128]{1,0:T(8,128)S(1)}, f32[8,128]{1,0:T(8,128)S(1)}, u32[]{:S(2)}, u32[]{:S(2)}) collective-permute-start(f32[8,128]{1,0:T(8,128)S(1)} %pad_maximum_fusion.1), channel_id=1, source_target_pairs={{1,0},{2,1},{3,2},{5,4},{6,5},{7,6},{9,8},{10,9},{11,10},{13,12},{... | collective-permute-start | bytes 12296 | tf_op jit(solution)/shard_map/ppermute | solution.py:28
  70.1 3.2 %similarities.7.refs_2_.refs_4_ = f32[16,128]{1,0:T(8,128)S(1)} custom-call(s32[14]{0:T(128)S(1)} %stack.67.pos_ref, s32[4,4]{1,0:T(4,128)S(1)} %copy-done, bf16[9,128,3840]{2,1,0:T(8,128)(2,1)S(1)} %get-tuple-element.26.query_ref, bf16[72,3840]{1,0:T(8,128)(2,1)S(1)} %collective-permute-done.3.refs_0_, bf16[72,3840]{1,0:T(8,128)(2,1)S(1)} %collective-permute-done.4.refs_1_), custom_call_target="tpu_custom_call" | custom-call | flops 1274019840 | bytes 1105920 | tf_op jit(solution)/shard_map/similarities/pallas_call | solution.py:174
  73.3 4.7 %collective-permute-start.7 = (f32[8,128]{1,0:T(8,128)S(1)}, f32[8,128]{1,0:T(8,128)S(1)}, u32[]{:S(2)}, u32[]{:S(2)}) collective-permute-start(f32[8,128]{1,0:T(8,128)S(1)} %pad_maximum_fusion), channel_id=1, source_target_pairs={{0,1},{1,2},{2,3},{4,5},{5,6},{6,7},{8,9},{9,10},{10,11},{12,13},{... | collective-permute-start | bytes 12296 | tf_op jit(solution)/shard_map/ppermute | solution.py:28
  78.1 3.2 %similarities.8.refs_3_.refs_5_ = f32[16,128]{1,0:T(8,128)S(1)} custom-call(s32[14]{0:T(128)S(1)} %stack.67.pos_ref, s32[4,4]{1,0:T(4,128)S(1)} %copy-done, bf16[9,128,3840]{2,1,0:T(8,128)(2,1)S(1)} %get-tuple-element.26.query_ref, bf16[72,3840]{1,0:T(8,128)(2,1)S(1)} %collective-permute-done.5.refs_0_, bf16[72,3840]{1,0:T(8,128)(2,1)S(1)} %collective-permute-done.6.refs_1_), custom_call_target="tpu_custom_call" | custom-call | flops 1274019840 | bytes 1105920 | tf_op jit(solution)/shard_map/similarities/pallas_call | solution.py:174
  81.3 3.2 %similarities.9 = (f32[16,128]{1,0:T(8,128)S(1)}, f32[8,144]{1,0:T(8,128)S(1)}, f32[8,144]{1,0:T(8,128)S(1)}) custom-call(s32[14]{0:T(128)S(1)} %stack.67.pos_ref, s32[4,4]{1,0:T(4,128)S(1)} %copy-done, bf16[9,128,3840]{2,1,0:T(8,128)(2,1)S(1)} %get-tuple-element.26.query_ref, bf16[72,3840]{1,0:T(8,128)(2,1)S(1)} %collective-permute-done.9.refs_0_, ...), custom_call_target="tpu_custom_call" | custom-call | flops 1274019840 | bytes 1105920 | tf_op jit(solution)/shard_map/similarities/pallas_call | solution.py:174
  84.6 1.8 %collective-permute-start.12 = (f32[8,144]{1,0:T(8,128)S(1)}, f32[8,144]{1,0:T(8,128)S(1)}, u32[]{:S(2)}, u32[]{:S(2)}) collective-permute-start(f32[8,144]{1,0:T(8,128)S(1)} %get-tuple-element.40), channel_id=1, source_target_pairs={{4,8},{12,0},{8,4},{0,12},{5,9},{13,1},{9,5},{1,13},{6,10},{14,2},... | collective-permute-start | bytes 13832 | tf_op jit(solution)/shard_map/ppermute | solution.py:28
  86.4 1.5 %assemble.1 = (f32[4,56,256]{2,1,0:T(8,128)S(1)}, f32[36,40,128]{2,1,0:T(8,128)S(1)}, f32[34,40,128]{2,1,0:T(8,128)S(1)}) custom-call(s32[14]{0:T(128)S(1)} %stack.67.pos_ref, f32[64,128]{1,0:T(8,128)S(1)} %get-tuple-element.25.refs_0_.refs_2_, f32[16,128]{1,0:T(8,128)S(1)} %similarities.6.refs_1_.refs_3_, f32[16,128]{1,0:T(8,128)S(1)} %similarities.7.refs_2_.refs_4_, ...), custom_call_target="tpu_custom_call" | custom-call | flops 1000000000 | bytes 500000 | tf_op jit(solution)/shard_map/assemble/pallas_call | solution.py:391
  88.0 3.5 %network.1 = (f32[32,32]{1,0:T(8,128)}, f32[2,32]{1,0:T(2,128)S(1)}, f32[4,56,256]{2,1,0:T(8,128)S(1)}, f32[36,40,128]{2,1,0:T(8,128)S(1)}, f32[34,40,128]{2,1,0:T(8,128)S(1)}) custom-call(s32[14]{0:T(128)S(1)} %stack.67.pos_ref, s32[2]{0:T(128)S(1)} %copy-done.8, ...), custom_call_target="tpu_custom_call", output_to_operand_aliasing={{2}: (2, {}), {3}: (3, {}), {4}: (4, {})} | custom-call | flops 6000000000 | bytes 4000000 | tf_op jit(solution)/shard_map/network/pallas_call | solution.py:459
  92.6 1.6 %collective-permute-start.14 = (f32[2,2,32]{2,1,0:T(2,128)S(1)}, f32[2,2,32]{2,1,0:T(2,128)S(1)}, u32[]{:S(2)}, u32[]{:S(2)}) collective-permute-start(f32[2,2,32]{2,1,0:T(2,128)S(1)} %maximum_select_fusion), channel_id=1, source_target_pairs={{0,5},{1,4},{2,7},{3,6},{4,1},{5,0},{6,3},{7,2},{8,13},{9,12},{10,... | collective-permute-start | bytes 1544 | tf_op jit(solution)/shard_map/ppermute | solution.py:28
  95.6 2.6 %collective-permute-start.15 = (f32[2,2,32]{2,1,0:T(2,128)S(1)}, f32[2,2,32]{2,1,0:T(2,128)S(1)}, u32[]{:S(2)}, u32[]{:S(2)}) collective-permute-start(f32[2,2,32]{2,1,0:T(2,128)S(1)} %fusion.3), channel_id=1, source_target_pairs={{0,6},{1,7},{2,4},{3,5},{4,2},{5,3},{6,0},{7,1},{8,14},{9,15},{10,... | collective-permute-start | bytes 1544 | tf_op jit(solution)/shard_map/ppermute | solution.py:28
  98.2 1.3 %collective-permute-done.15 = f32[2,2,32]{2,1,0:T(2,128)S(1)} collective-permute-done((f32[2,2,32]{2,1,0:T(2,128)S(1)}, f32[2,2,32]{2,1,0:T(2,128)S(1)}, u32[]{:S(2)}, u32[]{:S(2)}) %collective-permute-start.15) | collective-permute-done | bytes 544 | tf_op jit(solution)/shard_map/ppermute | solution.py:28
  99.7 1.6 %collective-permute-start.16 = (f32[2]{0:T(128)S(1)}, f32[2]{0:T(128)S(1)}, u32[]{:S(2)}, u32[]{:S(2)}) collective-permute-start(f32[2]{0:T(128)S(1)} %select_reduce_fusion), channel_id=1, source_target_pairs={{0,12},{1,13},{2,14},{3,15},{4,8},{5,9},{6,10},{7,11},{8,4},{9,5},... | collective-permute-start | bytes 32 | tf_op jit(solution)/shard_map/ppermute | solution.py:28
  101.2 1.5 %collective-permute-done.16 = f32[2]{0:T(128)S(1)} collective-permute-done((f32[2]{0:T(128)S(1)}, f32[2]{0:T(128)S(1)}, u32[]{:S(2)}, u32[]{:S(2)}) %collective-permute-start.16) | collective-permute-done | bytes 40 | tf_op jit(solution)/shard_map/ppermute | solution.py:28
  (49 shorter events, 9.3 us)
Async XLA Ops:
  1.8 51.8 %collective-permute-start = (bf16[288,3840]{1,0:T(8,128)(2,1)}, bf16[288,3840]{1,0:T(8,128)(2,1)}, u32[]{:S(2)}, u32[]{:S(2)}) collective-permute-start(bf16[288,3840]{1,0:T(8,128)(2,1)} %bitcast.43), channel_id=1, source_target_pairs={{0,4},{4,0},{8,12},{12,8},{1,5},{5,1},{9,13},{13,9},{2,6},{6,2},{1... | collective-permute-start | bytes 6635528 | tf_op jit(solution)/shard_map/ppermute | solution.py:28
  2.3 15.9 %collective-permute-start.1 = (bf16[72,3840]{1,0:T(8,128)(2,1)S(1)}, bf16[72,3840]{1,0:T(8,128)(2,1)S(1)}, u32[]{:S(2)}, u32[]{:S(2)}) collective-permute-start(bf16[72,3840]{1,0:T(8,128)(2,1)S(1)} %bitcast.32), channel_id=1, source_target_pairs={{0,8},{4,12},{8,0},{12,4},{1,9},{5,13},{9,1},{13,5},{2,10},{6,14},... | collective-permute-start | bytes 1658888 | tf_op jit(solution)/shard_map/ppermute | solution.py:28
  7.6 22.6 %collective-permute-start.3 = (bf16[72,3840]{1,0:T(8,128)(2,1)}, bf16[72,3840]{1,0:T(8,128)(2,1)S(1)}, u32[]{:S(2)}, u32[]{:S(2)}) collective-permute-start(bf16[72,3840]{1,0:T(8,128)(2,1)} %bitcast.18), channel_id=1, source_target_pairs={{0,8},{4,12},{8,0},{12,4},{1,9},{5,13},{9,1},{13,5},{2,10},{6,14},... | collective-permute-start | bytes 1658888 | tf_op jit(solution)/shard_map/ppermute | solution.py:28
  7.7 34.3 %collective-permute-start.5 = (bf16[72,3840]{1,0:T(8,128)(2,1)}, bf16[72,3840]{1,0:T(8,128)(2,1)S(1)}, u32[]{:S(2)}, u32[]{:S(2)}) collective-permute-start(bf16[72,3840]{1,0:T(8,128)(2,1)} %bitcast.19), channel_id=1, source_target_pairs={{0,8},{4,12},{8,0},{12,4},{1,9},{5,13},{9,1},{13,5},{2,10},{6,14},... | collective-permute-start | bytes 1658888 | tf_op jit(solution)/shard_map/ppermute | solution.py:28
  9.7 43.9 %collective-permute-start.9 = (bf16[72,3840]{1,0:T(8,128)(2,1)S(1)}, bf16[72,3840]{1,0:T(8,128)(2,1)S(1)}, u32[]{:S(2)}, u32[]{:S(2)}) collective-permute-start(bf16[72,3840]{1,0:T(8,128)(2,1)S(1)} %bitcast.35), channel_id=1, source_target_pairs={{0,8},{4,12},{8,0},{12,4},{1,9},{5,13},{9,1},{13,5},{2,10},{6,14},... | collective-permute-start | bytes 1658888 | tf_op jit(solution)/shard_map/ppermute | solution.py:28
  18.3 47.2 %collective-permute-start.2 = (bf16[72,3840]{1,0:T(8,128)(2,1)S(1)}, bf16[72,3840]{1,0:T(8,128)(2,1)S(1)}, u32[]{:S(2)}, u32[]{:S(2)}) collective-permute-start(bf16[72,3840]{1,0:T(8,128)(2,1)S(1)} %collective-permute-done.1.refs_0_), channel_id=1, source_target_pairs={{0,4},{4,0},{8,12},{12,8},{1,5},{5,1},{9,13},{13,9},{2,6},{6,2},{1... | collective-permute-start | bytes 1658888 | tf_op jit(solution)/shard_map/ppermute | solution.py:28
  19.0 0.9 copy-start.1
  20.0 0.9 copy-start.2
  20.8 0.7 copy-start.3
  21.5 0.7 copy-start.4
  22.2 0.7 copy-start.5
  30.1 39.9 %collective-permute-start.4 = (bf16[72,3840]{1,0:T(8,128)(2,1)S(1)}, bf16[72,3840]{1,0:T(8,128)(2,1)S(1)}, u32[]{:S(2)}, u32[]{:S(2)}) collective-permute-start(bf16[72,3840]{1,0:T(8,128)(2,1)S(1)} %collective-permute-done.3.refs_0_), channel_id=1, source_target_pairs={{0,4},{4,0},{8,12},{12,8},{1,5},{5,1},{9,13},{13,9},{2,6},{6,2},{1... | collective-permute-start | bytes 1658888 | tf_op jit(solution)/shard_map/ppermute | solution.py:28
  42.0 36.1 %collective-permute-start.6 = (bf16[72,3840]{1,0:T(8,128)(2,1)S(1)}, bf16[72,3840]{1,0:T(8,128)(2,1)S(1)}, u32[]{:S(2)}, u32[]{:S(2)}) collective-permute-start(bf16[72,3840]{1,0:T(8,128)(2,1)S(1)} %collective-permute-done.5.refs_0_), channel_id=1, source_target_pairs={{0,4},{4,0},{8,12},{12,8},{1,5},{5,1},{9,13},{13,9},{2,6},{6,2},{1... | collective-permute-start | bytes 1658888 | tf_op jit(solution)/shard_map/ppermute | solution.py:28
  53.6 27.7 %collective-permute-start.10 = (bf16[72,3840]{1,0:T(8,128)(2,1)S(1)}, bf16[72,3840]{1,0:T(8,128)(2,1)S(1)}, u32[]{:S(2)}, u32[]{:S(2)}) collective-permute-start(bf16[72,3840]{1,0:T(8,128)(2,1)S(1)} %collective-permute-done.9.refs_0_), channel_id=1, source_target_pairs={{0,4},{4,0},{8,12},{12,8},{1,5},{5,1},{9,13},{13,9},{2,6},{6,2},{1... | collective-permute-start | bytes 1658888 | tf_op jit(solution)/shard_map/ppermute | solution.py:28
  53.6 0.7 copy-start
  68.8 12.5 %collective-permute-start.8 = (f32[8,128]{1,0:T(8,128)S(1)}, f32[8,128]{1,0:T(8,128)S(1)}, u32[]{:S(2)}, u32[]{:S(2)}) collective-permute-start(f32[8,128]{1,0:T(8,128)S(1)} %pad_maximum_fusion.1), channel_id=1, source_target_pairs={{1,0},{2,1},{3,2},{5,4},{6,5},{7,6},{9,8},{10,9},{11,10},{13,12},{... | collective-permute-start | bytes 12296 | tf_op jit(solution)/shard_map/ppermute | solution.py:28
  73.3 8.0 %collective-permute-start.7 = (f32[8,128]{1,0:T(8,128)S(1)}, f32[8,128]{1,0:T(8,128)S(1)}, u32[]{:S(2)}, u32[]{:S(2)}) collective-permute-start(f32[8,128]{1,0:T(8,128)S(1)} %pad_maximum_fusion), channel_id=1, source_target_pairs={{0,1},{1,2},{2,3},{4,5},{5,6},{6,7},{8,9},{9,10},{10,11},{12,13},{... | collective-permute-start | bytes 12296 | tf_op jit(solution)/shard_map/ppermute | solution.py:28
  81.3 6.7 %copy-start.8 = (s32[2]{0:T(128)S(1)}, s32[2]{0:T(128)}, u32[]{:S(2)}) copy-start(s32[2]{0:T(128)} %len_ref.1) | copy-start | bytes 28
  84.5 3.4 %collective-permute-start.11 = (f32[8,144]{1,0:T(8,128)S(1)}, f32[8,144]{1,0:T(8,128)S(1)}, u32[]{:S(2)}, u32[]{:S(2)}) collective-permute-start(f32[8,144]{1,0:T(8,128)S(1)} %get-tuple-element.39), channel_id=1, source_target_pairs={{0,4},{4,0},{8,12},{12,8},{1,5},{5,1},{9,13},{13,9},{2,6},{6,2},{1... | collective-permute-start | bytes 13832 | tf_op jit(solution)/shard_map/ppermute | solution.py:28
  84.6 3.4 %collective-permute-start.12 = (f32[8,144]{1,0:T(8,128)S(1)}, f32[8,144]{1,0:T(8,128)S(1)}, u32[]{:S(2)}, u32[]{:S(2)}) collective-permute-start(f32[8,144]{1,0:T(8,128)S(1)} %get-tuple-element.40), channel_id=1, source_target_pairs={{4,8},{12,0},{8,4},{0,12},{5,9},{13,1},{9,5},{1,13},{6,10},{14,2},... | collective-permute-start | bytes 13832 | tf_op jit(solution)/shard_map/ppermute | solution.py:28
  91.4 1.2 %collective-permute-start.13 = (f32[2,32]{1,0:T(2,128)S(1)}, f32[2,32]{1,0:T(2,128)S(1)}, u32[]{:S(2)}, u32[]{:S(2)}) collective-permute-start(f32[2,32]{1,0:T(2,128)S(1)} %get-tuple-element.45), channel_id=1, source_target_pairs={{0,4},{4,0},{8,12},{12,8},{1,5},{5,1},{9,13},{13,9},{2,6},{6,2},{1... | collective-permute-start | bytes 776 | tf_op jit(solution)/shard_map/ppermute | solution.py:28
  92.6 3.0 %collective-permute-start.14 = (f32[2,2,32]{2,1,0:T(2,128)S(1)}, f32[2,2,32]{2,1,0:T(2,128)S(1)}, u32[]{:S(2)}, u32[]{:S(2)}) collective-permute-start(f32[2,2,32]{2,1,0:T(2,128)S(1)} %maximum_select_fusion), channel_id=1, source_target_pairs={{0,5},{1,4},{2,7},{3,6},{4,1},{5,0},{6,3},{7,2},{8,13},{9,12},{10,... | collective-permute-start | bytes 1544 | tf_op jit(solution)/shard_map/ppermute | solution.py:28
  95.6 3.9 %collective-permute-start.15 = (f32[2,2,32]{2,1,0:T(2,128)S(1)}, f32[2,2,32]{2,1,0:T(2,128)S(1)}, u32[]{:S(2)}, u32[]{:S(2)}) collective-permute-start(f32[2,2,32]{2,1,0:T(2,128)S(1)} %fusion.3), channel_id=1, source_target_pairs={{0,6},{1,7},{2,4},{3,5},{4,2},{5,3},{6,0},{7,1},{8,14},{9,15},{10,... | collective-permute-start | bytes 1544 | tf_op jit(solution)/shard_map/ppermute | solution.py:28
  99.7 3.1 %collective-permute-start.16 = (f32[2]{0:T(128)S(1)}, f32[2]{0:T(128)S(1)}, u32[]{:S(2)}, u32[]{:S(2)}) collective-permute-start(f32[2]{0:T(128)S(1)} %select_reduce_fusion), channel_id=1, source_target_pairs={{0,12},{1,13},{2,14},{3,15},{4,8},{5,9},{6,10},{7,11},{8,4},{9,5},... | collective-permute-start | bytes 32 | tf_op jit(solution)/shard_map/ppermute | solution.py:28
  (2 other events, 1.3 us)

commit v8 on v6

--- a/solution.py
+++ b/solution.py
@@ -58,35 +58,23 @@
     return [piece.reshape(regions * PIECE, channels) for piece in pieces]
 
 
-def write_edges(pos_ref, arrays, core_ref, chip_ref):
+def write_edges(pos_ref, arrays, core_ref, chip_ref, ready=None):
     total = jnp.concatenate(arrays, axis=0)
     frames = total.shape[1]
     eights = [total[at : at + 8] for at in range(0, total.shape[0], 8)]
     first = jnp.concatenate([eight[:, 0:EDGE] for eight in eights], axis=1)
     last = jnp.concatenate([eight[:, frames - EDGE : frames] for eight in eights], axis=1)
     even = pos_ref[0] % 2 == 0
-    core_ref[...] = jnp.where(even, last, first)
-    chip_ref[...] = jnp.where(even, first, last)
+    core, chip = jnp.where(even, last, first), jnp.where(even, first, last)
+    if ready is not None:
+        core = jnp.concatenate([ready[0], core], axis=1)
+        chip = jnp.concatenate([ready[1], chip], axis=1)
+    core_ref[...] = core
+    chip_ref[...] = chip
 
 
 def edge_shapes(columns):
     return [jax.ShapeDtypeStruct((8, columns // 8 * EDGE), F32)] * 2
-
-
-def edges_kernel(pos_ref, *refs):
-    write_edges(pos_ref, [ref[...] for ref in refs[:-2]], *refs[-2:])
-
-
-def edge_rows(position, sources):
-    smem = pl.BlockSpec(memory_space=pltpu.SMEM)
-    vmem = pl.BlockSpec(memory_space=pltpu.VMEM)
-    return pl.pallas_call(
-        edges_kernel,
-        in_specs=[smem] + [vmem for _ in sources],
-        out_specs=[vmem, vmem],
-        out_shape=edge_shapes(sum(source.shape[0] for source in sources)),
-        name="edges",
-    )(position, *sources)
 
 
 def sims_kernel(scale, spans, others, fetch, pos_ref, table_ref, query_ref, *refs):
@@ -153,7 +141,7 @@
     total = total * jnp.where(active, scale, 0.0).astype(F32)
     out_ref[...] = total
     if done:
-        write_edges(pos_ref, [ref[...] for ref in done] + [total], *refs[1:3])
+        write_edges(pos_ref, [total], *refs[1:3], [ref[...] for ref in done])
 
 
 def similarities(query, pieces, position, table, done=(), fetch=False):
@@ -163,7 +151,7 @@
     rows = sum(spans)
     shapes = [jax.ShapeDtypeStruct((rows, frames), F32)]
     if done:
-        shapes += edge_shapes(rows + sum(array.shape[0] for array in done))
+        shapes += edge_shapes(rows + done[0].shape[1] // EDGE * 8)
     steps = 0
     if fetch:
         shapes.append(pltpu.VMEM(query.shape, query.dtype))
@@ -373,8 +361,9 @@
 
 
 def assemble_kernel(segments, tiles, block, limits, pos_ref, *refs):
-    sources, refs = refs[:-9], refs[-9:]
-    w1_ref, b1_ref, w2_ref, b2_ref, sims_ref, first_ref, second_ref, y_ref, lhs_ref = refs
+    sources, refs = refs[:-11], refs[-11:]
+    w1_ref, b1_ref, w2_ref, b2_ref, sims_ref, first_ref, second_ref, *rims, y_ref, lhs_ref = refs
+    write_edges(pos_ref, [source[...] for source in sources], *rims)
     sims_ref[...] = jnp.zeros_like(sims_ref)
     place(pos_ref, sims_ref, sources, segments)
     first_map(sims_ref, w1_ref, b1_ref, y_ref, first_ref, pos_ref, block, limits, tiles[0])
@@ -390,12 +379,13 @@
     return pl.pallas_call(
         functools.partial(assemble_kernel, segments, tiles, block, limits),
         in_specs=[smem] + [vmem for _ in sources] + [vmem] * 4,
-        out_specs=[vmem] * 3,
+        out_specs=[vmem] * 5,
         out_shape=[
             jax.ShapeDtypeStruct((PHASES, block + 24, 2 * frames), F32),
             jax.ShapeDtypeStruct((block + 2 * HALO, jf, 128), F32),
             jax.ShapeDtypeStruct((block + 2, max(js, jt + 8), 128), F32),
-        ],
+        ]
+        + edge_shapes(sum(source.shape[0] for source in sources)),
         scratch_shapes=[
             pltpu.VMEM((max(8, sum(size for _, _, size in part)), lanes), BF)
             for part, lanes in zip(tiles, (256, 512))
@@ -688,7 +678,7 @@
     spot = late * PIECE if split else 2 * PIECE
     firsts = first_tiles(block, frames, jf, spot)
     seconds = second_tiles(block, js, spot, split)
-    maps = assembled(
+    *maps, core, chip = assembled(
         position, sources, segments, weights[:4], (firsts[0], seconds[0]), block, limits
     )
     if not split:
@@ -697,10 +687,11 @@
     if split:
         for half in range(2):
             segments.append((len(sources), PIECE * half, PIECE, 2 + half, late * PIECE))
-        done, core, chip = similarities(query, last, position, pair_table, sources)
+        done, core, chip = similarities(
+            query, last, position, pair_table, (core, chip)
+        )
         sources.append(done)
     else:
-        core, chip = edge_rows(position, sources)
         done = sources[-1]
     starts = [0]
     for source in sources[:-1]:

time: 104 us -> 108 us (1.038)
  waiting for transfers between devices: 39.7 us -> 44.6 us
    ppermute x17, waiting for transfers between devices: 39.7 us -> 44.6 us  [shift(): return lax.ppermute(array, axis, pairs)]
    unnamed x18 -> x20, local copies, waits for them, and re-layouts: 5.79 us -> 5.79 us
  transfers between devices with their start and end apart: 17 -> 17, of which waited for: 8 -> 10; matrix products, arithmetic and copies ran while one was open for 0% -> 0% of each run, Pallas kernels for 27% -> 26%
where the time goes in v8:
time: 108 us; the launch traced here: 107 us
  waiting for transfers between devices  44.6 us (41%)
  Pallas kernels  35.6 us (33%)
  starting transfers between devices  18.3 us (17%)
  local copies, waits for them, and re-layouts  5.89 us (5%)
  between operations  2.15 us (2%)
    ppermute x17, waiting for transfers between devices, shift(): return lax.ppermute(array, axis, pairs)  44.6 us
    pallas_call x5, Pallas kernels, similarities(): pl.pallas_call(functools.partial(sims_kernel, scale, spans, len(done), fe...  24.1 us
    ppermute x17, starting transfers between devices, shift(): return lax.ppermute(array, axis, pairs)  18.3 us
    unnamed x20, local copies, waits for them, and re-layouts  5.79 us
    pallas_call x2, Pallas kernels, cut(): pl.pallas_call(functools.partial(cut_kernel, order), in_specs=[pl.BlockSp...  3.48 us
    pallas_call x1, Pallas kernels, network(): pl.pallas_call(functools.partial(network_kernel, limits, padding, starts,...  3.44 us
    pallas_call x1, Pallas kernels, network_weights(): pl.pallas_call(weights_kernel, out_shape=[jax.ShapeDtypeStruct(shape, dty...  3.09 us
  transfers between devices with their start and end apart: 17, of which 10 were waited for; matrix products, arithmetic and copies ran while one was open for 0% of the time, Pallas kernels for 26%

profile of v8, /device:TPU:0, one launch (start us, length us, event | category | flops | bytes accessed | tf_op | source)
XLA Modules:
  0.0 107.2 jit_solution(767995170265340224)
XLA Ops:
  0.6 1.1 cut.2
  2.3 2.4 %cut.3 = (bf16[9,8,3840]{2,1,0:T(8,128)(2,1)S(1)}, bf16[9,8,3840]{2,1,0:T(8,128)(2,1)}, bf16[9,8,3840]{2,1,0:T(8,128)(2,1)}) custom-call(bf16[9,32,3840]{2,1,0:T(8,128)(2,1)} %bitcast.44), custom_call_target="tpu_custom_call" | custom-call | bytes 4423680 | tf_op jit(solution)/shard_map/cut/pallas_call | solution.py:46
  4.7 2.6 %collective-permute-start.3 = (bf16[72,3840]{1,0:T(8,128)(2,1)S(1)}, bf16[72,3840]{1,0:T(8,128)(2,1)S(1)}, u32[]{:S(2)}, u32[]{:S(2)}) collective-permute-start(bf16[72,3840]{1,0:T(8,128)(2,1)S(1)} %bitcast.35), channel_id=1, source_target_pairs={{0,8},{4,12},{8,0},{12,4},{1,9},{5,13},{9,1},{13,5},{2,10},{6,14},... | collective-permute-start | bytes 1658888 | tf_op jit(solution)/shard_map/ppermute | solution.py:28
  7.3 1.9 %collective-permute-start.5 = (bf16[72,3840]{1,0:T(8,128)(2,1)}, bf16[72,3840]{1,0:T(8,128)(2,1)S(1)}, u32[]{:S(2)}, u32[]{:S(2)}) collective-permute-start(bf16[72,3840]{1,0:T(8,128)(2,1)} %bitcast.19), channel_id=1, source_target_pairs={{0,8},{4,12},{8,0},{12,4},{1,9},{5,13},{9,1},{13,5},{2,10},{6,14},... | collective-permute-start | bytes 1658888 | tf_op jit(solution)/shard_map/ppermute | solution.py:28
  9.3 11.3 %collective-permute-done.3.refs_0_ = bf16[72,3840]{1,0:T(8,128)(2,1)S(1)} collective-permute-done((bf16[72,3840]{1,0:T(8,128)(2,1)S(1)}, bf16[72,3840]{1,0:T(8,128)(2,1)S(1)}, u32[]{:S(2)}, u32[]{:S(2)}) %collective-permute-start.3) | collective-permute-done | bytes 552992 | tf_op jit(solution)/shard_map/ppermute | solution.py:28
  25.8 3.1 %weights.1 = (bf16[256,1536]{1,0:T(8,128)(2,1)S(1)}, f32[1,128]{1,0:T(1,128)S(1)}, bf16[512,256]{1,0:T(8,128)(2,1)S(1)}, f32[1,128]{1,0:T(1,128)S(1)}, bf16[768,...) custom-call(f32[3,3,32]{2,1,0:T(4,128)S(1)} %copy-done.4, f32[1,32]{1,0:T(1,128)S(1)} %bitcast.38, ...), custom_call_target="tpu_custom_call" | custom-call | flops 100000000 | bytes 4000000 | tf_op jit(solution)/shard_map/weights/pallas_call | solution.py:535
  28.9 3.5 %collective-permute-done.1.refs_0_ = bf16[72,3840]{1,0:T(8,128)(2,1)S(1)} collective-permute-done((bf16[72,3840]{1,0:T(8,128)(2,1)S(1)}, bf16[72,3840]{1,0:T(8,128)(2,1)S(1)}, u32[]{:S(2)}, u32[]{:S(2)}) %collective-permute-start.1) | collective-permute-done | bytes 552992 | tf_op jit(solution)/shard_map/ppermute | solution.py:28
  32.5 11.8 %collective-permute-done.5.refs_0_ = bf16[72,3840]{1,0:T(8,128)(2,1)S(1)} collective-permute-done((bf16[72,3840]{1,0:T(8,128)(2,1)}, bf16[72,3840]{1,0:T(8,128)(2,1)S(1)}, u32[]{:S(2)}, u32[]{:S(2)}) %collective-permute-start.5) | collective-permute-done | bytes 552992 | tf_op jit(solution)/shard_map/ppermute | solution.py:28
  44.3 11.6 %collective-permute-done.9.refs_0_ = bf16[72,3840]{1,0:T(8,128)(2,1)S(1)} collective-permute-done((bf16[72,3840]{1,0:T(8,128)(2,1)}, bf16[72,3840]{1,0:T(8,128)(2,1)S(1)}, u32[]{:S(2)}, u32[]{:S(2)}) %collective-permute-start.9) | collective-permute-done | bytes 552992 | tf_op jit(solution)/shard_map/ppermute | solution.py:28
  56.7 11.2 %similarities.5 = (f32[64,128]{1,0:T(8,128)S(1)}, bf16[9,128,3840]{2,1,0:T(8,128)(2,1)S(1)}) custom-call(s32[14]{0:T(128)S(1)} %stack.67.pos_ref, s32[4,4]{1,0:T(4,128)S(1)} %copy-done, bf16[9,128,3840]{2,1,0:T(8,128)(2,1)} %bitcast.48, bf16[288,3840]{1,0:T(8,128)(2,1)} %bitcast.45, bf16[288,3840]{1,0:T(8,128)(2,1)} %collective-permute-done.refs_1_), custom_call_target="tpu_custom_call" | custom-call | flops 5096079360 | bytes 4423680 | tf_op jit(solution)/shard_map/similarities/pallas_call | solution.py:161
  67.9 3.2 %similarities.7.refs_2_ = f32[16,128]{1,0:T(8,128)S(1)} custom-call(s32[14]{0:T(128)S(1)} %stack.67.pos_ref, s32[4,4]{1,0:T(4,128)S(1)} %copy-done, bf16[9,128,3840]{2,1,0:T(8,128)(2,1)S(1)} %get-tuple-element.28.query_ref, bf16[72,3840]{1,0:T(8,128)(2,1)S(1)} %collective-permute-done.3.refs_0_, bf16[72,3840]{1,0:T(8,128)(2,1)S(1)} %collective-permute-done.4.refs_1_), custom_call_target="tpu_custom_call" | custom-call | flops 1274019840 | bytes 1105920 | tf_op jit(solution)/shard_map/similarities/pallas_call | solution.py:161
  71.2 3.7 %collective-permute-start.7 = (f32[8,128]{1,0:T(8,128)S(1)}, f32[8,128]{1,0:T(8,128)S(1)}, u32[]{:S(2)}, u32[]{:S(2)}) collective-permute-start(f32[8,128]{1,0:T(8,128)S(1)} %pad_maximum_fusion), channel_id=1, source_target_pairs={{0,1},{1,2},{2,3},{4,5},{5,6},{6,7},{8,9},{9,10},{10,11},{12,13},{... | collective-permute-start | bytes 12296 | tf_op jit(solution)/shard_map/ppermute | solution.py:28
  74.9 3.2 %similarities.6.refs_1_ = f32[16,128]{1,0:T(8,128)S(1)} custom-call(s32[14]{0:T(128)S(1)} %stack.67.pos_ref, s32[4,4]{1,0:T(4,128)S(1)} %copy-done, bf16[9,128,3840]{2,1,0:T(8,128)(2,1)S(1)} %get-tuple-element.28.query_ref, bf16[72,3840]{1,0:T(8,128)(2,1)S(1)} %collective-permute-done.1.refs_0_, bf16[72,3840]{1,0:T(8,128)(2,1)S(1)} %collective-permute-done.2.refs_1_), custom_call_target="tpu_custom_call" | custom-call | flops 1274019840 | bytes 1105920 | tf_op jit(solution)/shard_map/similarities/pallas_call | solution.py:161
  78.2 1.5 %collective-permute-start.8 = (f32[8,128]{1,0:T(8,128)S(1)}, f32[8,128]{1,0:T(8,128)S(1)}, u32[]{:S(2)}, u32[]{:S(2)}) collective-permute-start(f32[8,128]{1,0:T(8,128)S(1)} %pad_maximum_fusion.1), channel_id=1, source_target_pairs={{1,0},{2,1},{3,2},{5,4},{6,5},{7,6},{9,8},{10,9},{11,10},{13,12},{... | collective-permute-start | bytes 12296 | tf_op jit(solution)/shard_map/ppermute | solution.py:28
  79.7 3.2 %similarities.8.refs_3_ = f32[16,128]{1,0:T(8,128)S(1)} custom-call(s32[14]{0:T(128)S(1)} %stack.67.pos_ref, s32[4,4]{1,0:T(4,128)S(1)} %copy-done, bf16[9,128,3840]{2,1,0:T(8,128)(2,1)S(1)} %get-tuple-element.28.query_ref, bf16[72,3840]{1,0:T(8,128)(2,1)S(1)} %collective-permute-done.5.refs_0_, bf16[72,3840]{1,0:T(8,128)(2,1)S(1)} %collective-permute-done.6.refs_1_), custom_call_target="tpu_custom_call" | custom-call | flops 1274019840 | bytes 1105920 | tf_op jit(solution)/shard_map/similarities/pallas_call | solution.py:161
  83.7 1.5 %assemble.1 = (f32[4,56,256]{2,1,0:T(8,128)S(1)}, f32[36,40,128]{2,1,0:T(8,128)S(1)}, f32[34,40,128]{2,1,0:T(8,128)S(1)}, f32[8,128]{1,0:T(8,128)S(1)}, f32[8,128]{1,0:T(8,128)S(1)}) custom-call(s32[14]{0:T(128)S(1)} %stack.67.pos_ref, f32[64,128]{1,0:T(8,128)S(1)} %get-tuple-element.27.refs_0_, f32[16,128]{1,0:T(8,128)S(1)} %similarities.6.refs_1_, ...), custom_call_target="tpu_custom_call" | custom-call | flops 1000000000 | bytes 500000 | tf_op jit(solution)/shard_map/assemble/pallas_call | solution.py:379
  85.2 3.3 %similarities.9 = (f32[16,128]{1,0:T(8,128)S(1)}, f32[8,144]{1,0:T(8,128)S(1)}, f32[8,144]{1,0:T(8,128)S(1)}) custom-call(s32[14]{0:T(128)S(1)} %stack.67.pos_ref, s32[4,4]{1,0:T(4,128)S(1)} %copy-done.1, bf16[9,128,3840]{2,1,0:T(8,128)(2,1)S(1)} %get-tuple-element.28.query_ref, bf16[72,3840]{1,0:T(8,128)(2,1)S(1)} %collective-permute-done.9.refs_0_, ...), custom_call_target="tpu_custom_call" | custom-call | flops 1274019840 | bytes 1105920 | tf_op jit(solution)/shard_map/similarities/pallas_call | solution.py:161
  88.5 1.6 %collective-permute-start.12 = (f32[8,144]{1,0:T(8,128)S(1)}, f32[8,144]{1,0:T(8,128)S(1)}, u32[]{:S(2)}, u32[]{:S(2)}) collective-permute-start(f32[8,144]{1,0:T(8,128)S(1)} %get-tuple-element.44), channel_id=1, source_target_pairs={{4,8},{12,0},{8,4},{0,12},{5,9},{13,1},{9,5},{1,13},{6,10},{14,2},... | collective-permute-start | bytes 13832 | tf_op jit(solution)/shard_map/ppermute | solution.py:28
  91.6 3.4 %network.1 = (f32[32,32]{1,0:T(8,128)}, f32[2,32]{1,0:T(2,128)S(1)}, f32[4,56,256]{2,1,0:T(8,128)S(1)}, f32[36,40,128]{2,1,0:T(8,128)S(1)}, f32[34,40,128]{2,1,0:T(8,128)S(1)}) custom-call(s32[14]{0:T(128)S(1)} %stack.67.pos_ref, s32[2]{0:T(128)S(1)} %copy-done.9, ...), custom_call_target="tpu_custom_call", output_to_operand_aliasing={{2}: (2, {}), {3}: (3, {}), {4}: (4, {})} | custom-call | flops 6000000000 | bytes 4000000 | tf_op jit(solution)/shard_map/network/pallas_call | solution.py:448
  96.3 1.8 %collective-permute-start.14 = (f32[2,2,32]{2,1,0:T(2,128)S(1)}, f32[2,2,32]{2,1,0:T(2,128)S(1)}, u32[]{:S(2)}, u32[]{:S(2)}) collective-permute-start(f32[2,2,32]{2,1,0:T(2,128)S(1)} %maximum_select_fusion), channel_id=1, source_target_pairs={{0,5},{1,4},{2,7},{3,6},{4,1},{5,0},{6,3},{7,2},{8,13},{9,12},{10,... | collective-permute-start | bytes 1544 | tf_op jit(solution)/shard_map/ppermute | solution.py:28
  99.5 2.7 %collective-permute-start.15 = (f32[2,2,32]{2,1,0:T(2,128)S(1)}, f32[2,2,32]{2,1,0:T(2,128)S(1)}, u32[]{:S(2)}, u32[]{:S(2)}) collective-permute-start(f32[2,2,32]{2,1,0:T(2,128)S(1)} %fusion.3), channel_id=1, source_target_pairs={{0,6},{1,7},{2,4},{3,5},{4,2},{5,3},{6,0},{7,1},{8,14},{9,15},{10,... | collective-permute-start | bytes 1544 | tf_op jit(solution)/shard_map/ppermute | solution.py:28
  102.2 1.3 %collective-permute-done.15 = f32[2,2,32]{2,1,0:T(2,128)S(1)} collective-permute-done((f32[2,2,32]{2,1,0:T(2,128)S(1)}, f32[2,2,32]{2,1,0:T(2,128)S(1)}, u32[]{:S(2)}, u32[]{:S(2)}) %collective-permute-start.15) | collective-permute-done | bytes 544 | tf_op jit(solution)/shard_map/ppermute | solution.py:28
  103.6 1.3 %collective-permute-start.16 = (f32[2]{0:T(128)S(1)}, f32[2]{0:T(128)S(1)}, u32[]{:S(2)}, u32[]{:S(2)}) collective-permute-start(f32[2]{0:T(128)S(1)} %select_reduce_fusion), channel_id=1, source_target_pairs={{0,12},{1,13},{2,14},{3,15},{4,8},{5,9},{6,10},{7,11},{8,4},{9,5},... | collective-permute-start | bytes 32 | tf_op jit(solution)/shard_map/ppermute | solution.py:28
  104.9 1.8 %collective-permute-done.16 = f32[2]{0:T(128)S(1)} collective-permute-done((f32[2]{0:T(128)S(1)}, f32[2]{0:T(128)S(1)}, u32[]{:S(2)}, u32[]{:S(2)}) %collective-permute-start.16) | collective-permute-done | bytes 40 | tf_op jit(solution)/shard_map/ppermute | solution.py:28
  (51 shorter events, 10.9 us)
Async XLA Ops:
  1.7 54.3 %collective-permute-start = (bf16[288,3840]{1,0:T(8,128)(2,1)}, bf16[288,3840]{1,0:T(8,128)(2,1)}, u32[]{:S(2)}, u32[]{:S(2)}) collective-permute-start(bf16[288,3840]{1,0:T(8,128)(2,1)} %bitcast.43), channel_id=1, source_target_pairs={{0,4},{4,0},{8,12},{12,8},{1,5},{5,1},{9,13},{13,9},{2,6},{6,2},{1... | collective-permute-start | bytes 6635528 | tf_op jit(solution)/shard_map/ppermute | solution.py:28
  4.7 15.9 %collective-permute-start.3 = (bf16[72,3840]{1,0:T(8,128)(2,1)S(1)}, bf16[72,3840]{1,0:T(8,128)(2,1)S(1)}, u32[]{:S(2)}, u32[]{:S(2)}) collective-permute-start(bf16[72,3840]{1,0:T(8,128)(2,1)S(1)} %bitcast.35), channel_id=1, source_target_pairs={{0,8},{4,12},{8,0},{12,4},{1,9},{5,13},{9,1},{13,5},{2,10},{6,14},... | collective-permute-start | bytes 1658888 | tf_op jit(solution)/shard_map/ppermute | solution.py:28
  7.2 25.2 %collective-permute-start.1 = (bf16[72,3840]{1,0:T(8,128)(2,1)S(1)}, bf16[72,3840]{1,0:T(8,128)(2,1)S(1)}, u32[]{:S(2)}, u32[]{:S(2)}) collective-permute-start(bf16[72,3840]{1,0:T(8,128)(2,1)S(1)} %bitcast.32), channel_id=1, source_target_pairs={{0,8},{4,12},{8,0},{12,4},{1,9},{5,13},{9,1},{13,5},{2,10},{6,14},... | collective-permute-start | bytes 1658888 | tf_op jit(solution)/shard_map/ppermute | solution.py:28
  7.3 37.0 %collective-permute-start.5 = (bf16[72,3840]{1,0:T(8,128)(2,1)}, bf16[72,3840]{1,0:T(8,128)(2,1)S(1)}, u32[]{:S(2)}, u32[]{:S(2)}) collective-permute-start(bf16[72,3840]{1,0:T(8,128)(2,1)} %bitcast.19), channel_id=1, source_target_pairs={{0,8},{4,12},{8,0},{12,4},{1,9},{5,13},{9,1},{13,5},{2,10},{6,14},... | collective-permute-start | bytes 1658888 | tf_op jit(solution)/shard_map/ppermute | solution.py:28
  9.3 46.7 %collective-permute-start.9 = (bf16[72,3840]{1,0:T(8,128)(2,1)}, bf16[72,3840]{1,0:T(8,128)(2,1)S(1)}, u32[]{:S(2)}, u32[]{:S(2)}) collective-permute-start(bf16[72,3840]{1,0:T(8,128)(2,1)} %bitcast.26), channel_id=1, source_target_pairs={{0,8},{4,12},{8,0},{12,4},{1,9},{5,13},{9,1},{13,5},{2,10},{6,14},... | collective-permute-start | bytes 1658888 | tf_op jit(solution)/shard_map/ppermute | solution.py:28
  20.6 47.3 %collective-permute-start.4 = (bf16[72,3840]{1,0:T(8,128)(2,1)S(1)}, bf16[72,3840]{1,0:T(8,128)(2,1)S(1)}, u32[]{:S(2)}, u32[]{:S(2)}) collective-permute-start(bf16[72,3840]{1,0:T(8,128)(2,1)S(1)} %collective-permute-done.3.refs_0_), channel_id=1, source_target_pairs={{0,4},{4,0},{8,12},{12,8},{1,5},{5,1},{9,13},{13,9},{2,6},{6,2},{1... | collective-permute-start | bytes 1658888 | tf_op jit(solution)/shard_map/ppermute | solution.py:28
  20.7 0.9 copy-start.2
  21.6 0.9 copy-start.3
  22.5 0.7 copy-start.4
  25.2 0.7 copy-start.8
  32.5 42.4 %collective-permute-start.2 = (bf16[72,3840]{1,0:T(8,128)(2,1)S(1)}, bf16[72,3840]{1,0:T(8,128)(2,1)S(1)}, u32[]{:S(2)}, u32[]{:S(2)}) collective-permute-start(bf16[72,3840]{1,0:T(8,128)(2,1)S(1)} %collective-permute-done.1.refs_0_), channel_id=1, source_target_pairs={{0,4},{4,0},{8,12},{12,8},{1,5},{5,1},{9,13},{13,9},{2,6},{6,2},{1... | collective-permute-start | bytes 1658888 | tf_op jit(solution)/shard_map/ppermute | solution.py:28
  44.3 35.3 %collective-permute-start.6 = (bf16[72,3840]{1,0:T(8,128)(2,1)S(1)}, bf16[72,3840]{1,0:T(8,128)(2,1)S(1)}, u32[]{:S(2)}, u32[]{:S(2)}) collective-permute-start(bf16[72,3840]{1,0:T(8,128)(2,1)S(1)} %collective-permute-done.5.refs_0_), channel_id=1, source_target_pairs={{0,4},{4,0},{8,12},{12,8},{1,5},{5,1},{9,13},{13,9},{2,6},{6,2},{1... | collective-permute-start | bytes 1658888 | tf_op jit(solution)/shard_map/ppermute | solution.py:28
  56.0 29.2 %collective-permute-start.10 = (bf16[72,3840]{1,0:T(8,128)(2,1)S(1)}, bf16[72,3840]{1,0:T(8,128)(2,1)S(1)}, u32[]{:S(2)}, u32[]{:S(2)}) collective-permute-start(bf16[72,3840]{1,0:T(8,128)(2,1)S(1)} %collective-permute-done.9.refs_0_), channel_id=1, source_target_pairs={{0,4},{4,0},{8,12},{12,8},{1,5},{5,1},{9,13},{13,9},{2,6},{6,2},{1... | collective-permute-start | bytes 1658888 | tf_op jit(solution)/shard_map/ppermute | solution.py:28
  56.0 0.7 copy-start
  71.2 11.7 %collective-permute-start.7 = (f32[8,128]{1,0:T(8,128)S(1)}, f32[8,128]{1,0:T(8,128)S(1)}, u32[]{:S(2)}, u32[]{:S(2)}) collective-permute-start(f32[8,128]{1,0:T(8,128)S(1)} %pad_maximum_fusion), channel_id=1, source_target_pairs={{0,1},{1,2},{2,3},{4,5},{5,6},{6,7},{8,9},{9,10},{10,11},{12,13},{... | collective-permute-start | bytes 12296 | tf_op jit(solution)/shard_map/ppermute | solution.py:28
  78.1 7.1 %copy-start.1 = (s32[4,4]{1,0:T(4,128)S(1)}, s32[4,4]{1,0:T(4,128)}, u32[]{:S(2)}) copy-start(s32[4,4]{1,0:T(4,128)} %table_ref.9) | copy-start | bytes 196
  78.2 5.5 %collective-permute-start.8 = (f32[8,128]{1,0:T(8,128)S(1)}, f32[8,128]{1,0:T(8,128)S(1)}, u32[]{:S(2)}, u32[]{:S(2)}) collective-permute-start(f32[8,128]{1,0:T(8,128)S(1)} %pad_maximum_fusion.1), channel_id=1, source_target_pairs={{1,0},{2,1},{3,2},{5,4},{6,5},{7,6},{9,8},{10,9},{11,10},{13,12},{... | collective-permute-start | bytes 12296 | tf_op jit(solution)/shard_map/ppermute | solution.py:28
  82.9 8.8 %copy-start.9 = (s32[2]{0:T(128)S(1)}, s32[2]{0:T(128)}, u32[]{:S(2)}) copy-start(s32[2]{0:T(128)} %len_ref.1) | copy-start | bytes 28
  88.5 2.3 %collective-permute-start.11 = (f32[8,144]{1,0:T(8,128)S(1)}, f32[8,144]{1,0:T(8,128)S(1)}, u32[]{:S(2)}, u32[]{:S(2)}) collective-permute-start(f32[8,144]{1,0:T(8,128)S(1)} %get-tuple-element.43), channel_id=1, source_target_pairs={{0,4},{4,0},{8,12},{12,8},{1,5},{5,1},{9,13},{13,9},{2,6},{6,2},{1... | collective-permute-start | bytes 13832 | tf_op jit(solution)/shard_map/ppermute | solution.py:28
  88.5 3.1 %collective-permute-start.12 = (f32[8,144]{1,0:T(8,128)S(1)}, f32[8,144]{1,0:T(8,128)S(1)}, u32[]{:S(2)}, u32[]{:S(2)}) collective-permute-start(f32[8,144]{1,0:T(8,128)S(1)} %get-tuple-element.44), channel_id=1, source_target_pairs={{4,8},{12,0},{8,4},{0,12},{5,9},{13,1},{9,5},{1,13},{6,10},{14,2},... | collective-permute-start | bytes 13832 | tf_op jit(solution)/shard_map/ppermute | solution.py:28
  95.1 1.3 %collective-permute-start.13 = (f32[2,32]{1,0:T(2,128)S(1)}, f32[2,32]{1,0:T(2,128)S(1)}, u32[]{:S(2)}, u32[]{:S(2)}) collective-permute-start(f32[2,32]{1,0:T(2,128)S(1)} %get-tuple-element.49), channel_id=1, source_target_pairs={{0,4},{4,0},{8,12},{12,8},{1,5},{5,1},{9,13},{13,9},{2,6},{6,2},{1... | collective-permute-start | bytes 776 | tf_op jit(solution)/shard_map/ppermute | solution.py:28
  96.3 3.1 %collective-permute-start.14 = (f32[2,2,32]{2,1,0:T(2,128)S(1)}, f32[2,2,32]{2,1,0:T(2,128)S(1)}, u32[]{:S(2)}, u32[]{:S(2)}) collective-permute-start(f32[2,2,32]{2,1,0:T(2,128)S(1)} %maximum_select_fusion), channel_id=1, source_target_pairs={{0,5},{1,4},{2,7},{3,6},{4,1},{5,0},{6,3},{7,2},{8,13},{9,12},{10,... | collective-permute-start | bytes 1544 | tf_op jit(solution)/shard_map/ppermute | solution.py:28
  99.5 4.0 %collective-permute-start.15 = (f32[2,2,32]{2,1,0:T(2,128)S(1)}, f32[2,2,32]{2,1,0:T(2,128)S(1)}, u32[]{:S(2)}, u32[]{:S(2)}) collective-permute-start(f32[2,2,32]{2,1,0:T(2,128)S(1)} %fusion.3), channel_id=1, source_target_pairs={{0,6},{1,7},{2,4},{3,5},{4,2},{5,3},{6,0},{7,1},{8,14},{9,15},{10,... | collective-permute-start | bytes 1544 | tf_op jit(solution)/shard_map/ppermute | solution.py:28
  103.6 3.1 %collective-permute-start.16 = (f32[2]{0:T(128)S(1)}, f32[2]{0:T(128)S(1)}, u32[]{:S(2)}, u32[]{:S(2)}) collective-permute-start(f32[2]{0:T(128)S(1)} %select_reduce_fusion), channel_id=1, source_target_pairs={{0,12},{1,13},{2,14},{3,15},{4,8},{5,9},{6,10},{7,11},{8,4},{9,5},... | collective-permute-start | bytes 32 | tf_op jit(solution)/shard_map/ppermute | solution.py:28
  (3 other events, 2.0 us)
